TPU v7x, 128 devices: a whole 4x4x4 slice. The times are simulated.
128 devices in a mesh: seg: 32 (over y, z, core), rep: 4 (over x).
Axes of the slice: x: 4, y: 4, z: 4, core: 2. Of those that a mesh axis runs over, the one named last changes fastest.
Arguments:
- speeds: float32 [384, 16384], P(('rep', 'seg')), may hold values from -6 to 6
- w_start: float32 [32], replicated, may hold values from -4 to 4
- b_start: float32 [32], replicated, may hold values from -3 to 3
- w_filter: bfloat16 [2, 32, 32], replicated, may hold values from -0.75 to 0.75
- b_filter: float32 [32], replicated, may hold values from -3 to 3
- w_gate: bfloat16 [2, 32, 32], replicated, may hold values from -0.75 to 0.75
- b_gate: float32 [32], replicated, may hold values from -3 to 3
- adj_cols: int32 [128, 3], P('seg'), may hold values from 0 to 127, as said below
- adj_vals: bfloat16 [128, 3, 128, 128], P('seg'), may hold values from -0.3125 to 0.3125
- w_mix: bfloat16 [32, 96], replicated, may hold values from -0.625 to 0.625
- b_mix: float32 [32], replicated, may hold values from -3 to 3
- w_skip: bfloat16 [256, 32], replicated, may hold values from -1 to 1
- b_skip: float32 [256], replicated, may hold values from -3 to 3
- grad_res: bfloat16 [8, 32, 32, 16384], P('rep', None, None, 'seg'), may hold values from -6 to 6
- grad_skip: bfloat16 [8, 256, 16384], P('rep', None, 'seg'), may hold values from -6 to 6
Outputs:
- res_out: bfloat16 [8, 32, 32, 16384], P('rep', None, None, 'seg')
- skip_out: bfloat16 [8, 256, 16384], P('rep', None, 'seg')
- start_weight_gradient: float32 [32], replicated
- d_start_b: float32 [32], replicated
- d_filter: float32 [2, 32, 32], replicated
- d_filter_b: float32 [32], replicated
- d_gate: float32 [2, 32, 32], replicated
- d_gate_b: float32 [32], replicated
- d_mix: float32 [32, 96], replicated
- d_mix_b: float32 [32], replicated
- d_skip: float32 [256, 32], replicated
- d_skip_b: float32 [256], replicated
Inputs may be any that keep to these rules, and one draw needn't show every extreme that they name: adj_cols[i, 0] = i; the 3 entries of a row are distinct and lie within 2 tiles of i; adj_cols[i, 1] is i - 2 or i + 2.
All inputs are finite; a program needn't handle non-finite values.
Results may differ from a plain program's by a relative error of at most 0.01.
Values may be sent and summed in bfloat16 or wider, within the bound.
No kernel may reach another device: no remote copies, remote signals or barrier semaphores. Data moves between devices by JAX's collectives and lax.ppermute only.
A program may use at most 192 MiB of HBM per device.

v0:
```python
import math

import jax
import jax.numpy as jnp
from jax import lax
from jax.sharding import PartitionSpec as P

C = 32
TILE = 128
R = 2
DILATION_SIZE = 16
OUTPUT_STEPS = 32
BR = 2
TILES_DEV = 4
T_IN = 48


def shifted(value, axis, steps):
    count = lax.axis_size(axis)
    leading, last = (max(0, -steps), min(count, count - steps))
    return lax.ppermute(value, axis, [(source, source + steps) for source in range(leading, last)])


def extended_2(cells, sides, width):
    for axis, dim in sides:
        count = lax.axis_size(axis)
        ends = count - 1
        head = lax.slice_in_dim(cells, 0, width, axis=dim)
        tail = lax.slice_in_dim(cells, cells.shape[dim] - width, cells.shape[dim], axis=dim)
        cells = jnp.concatenate(
            [
                lax.ppermute(tail, axis, [(i, (i + 1) % count) for i in range(ends)]),
                cells,
                lax.ppermute(head, axis, [((i + 1) % count, i) for i in range(ends)]),
            ],
            axis=dim,
        )
    return cells


def diffuse(source, offsets, block_list, lead_tiles):
    tile_count = offsets.shape[0]
    places = jnp.arange(tile_count, dtype=jnp.int32)[:, None] + lead_tiles + offsets
    summed_values = None
    for column_vector in range(offsets.shape[1]):
        selected_entries = jnp.take(source, places[:, column_vector], axis=1)
        matrix_product = jnp.einsum(
            "enb,ntb->ent",
            selected_entries,
            block_list[:, column_vector],
            preferred_element_type=jnp.float32,
        )
        summed_values = matrix_product if summed_values is None else summed_values + matrix_product
    return summed_values


def spread_back(receptive_input, offsets, block_list, reach_tiles):
    tile_count = offsets.shape[0]
    targets = jnp.arange(tile_count, dtype=jnp.int32)[:, None] + reach_tiles + offsets
    widened = jnp.zeros(
        (receptive_input.shape[0], tile_count + 2 * reach_tiles, receptive_input.shape[2]),
        jnp.float32,
    )
    for column_vector in range(offsets.shape[1]):
        matrix_product = jnp.einsum(
            "htg,tgd->htd",
            receptive_input,
            block_list[:, column_vector],
            preferred_element_type=jnp.float32,
        )
        widened = widened.at[:, targets[:, column_vector]].add(matrix_product)
    return widened


def adjoint(receptive_input, offsets, block_list):
    row_total, tile_count, tile_len = receptive_input.shape
    widened = spread_back(receptive_input, offsets, block_list, R)
    own_part = widened[:, R : R + tile_count]
    low_part = shifted(widened[:, tile_count + R :].astype(jnp.bfloat16), "seg", 1).astype(
        jnp.float32
    )
    high_part = shifted(widened[:, :R].astype(jnp.bfloat16), "seg", -1).astype(jnp.float32)
    return jnp.concatenate(
        [
            own_part[:, :R] + low_part,
            own_part[:, R : tile_count - R],
            own_part[:, tile_count - R :] + high_part,
        ],
        axis=1,
    )


def body(
    speeds,
    w_start,
    b_start,
    w_filter,
    b_filter,
    w_gate,
    b_gate,
    adj_cols,
    adj_vals,
    w_mix,
    b_mix,
    w_skip,
    b_skip,
    grad_res,
    grad_skip,
):
    seg_count = lax.axis_size("seg")
    batch_total = BR * lax.axis_size("rep")
    seg_width = TILES_DEV * TILE
    segment_total = seg_width * seg_count
    res_scale = 1.0 / math.sqrt(batch_total * OUTPUT_STEPS * segment_total)
    skip_scale = 1.0 / math.sqrt(batch_total * segment_total)
    row_total = BR * OUTPUT_STEPS * C
    regrouped = lax.all_to_all(speeds, "seg", split_axis=1, concat_axis=0, tiled=True)
    signal_series = regrouped.reshape(BR, T_IN, seg_width)
    first_tile = lax.axis_index("seg") * TILES_DEV
    offsets = adj_cols - (first_tile + jnp.arange(TILES_DEV, dtype=jnp.int32))[:, None]
    hidden_values = (
        w_start[None, None, :, None] * signal_series[:, :, None, :] + b_start[None, None, :, None]
    ).astype(jnp.bfloat16)
    low_arr = hidden_values[:, :OUTPUT_STEPS]
    high_values = hidden_values[:, DILATION_SIZE:]

    def temporal(weights, bias):
        first_tap = jnp.einsum(
            "oi,btis->btos", weights[0], low_arr, preferred_element_type=jnp.float32
        )
        second_tap = jnp.einsum(
            "oi,btis->btos", weights[1], high_values, preferred_element_type=jnp.float32
        )
        return first_tap + second_tap + bias[None, None, :, None]

    filt_arr = jnp.tanh(temporal(w_filter, b_filter))
    gate_arr = jax.nn.sigmoid(temporal(w_gate, b_gate))
    gated = (filt_arr * gate_arr).astype(jnp.bfloat16)
    flat_gated = gated.reshape(row_total, seg_width)
    extended = extended_2(flat_gated, (("seg", 1),), R * TILE).reshape(
        row_total, TILES_DEV + 2 * R, TILE
    )
    hop_one_t = diffuse(extended, offsets, adj_vals, R).astype(jnp.bfloat16)
    extended_one = extended_2(
        hop_one_t.reshape(row_total, seg_width), (("seg", 1),), R * TILE
    ).reshape(row_total, TILES_DEV + 2 * R, TILE)
    hop_two_t = diffuse(extended_one, offsets, adj_vals, R).astype(jnp.bfloat16)
    lower = hidden_values[:, :OUTPUT_STEPS]
    upper_bound = hidden_values[:, DILATION_SIZE:]
    hop_one = hop_one_t.reshape(BR, OUTPUT_STEPS, C, seg_width)
    hop_two = hop_two_t.reshape(BR, OUTPUT_STEPS, C, seg_width)
    mixed = jnp.einsum("oj,btjs->btos", w_mix[:, :C], gated, preferred_element_type=jnp.float32)
    mixed = mixed + jnp.einsum(
        "oj,btjs->btos", w_mix[:, C : 2 * C], hop_one, preferred_element_type=jnp.float32
    )
    mixed = mixed + jnp.einsum(
        "oj,btjs->btos", w_mix[:, 2 * C :], hop_two, preferred_element_type=jnp.float32
    )
    res_out = (mixed + b_mix[None, None, :, None] + upper_bound.astype(jnp.float32)).astype(
        jnp.bfloat16
    )
    last_step = gated[:, OUTPUT_STEPS - 1]
    skip_out = (
        jnp.einsum("sc,bcn->bsn", w_skip, last_step, preferred_element_type=jnp.float32)
        + b_skip[None, :, None]
    ).astype(jnp.bfloat16)
    d_mix = (
        jnp.concatenate(
            [
                jnp.einsum("btos,btjs->oj", grad_res, operand, preferred_element_type=jnp.float32)
                for operand in (gated, hop_one, hop_two)
            ],
            axis=1,
        )
        * res_scale
    )
    d_mix_b = jnp.sum(grad_res, axis=(0, 1, 3), dtype=jnp.float32) * res_scale
    back_mix = (
        jnp.einsum("oj,btos->btjs", w_mix, grad_res, preferred_element_type=jnp.float32) * res_scale
    )
    dz_two = back_mix[:, :, 2 * C :].astype(jnp.bfloat16).reshape(row_total, TILES_DEV, TILE)
    dz_one = (
        back_mix[:, :, C : 2 * C]
        + adjoint(dz_two, offsets, adj_vals).reshape(BR, OUTPUT_STEPS, C, seg_width)
    ).astype(jnp.bfloat16)
    dz_zero = back_mix[:, :, :C] + adjoint(
        dz_one.reshape(row_total, TILES_DEV, TILE), offsets, adj_vals
    ).reshape(BR, OUTPUT_STEPS, C, seg_width)
    skip_back = (
        jnp.einsum("sc,bsn->bcn", w_skip, grad_skip, preferred_element_type=jnp.float32)
        * skip_scale
    )
    dz_zero = dz_zero.at[:, OUTPUT_STEPS - 1].add(skip_back)
    d_skip = (
        jnp.einsum("bsn,bcn->sc", grad_skip, last_step, preferred_element_type=jnp.float32)
        * skip_scale
    )
    d_skip_b = jnp.sum(grad_skip, axis=(0, 2), dtype=jnp.float32) * skip_scale
    d_filt = (dz_zero * gate_arr * (1.0 - filt_arr * filt_arr)).astype(jnp.bfloat16)
    d_gt = (dz_zero * filt_arr * gate_arr * (1.0 - gate_arr)).astype(jnp.bfloat16)
    d_filter = jnp.stack(
        [
            jnp.einsum("btos,btis->oi", d_filt, lower, preferred_element_type=jnp.float32),
            jnp.einsum("btos,btis->oi", d_filt, upper_bound, preferred_element_type=jnp.float32),
        ]
    )
    d_gate = jnp.stack(
        [
            jnp.einsum("btos,btis->oi", d_gt, lower, preferred_element_type=jnp.float32),
            jnp.einsum("btos,btis->oi", d_gt, upper_bound, preferred_element_type=jnp.float32),
        ]
    )
    d_filter_b = jnp.sum(d_filt, axis=(0, 1, 3), dtype=jnp.float32)
    d_gate_b = jnp.sum(d_gt, axis=(0, 1, 3), dtype=jnp.float32)
    backward_low = jnp.einsum(
        "oi,btos->btis", w_filter[0], d_filt, preferred_element_type=jnp.float32
    ) + jnp.einsum("oi,btos->btis", w_gate[0], d_gt, preferred_element_type=jnp.float32)
    backward_high = (
        jnp.einsum("oi,btos->btis", w_filter[1], d_filt, preferred_element_type=jnp.float32)
        + jnp.einsum("oi,btos->btis", w_gate[1], d_gt, preferred_element_type=jnp.float32)
        + grad_res.astype(jnp.float32) * res_scale
    )
    start_weight_gradient = jnp.sum(
        backward_low * signal_series[:, :OUTPUT_STEPS, None, :], axis=(0, 1, 3)
    ) + jnp.sum(backward_high * signal_series[:, DILATION_SIZE:, None, :], axis=(0, 1, 3))
    d_start_b = jnp.sum(backward_low, axis=(0, 1, 3)) + jnp.sum(backward_high, axis=(0, 1, 3))
    summed_grads = lax.psum(
        (
            start_weight_gradient,
            d_start_b,
            d_filter,
            d_filter_b,
            d_gate,
            d_gate_b,
            d_mix,
            d_mix_b,
            d_skip,
            d_skip_b,
        ),
        ("seg", "rep"),
    )
    return (
        res_out,
        skip_out,
        summed_grads[0],
        summed_grads[1],
        summed_grads[2],
        summed_grads[3],
        summed_grads[4],
        summed_grads[5],
        summed_grads[6],
        summed_grads[7],
        summed_grads[8],
        summed_grads[9],
    )


def solution(mesh):
    placed = (
        P(("rep", "seg"), None),
        P(),
        P(),
        P(),
        P(),
        P(),
        P(),
        P("seg", None),
        P("seg", None, None, None),
        P(),
        P(),
        P(),
        P(),
        P("rep", None, None, "seg"),
        P("rep", None, "seg"),
    )
    return jax.shard_map(
        body,
        mesh=mesh,
        in_specs=placed,
        out_specs=(
            P("rep", None, None, "seg"),
            P("rep", None, "seg"),
            P(),
            P(),
            P(),
            P(),
            P(),
            P(),
            P(),
            P(),
            P(),
            P(),
        ),
        check_vma=False,
    )
```

profile of v0, /device:TPU:0, one launch (start us, length us, event | category | flops | bytes accessed | tf_op | source)
XLA Modules:
  0.0 418.4 jit_solution(4189370211536466682)
XLA Ops:
  0.7 3.7 multiply_bitcast_fusion
  4.4 4.6 %copy-done.2 = f32[2,32,96,512]{3,2,1,0:T(8,128)} copy-done((f32[2,32,96,512]{3,2,1,0:T(8,128)}, f32[2,32,96,512]{3,2,1,0:T(8,128)S(1)}, u32[]{:S(2)}) %copy-start.2) | copy-done | bytes 12582936
  10.6 2.5 reshape.126
  13.1 2.6 fusion.42
  15.8 2.7 fusion.40
  18.4 2.7 fusion.38
  21.4 3.9 broadcast.81.clone
  25.3 9.0 %scatter_fusion = f32[2048,8,128]{2,0,1:T(8,128)} fusion(f32[2048,8,128]{2,0,1:T(8,128)} %broadcast.81.clone, s32[4]{0:T(128)S(1)} %get-tuple-element.66, f32[4,2048,128]{2,1,0:T(8,128)} %fusion.42), kind=kCustom, calls=%fused_computation.6 | custom fusion | flops 1048576 | bytes 12582928 | tf_op jit(solution)/shard_map/scatter-add | solution.py:71
  34.3 9.0 %scatter_fusion.1 = f32[2048,8,128]{2,0,1:T(8,128)} fusion(f32[2048,8,128]{2,0,1:T(8,128)} %scatter_fusion, s32[4]{0:T(128)S(1)} %get-tuple-element.67, f32[4,2048,128]{2,1,0:T(8,128)} %fusion.40), kind=kCustom, calls=%fused_computation.7 | custom fusion | flops 1048576 | bytes 12582928 | tf_op jit(solution)/shard_map/scatter-add | solution.py:71
  43.3 9.0 %scatter_fusion.2 = f32[2048,8,128]{2,0,1:T(8,128)} fusion(f32[2048,8,128]{2,0,1:T(8,128)} %scatter_fusion.1, s32[4]{0:T(128)S(1)} %get-tuple-element.65, f32[4,2048,128]{2,1,0:T(8,128)} %fusion.38), kind=kCustom, calls=%fused_computation.8 | custom fusion | flops 1048576 | bytes 12582928 | tf_op jit(solution)/shard_map/scatter-add | solution.py:71
  52.2 4.0 convert.12
  57.8 2.5 collective-permute-start.4
  61.6 10.5 %all-to-all-start = ((f32[3,32,512]{2,0,1:T(4,128)}), f32[3,32,512]{2,0,1:T(4,128)S(1)}, u32[]{:S(2)}, u32[]{:S(2)}) async-start(f32[3,32,512]{2,0,1:T(4,128)} %bitcast.272), calls=%async_computation | async-start | bytes 524288 | tf_op jit(solution)/shard_map/all_to_all | solution.py:117
  73.3 9.3 %all-to-all-done = f32[3,32,512]{2,0,1:T(4,128)S(1)} async-done(((f32[3,32,512]{2,0,1:T(4,128)}), f32[3,32,512]{2,0,1:T(4,128)S(1)}, u32[]{:S(2)}, u32[]{:S(2)}) %all-to-all-start) | async-done | bytes 196640 | tf_op jit(solution)/shard_map/all_to_all | solution.py:117
  84.3 3.0 fusion.48
  87.2 3.1 slice_add_fusion.5
  90.7 10.0 %copy.83 = f32[2048,4,128]{2,1,0:T(4,128)} copy(f32[2048,4,128]{2,0,1:T(8,128)S(1)} %pad_maximum_fusion.2) | data formatting | bytes 8388608 | tf_op jit(solution)/shard_map/concatenate | solution.py:83
  100.7 5.5 %reshape.127 = f32[2,32,32,512]{3,2,1,0:T(8,128)} reshape(f32[2048,4,128]{2,1,0:T(4,128)} %copy.83) | data formatting | bytes 8388608 | tf_op jit(solution)/shard_map/reshape | solution.py:184
  106.1 5.6 %fusion.1 = bf16[2,32,32,512]{3,2,1,0:T(8,128)(2,1)} fusion(f32[2,32,32,512]{3,2,1,0:T(8,128)} %reshape.127, f32[2,32,96,512]{3,2,1,0:T(8,128)} %copy-done.2), kind=kLoop, calls=%fused_computation.19 | loop fusion | flops 2097152 | bytes 10485760 | tf_op jit(solution)/shard_map/convert_element_type | solution.py:185
  111.7 4.0 reshape.128
  115.7 4.5 %fusion.36 = f32[4,2048,128]{2,1,0:T(8,128)} fusion(bf16[2048,4,128]{2,1,0:T(4,128)(2,1)} %reshape.128, bf16[4,3,128,128]{3,2,1,0:T(8,128)(2,1)S(1)} %copy-done.22), kind=kOutput, calls=%fused_computation.79 | convolution fusion | flops 268435456 | bytes 6422528 | tf_op jit(solution)/shard_map/htg,tgd->htd/dot_general | solution.py:65
  120.1 2.6 fusion.34
  122.8 2.7 fusion.32
  125.5 3.9 broadcast.81
  129.3 9.0 %scatter_fusion.3 = f32[2048,8,128]{2,0,1:T(8,128)} fusion(f32[2048,8,128]{2,0,1:T(8,128)} %broadcast.81, s32[4]{0:T(128)S(1)} %get-tuple-element.66, f32[4,2048,128]{2,1,0:T(8,128)} %fusion.36), kind=kCustom, calls=%fused_computation.9 | custom fusion | flops 1048576 | bytes 12582928 | tf_op jit(solution)/shard_map/scatter-add | solution.py:71
  138.3 9.4 %scatter_fusion.4 = f32[2048,8,128]{2,0,1:T(8,128)} fusion(f32[2048,8,128]{2,0,1:T(8,128)} %scatter_fusion.3, s32[4]{0:T(128)S(1)} %get-tuple-element.67, f32[4,2048,128]{2,1,0:T(8,128)} %fusion.34), kind=kCustom, calls=%fused_computation.10 | custom fusion | flops 1048576 | bytes 12582928 | tf_op jit(solution)/shard_map/scatter-add | solution.py:71
  147.7 9.0 %scatter_fusion.5 = f32[2048,8,128]{2,0,1:T(8,128)} fusion(f32[2048,8,128]{2,0,1:T(8,128)} %scatter_fusion.4, s32[4]{0:T(128)S(1)} %get-tuple-element.65, f32[4,2048,128]{2,1,0:T(8,128)} %fusion.32), kind=kCustom, calls=%fused_computation.11 | custom fusion | flops 1048576 | bytes 12582928 | tf_op jit(solution)/shard_map/scatter-add | solution.py:71
  156.6 4.0 convert.13
  160.9 2.6 collective-permute-start.6
  164.8 2.8 fusion.50
  168.2 2.8 add_tanh_fusion
  173.3 10.0 %copy.87 = f32[2048,4,128]{2,1,0:T(4,128)} copy(f32[2048,4,128]{2,0,1:T(8,128)S(1)} %pad_maximum_fusion.3) | data formatting | bytes 8388608 | tf_op jit(solution)/shard_map/concatenate | solution.py:83
  183.3 5.5 %reshape.129 = f32[2,32,32,512]{3,2,1,0:T(8,128)} reshape(f32[2048,4,128]{2,1,0:T(4,128)} %copy.87) | data formatting | bytes 8388608 | tf_op jit(solution)/shard_map/reshape | solution.py:188
  188.8 4.7 %slice_add_fusion.1 = f32[2,32,32,512]{3,2,1,0:T(8,128)S(1)} fusion(f32[2,32,32,512]{3,2,1,0:T(8,128)} %reshape.129, f32[2,32,96,512]{3,2,1,0:T(8,128)} %copy-done.2), kind=kLoop, calls=%fused_computation.20 | loop fusion | flops 1048576 | bytes 12582912 | tf_op jit(solution)/shard_map/add | solution.py:186
  195.5 3.4 convert_reduce_fusion.1
  201.7 2.8 fusion.111
  204.5 2.8 fusion.114
  207.6 2.6 fusion.105
  210.2 3.9 copy.66
  216.0 11.2 %collective-permute-start = (bf16[2048,256]{0,1:T(8,128)(2,1)S(1)}, bf16[2048,256]{0,1:T(8,128)(2,1)S(1)}, u32[]{:S(2)}, u32[]{:S(2)}) collective-permute-start(bf16[2048,256]{0,1:T(8,128)(2,1)S(1)} %get-tuple-element.98), channel_id=1, source_target_pairs={{0,4},{4,8},{8,12},{12,16},{16,20},{20,24},{24,28},{28,32},{32,36}... | collective-permute-start | bytes 3145736 | tf_op jit(solution)/shard_map/ppermute | solution.py:32
  229.9 2.8 fusion.138
  235.0 2.3 pad_maximum_fusion
  237.2 6.5 %copy.69 = bf16[2048,8,128]{2,0,1:T(8,128)(2,1)} copy(bf16[2048,8,128]{0,2,1:T(8,128)(2,1)} %bitcast.269) | data formatting | bytes 8388608 | tf_op jit(solution)/shard_map/reshape | solution.py:140
  243.7 4.3 %gather_fusion.1 = bf16[4,2048,128]{2,1,0:T(8,128)(2,1)} fusion(bf16[2048,8,128]{2,0,1:T(8,128)(2,1)} %copy.69, s32[1024]{0:T(1024)S(1)} %pad_clamp_fusion.1), kind=kCustom, calls=%fused_computation.1.clone | custom fusion | bytes 4194320 | tf_op jit(solution)/shard_map/jit(_take)/gather | solution.py:46
  248.0 4.4 %gather_fusion = bf16[4,2048,128]{2,1,0:T(8,128)(2,1)} fusion(bf16[2048,8,128]{2,0,1:T(8,128)(2,1)} %copy.69, s32[1024]{0:T(1024)S(1)} %pad_clamp_fusion.2), kind=kCustom, calls=%fused_computation.clone | custom fusion | bytes 4194320 | tf_op jit(solution)/shard_map/jit(_take)/gather | solution.py:46
  252.4 4.3 %gather_fusion.2 = bf16[4,2048,128]{2,1,0:T(8,128)(2,1)} fusion(bf16[2048,8,128]{2,0,1:T(8,128)(2,1)} %copy.69, s32[1024]{0:T(1024)S(1)} %pad_clamp_fusion), kind=kCustom, calls=%fused_computation.2.clone | custom fusion | bytes 4194320 | tf_op jit(solution)/shard_map/jit(_take)/gather | solution.py:46
  256.8 2.5 fusion.16
  264.6 11.2 %collective-permute-start.2 = (bf16[2048,256]{0,1:T(8,128)(2,1)}, bf16[2048,256]{0,1:T(8,128)(2,1)}, u32[]{:S(2)}, u32[]{:S(2)}) collective-permute-start(bf16[2048,256]{0,1:T(8,128)(2,1)} %get-tuple-element.96), channel_id=1, source_target_pairs={{0,4},{4,8},{8,12},{12,16},{16,20},{20,24},{24,28},{28,32},{32,36}... | collective-permute-start | bytes 3145736 | tf_op jit(solution)/shard_map/ppermute | solution.py:32
  278.0 2.3 convolution_bitcast_fusion.3
  280.3 4.3 %copy.75 = bf16[2048,4,128]{2,1,0:T(4,128)(2,1)} copy(bf16[2048,4,128]{0,2,1:T(8,128)(2,1)} %bitcast.266) | data formatting | bytes 4194304 | tf_op jit(solution)/shard_map/convert_element_type | solution.py:143
  284.6 4.1 reshape.122
  288.7 2.4 convolution_bitcast_fusion.2
  291.1 2.7 fusion.103
  293.8 3.4 pad_maximum_fusion.1
  297.3 6.5 %copy.76 = bf16[2048,8,128]{2,0,1:T(8,128)(2,1)} copy(bf16[2048,8,128]{0,2,1:T(8,128)(2,1)} %bitcast.270) | data formatting | bytes 8388608 | tf_op jit(solution)/shard_map/reshape | solution.py:146
  303.8 4.4 %gather_fusion.4 = bf16[4,2048,128]{2,1,0:T(8,128)(2,1)} fusion(bf16[2048,8,128]{2,0,1:T(8,128)(2,1)} %copy.76, s32[1024]{0:T(1024)S(1)} %pad_clamp_fusion.1), kind=kCustom, calls=%fused_computation.4.clone | custom fusion | bytes 4194320 | tf_op jit(solution)/shard_map/jit(_take)/gather | solution.py:46
  308.2 4.3 %gather_fusion.3 = bf16[4,2048,128]{2,1,0:T(8,128)(2,1)} fusion(bf16[2048,8,128]{2,0,1:T(8,128)(2,1)} %copy.76, s32[1024]{0:T(1024)S(1)} %pad_clamp_fusion.2), kind=kCustom, calls=%fused_computation.3.clone | custom fusion | bytes 4194320 | tf_op jit(solution)/shard_map/jit(_take)/gather | solution.py:46
  312.5 4.3 %gather_fusion.5 = bf16[4,2048,128]{2,1,0:T(8,128)(2,1)} fusion(bf16[2048,8,128]{2,0,1:T(8,128)(2,1)} %copy.76, s32[1024]{0:T(1024)S(1)} %pad_clamp_fusion), kind=kCustom, calls=%fused_computation.5.clone | custom fusion | bytes 4194320 | tf_op jit(solution)/shard_map/jit(_take)/gather | solution.py:46
  316.8 2.5 fusion.11
  321.7 10.7 %copy.79 = bf16[2048,4,128]{2,1,0:T(4,128)(2,1)} copy(bf16[2048,4,128]{2,0,1:T(8,128)(2,1)S(1)} %fusion.9) | data formatting | bytes 4194304 | tf_op jit(solution)/shard_map/convert_element_type | solution.py:147
  332.4 4.1 reshape.125
  336.5 2.4 convolution_bitcast_fusion.1
  339.0 6.5 %fusion.2 = bf16[2,32,32,512]{3,2,1,0:T(8,128)(2,1)} fusion(f32[2,32,512,32]{2,3,1,0:T(8,128)} %fusion.105, f32[2,32,512,32]{2,3,1,0:T(8,128)} %fusion.103, bf16[2,32,32,512]{3,2,1,0:T(8,128)(2,1)} %reshape.125, f32[32]{0:T(128)S(1)} %copy-done.30, bf16[2,48,32,512]{3,2,1,0:T(8,128)(2,1)S(1)} %copy-done.6, bf16[32,96]{1,0:T(8,128)(2,1)S(1)} %copy-done.26), kind=kOutput, calls=%fused_computation.26 | convolution fusion | flops 73400320 | bytes 14686336 | tf_op jit(solution)/shard_map/oj,btjs->btos/dot_general | solution.py:156
  345.6 72.6 %all-reduce = (f32[32]{0:T(128)}, f32[32]{0:T(128)}, f32[2,32,32]{2,1,0:T(8,128)}, f32[32]{0:T(128)}, f32[2,32,32]{2,1,0:T(8,128)}, /*index=5*/f32[32]{0:T(128)}...) all-reduce(f32[32]{0:T(128)S(1)} %add.259, ...), channel_id=1, replica_groups=mesh['seg'=32,'rep'=4] {'seg','rep'}, use_global_device_ids=true, to_apply=%region_8.10 | all-reduce | flops 15776 | bytes 126208 | tf_op jit(solution)/shard_map/psum | solution.py:227
  (133 shorter events, 33.8 us)
Async XLA Ops:
  0.6 192.8 %copy-start = (bf16[256,32]{0,1:T(8,128)(2,1)S(1)}, bf16[256,32]{0,1:T(8,128)(2,1)}, u32[]{:S(2)}) copy-start(bf16[256,32]{0,1:T(8,128)(2,1)} %param.30) | copy-start | bytes 49156
  4.4 4.6 %copy-start.2 = (f32[2,32,96,512]{3,2,1,0:T(8,128)}, f32[2,32,96,512]{3,2,1,0:T(8,128)S(1)}, u32[]{:S(2)}) copy-start(f32[2,32,96,512]{3,2,1,0:T(8,128)S(1)} %multiply_bitcast_fusion) | copy-start | bytes 37748740
  8.9 4.2 %copy-start.22 = (bf16[4,3,128,128]{3,2,1,0:T(8,128)(2,1)S(1)}, bf16[4,3,128,128]{3,2,1,0:T(8,128)(2,1)}, u32[]{:S(2)}) copy-start(bf16[4,3,128,128]{3,2,1,0:T(8,128)(2,1)} %param.27) | copy-start | bytes 1179652
  18.4 2.7 copy-start.31
  56.3 15.8 %copy-start.1 = (bf16[2,32,32,512]{3,2,1,0:T(8,128)(2,1)S(1)}, bf16[2,32,32,512]{3,2,1,0:T(8,128)(2,1)}, u32[]{:S(2)}) copy-start(bf16[2,32,32,512]{3,2,1,0:T(8,128)(2,1)} %param.32) | copy-start | bytes 6291460
  56.3 16.3 %copy-start.23 = (bf16[2,256,512]{2,1,0:T(8,128)(2,1)S(1)}, bf16[2,256,512]{2,1,0:T(8,128)(2,1)}, u32[]{:S(2)}) copy-start(bf16[2,256,512]{2,1,0:T(8,128)(2,1)} %param.33) | copy-start | bytes 1572868
  56.3 26.4 %copy-start.33 = (f32[32]{0:T(128)S(1)}, f32[32]{0:T(128)}, u32[]{:S(2)}) copy-start(f32[32]{0:T(128)} %param.21) | copy-start | bytes 388
  57.8 29.4 %collective-permute-start.4 = (bf16[2048,2,128]{2,0,1:T(8,128)(2,1)}, bf16[2048,2,128]{2,0,1:T(8,128)(2,1)}, u32[]{:S(2)}, u32[]{:S(2)}) collective-permute-start(bf16[2048,2,128]{2,0,1:T(8,128)(2,1)} %get-tuple-element.94), channel_id=1, source_target_pairs={{0,4},{4,8},{8,12},{12,16},{16,20},{20,24},{24,28},{28,32},{32,36}... | collective-permute-start | bytes 3145736 | tf_op jit(solution)/shard_map/ppermute | solution.py:21
  60.3 26.9 %collective-permute-start.5 = (bf16[2048,2,128]{2,0,1:T(8,128)(2,1)}, bf16[2048,2,128]{2,0,1:T(8,128)(2,1)}, u32[]{:S(2)}, u32[]{:S(2)}) collective-permute-start(bf16[2048,2,128]{2,0,1:T(8,128)(2,1)} %get-tuple-element.95), channel_id=1, source_target_pairs={{4,0},{8,4},{12,8},{16,12},{20,16},{24,20},{28,24},{32,28},{36,32}... | collective-permute-start | bytes 3145736 | tf_op jit(solution)/shard_map/ppermute | solution.py:21
  61.6 21.0 %all-to-all-start = ((f32[3,32,512]{2,0,1:T(4,128)}), f32[3,32,512]{2,0,1:T(4,128)S(1)}, u32[]{:S(2)}, u32[]{:S(2)}) async-start(f32[3,32,512]{2,0,1:T(4,128)} %bitcast.272), calls=%async_computation | async-start | bytes 524288 | tf_op jit(solution)/shard_map/all_to_all | solution.py:117
  72.1 12.1 %copy-start.27 = (bf16[2,32,32]{2,1,0:T(8,128)(2,1)S(1)}, bf16[2,32,32]{2,1,0:T(8,128)(2,1)}, u32[]{:S(2)}) copy-start(bf16[2,32,32]{2,1,0:T(8,128)(2,1)} %param.22) | copy-start | bytes 12292
  84.2 3.0 copy-start.3
  115.7 4.5 %copy-start.7 = (bf16[2048,4,128]{2,1,0:T(4,128)(2,1)S(1)}, bf16[2048,4,128]{2,1,0:T(4,128)(2,1)}, u32[]{:S(2)}) copy-start(bf16[2048,4,128]{2,1,0:T(4,128)(2,1)} %reshape.128) | copy-start | bytes 6291460
  160.7 4.1 copy-start.4
  160.7 4.1 copy-start.28
  160.7 6.9 %copy-start.29 = (f32[32]{0:T(128)S(1)}, f32[32]{0:T(128)}, u32[]{:S(2)}) copy-start(f32[32]{0:T(128)} %param.23) | copy-start | bytes 388
  160.9 10.1 %collective-permute-start.6 = (bf16[2048,2,128]{2,0,1:T(8,128)(2,1)S(1)}, bf16[2048,2,128]{2,0,1:T(8,128)(2,1)S(1)}, u32[]{:S(2)}, u32[]{:S(2)}) collective-permute-start(bf16[2048,2,128]{2,0,1:T(8,128)(2,1)S(1)} %get-tuple-element.92), channel_id=1, source_target_pairs={{0,4},{4,8},{8,12},{12,16},{16,20},{20,24},{24,28},{28,32},{32,36}... | collective-permute-start | bytes 3145736 | tf_op jit(solution)/shard_map/ppermute | solution.py:21
  163.4 7.6 %collective-permute-start.7 = (bf16[2048,2,128]{2,0,1:T(8,128)(2,1)S(1)}, bf16[2048,2,128]{2,0,1:T(8,128)(2,1)S(1)}, u32[]{:S(2)}, u32[]{:S(2)}) collective-permute-start(bf16[2048,2,128]{2,0,1:T(8,128)(2,1)S(1)} %get-tuple-element.93), channel_id=1, source_target_pairs={{4,0},{8,4},{12,8},{16,12},{20,16},{24,20},{28,24},{32,28},{36,32}... | collective-permute-start | bytes 3145736 | tf_op jit(solution)/shard_map/ppermute | solution.py:21
  164.7 3.4 copy-start.13
  164.8 6.2 %slice-start = ((s8[8388608]{0:T(1024)(128)(4,1)}), s8[4194304]{0:T(1024)(128)(4,1)S(1)}, s32[]{:S(2)}) async-start(s8[8388608]{0:T(1024)(128)(4,1)} %bitcast.263), calls=%async_computation.1 | async-start | bytes 8388608
  168.2 4.5 %slice-start.1 = ((s8[8388608]{0:T(1024)(128)(4,1)}), s8[4194304]{0:T(1024)(128)(4,1)S(1)}, s32[]{:S(2)}) async-start(s8[8388608]{0:T(1024)(128)(4,1)} %bitcast.263), calls=%async_computation.2 | async-start | bytes 8388608
  188.7 4.9 %copy-start.5 = (bf16[2,48,32,512]{3,2,1,0:T(8,128)(2,1)S(1)}, bf16[2,48,32,512]{3,2,1,0:T(8,128)(2,1)}, u32[]{:S(2)}) copy-start(bf16[2,48,32,512]{3,2,1,0:T(8,128)(2,1)} %copy-done.3) | copy-start | bytes 9437188
  188.7 5.6 %copy-start.24 = (f32[2,32,512,32]{2,3,1,0:T(8,128)S(1)}, f32[2,32,512,32]{2,3,1,0:T(8,128)}, u32[]{:S(2)}) copy-start(f32[2,32,512,32]{2,3,1,0:T(8,128)} %fusion.50) | copy-start | bytes 12582916
  188.7 6.8 %copy-start.25 = (f32[2,32,512,32]{2,3,1,0:T(8,128)S(1)}, f32[2,32,512,32]{2,3,1,0:T(8,128)}, u32[]{:S(2)}) copy-start(f32[2,32,512,32]{2,3,1,0:T(8,128)} %add_tanh_fusion) | copy-start | bytes 12582916
  188.7 6.8 %copy-start.35 = (f32[32]{0:T(128)S(1)}, f32[32]{0:T(128)}, u32[]{:S(2)}) copy-start(f32[32]{0:T(128)} %param.25) | copy-start | bytes 388
  199.0 1.4 copy-start.20
  199.0 8.5 %copy-start.10 = (bf16[2,32,32,512]{3,2,1,0:T(8,128)(2,1)}, bf16[2,32,32,512]{3,2,1,0:T(8,128)(2,1)S(1)}, u32[]{:S(2)}) copy-start(bf16[2,32,32,512]{3,2,1,0:T(8,128)(2,1)S(1)} %get-tuple-element.87) | copy-start | bytes 6291460
  204.5 3.1 copy-start.26
  214.1 14.6 %copy-start.32 = (f32[256]{0:T(256)S(1)}, f32[256]{0:T(256)}, u32[]{:S(2)}) copy-start(f32[256]{0:T(256)} %param.31) | copy-start | bytes 3076
  214.1 15.8 %copy-start.15 = (f32[2,32,512,32]{2,3,1,0:T(8,128)S(1)}, f32[2,32,512,32]{2,3,1,0:T(8,128)}, u32[]{:S(2)}) copy-start(f32[2,32,512,32]{2,3,1,0:T(8,128)} %fusion.114) | copy-start | bytes 12582916
  216.0 18.8 %collective-permute-start = (bf16[2048,256]{0,1:T(8,128)(2,1)S(1)}, bf16[2048,256]{0,1:T(8,128)(2,1)S(1)}, u32[]{:S(2)}, u32[]{:S(2)}) collective-permute-start(bf16[2048,256]{0,1:T(8,128)(2,1)S(1)} %get-tuple-element.98), channel_id=1, source_target_pairs={{0,4},{4,8},{8,12},{12,16},{16,20},{20,24},{24,28},{28,32},{32,36}... | collective-permute-start | bytes 3145736 | tf_op jit(solution)/shard_map/ppermute | solution.py:32
  227.2 7.5 %collective-permute-start.1 = (bf16[2048,256]{0,1:T(8,128)(2,1)S(1)}, bf16[2048,256]{0,1:T(8,128)(2,1)S(1)}, u32[]{:S(2)}, u32[]{:S(2)}) collective-permute-start(bf16[2048,256]{0,1:T(8,128)(2,1)S(1)} %get-tuple-element.99), channel_id=1, source_target_pairs={{4,0},{8,4},{12,8},{16,12},{20,16},{24,20},{28,24},{32,28},{36,32}... | collective-permute-start | bytes 3145736 | tf_op jit(solution)/shard_map/ppermute | solution.py:34
  229.9 2.9 copy-start.14
  229.9 3.5 copy-start.21
  233.4 1.6 copy-start.12
  256.8 2.5 copy-start.19
  259.3 1.6 copy-start.18
  261.7 1.4 copy-start.8
  264.6 29.3 %collective-permute-start.2 = (bf16[2048,256]{0,1:T(8,128)(2,1)}, bf16[2048,256]{0,1:T(8,128)(2,1)}, u32[]{:S(2)}, u32[]{:S(2)}) collective-permute-start(bf16[2048,256]{0,1:T(8,128)(2,1)} %get-tuple-element.96), channel_id=1, source_target_pairs={{0,4},{4,8},{8,12},{12,16},{16,20},{20,24},{24,28},{28,32},{32,36}... | collective-permute-start | bytes 3145736 | tf_op jit(solution)/shard_map/ppermute | solution.py:32
  275.7 18.1 %collective-permute-start.3 = (bf16[2048,256]{0,1:T(8,128)(2,1)}, bf16[2048,256]{0,1:T(8,128)(2,1)}, u32[]{:S(2)}, u32[]{:S(2)}) collective-permute-start(bf16[2048,256]{0,1:T(8,128)(2,1)} %get-tuple-element.97), channel_id=1, source_target_pairs={{4,0},{8,4},{12,8},{16,12},{20,16},{24,20},{28,24},{32,28},{36,32}... | collective-permute-start | bytes 3145736 | tf_op jit(solution)/shard_map/ppermute | solution.py:34
  288.7 2.4 copy-start.11
  291.1 2.7 copy-start.9
  316.8 2.5 copy-start.17
  319.3 1.6 copy-start.16
  336.5 2.5 copy-start.6
  336.5 2.5 copy-start.30
  339.0 6.5 %copy-start.34 = (f32[32]{0:T(128)S(1)}, f32[32]{0:T(128)}, u32[]{:S(2)}) copy-start(f32[32]{0:T(128)} %broadcast_multiply_fusion.1) | copy-start | bytes 388
where the time goes:
time: 427 us; the launch traced here: 418 us
  local copies, waits for them, and re-layouts  132 us (31%)
  other arithmetic  85.4 us (20%)
  matrix products  74.6 us (17%)
  blocking collectives  72.6 us (17%)
  starting transfers between devices  43.2 us (10%)
  waiting for transfers between devices  9.33 us (2%)
    psum x1, blocking collectives, body(): lax.psum((start_weight_gradient, d_start_b, d_filter, d_filter_b, d_gate,...  72.6 us
    scatter-add x6, other arithmetic, spread_back(): widened = widened.at[:, targets[:, column_vector]].add(matrix_product)  54.2 us
    gather x6, local copies, waits for them, and re-layouts, diffuse(): selected_entries = jnp.take(source, places[:, column_vector], axis=1)  26.1 us
    ppermute x2, starting transfers between devices, extended_2(): lax.ppermute(tail, axis, [(i, (i + 1) % count) for i in range(ends)])  22.4 us
    concatenate x2, local copies, waits for them, and re-layouts, adjoint(): jnp.concatenate([own_part[:, :R] + low_part, own_part[:, R:tile_count - R...  20 us
    dot_general x6, matrix products, spread_back(): jnp.einsum('htg,tgd->htd', receptive_input, block_list[:, column_vector],...  17.7 us
    unnamed x77, local copies, waits for them, and re-layouts  13.6 us
    convert_element_type x1, local copies, waits for them, and re-layouts, body(): hop_two_t = diffuse(extended_one, offsets, adj_vals, R).astype(jnp.bfloat16)  10.7 us
  transfers between devices with their start and end apart: 9, of which 1 were waited for; matrix products, arithmetic and copies ran while one was open for 8% of the time, Pallas kernels for 0%

commit v1 on v0

v1 whole, which is shorter than its diff:
```python
import math

import jax
import jax.numpy as jnp
from jax import lax
from jax.experimental import pallas as pl
from jax.experimental.pallas import tpu as pltpu
from jax.sharding import PartitionSpec as P

C = 32
SKIP = 256
TILE = 128
DIL = 16
TOUT = 32
T_IN = 48
BR = 2
TILES = 4
W = TILES * TILE
PAIR = 2 * TILE
TG = 8
ROWS = TG * C
F32 = jnp.float32
BF16 = jnp.bfloat16
A0F, A1F, CF, A0G, A1G, CG, WS, BS, BM = range(9)
PAY = 104
VMEM_LIMIT = 40 * 1024 * 1024


def dot(a, b):
    return jnp.dot(a, b, preferred_element_type=F32)


def dot_nt(a, b):
    return lax.dot_general(a, b, (((1,), (1,)), ((), ())), preferred_element_type=F32)


def column(row):
    n = row.shape[1]
    r = lax.broadcasted_iota(jnp.int32, (n, n), 0)
    c = lax.broadcasted_iota(jnp.int32, (n, n), 1)
    return jnp.sum(jnp.where(r == c, jnp.broadcast_to(row, (n, n)), 0.0), axis=1, keepdims=True)


def block_diag(w):
    row = jnp.concatenate([w] * TG, axis=1)
    full = jnp.concatenate([row] * TG, axis=0)
    r = lax.broadcasted_iota(jnp.int32, (ROWS, ROWS), 0) // C
    c = lax.broadcasted_iota(jnp.int32, (ROWS, ROWS), 1) // C
    return jnp.where(r == c, full, 0.0)


def prep_kernel(
    cl, co, cr, ws, bs, wf, bf, wg, bg, wm, bm, wmt, vl, vo, vr, coef, mix, mixt, band, bandt
):
    wrow, brow = ws[...], bs[...]

    def put(i, col):
        coef[i * C : (i + 1) * C, :] = jnp.broadcast_to(col, (C, TILE))

    def lane_sum(m):
        return jnp.sum(m, axis=1, keepdims=True)

    for w, bias, base, scale in ((wf, bf, A0F, 1.0), (wg, bg, A0G, 0.5)):
        w0, w1 = w[0].astype(F32), w[1].astype(F32)
        put(base, lane_sum(w0 * wrow) * scale)
        put(base + 1, lane_sum(w1 * wrow) * scale)
        put(base + 2, (lane_sum((w0 + w1) * brow) + column(bias[...])) * scale)
    put(WS, column(wrow))
    put(BS, column(brow))
    put(BM, column(bm[...]))
    for h in range(3):
        mix[:, h * ROWS : (h + 1) * ROWS] = block_diag(
            wm[:, h * C : (h + 1) * C].astype(F32)
        ).astype(BF16)
        mixt[:, h * ROWS : (h + 1) * ROWS] = block_diag(
            wmt[h * C : (h + 1) * C, :].astype(F32)
        ).astype(BF16)

    band[...] = jnp.zeros_like(band)
    bandt[...] = jnp.zeros_like(bandt)
    base = lax.axis_index("seg") * TILES - TILES
    for src, (cols, vals) in enumerate(((cl, vl), (co, vo), (cr, vr))):

        def place(n, carry, src=src, cols=cols, vals=vals):
            r, k = n // 3, n % 3
            rel = cols[r, k] - base

            @pl.when(jnp.logical_and(rel >= 0, rel < 3 * TILES))
            def _():
                block = vals[r, k]
                at = pl.multiple_of(rel * TILE, TILE)
                row = pl.multiple_of((src * TILES + r) * TILE, TILE)
                band[pl.ds(row, TILE), pl.ds(at, TILE)] = block
                bandt[pl.ds(at, TILE), pl.ds(row, TILE)] = block.T

            return carry

        lax.fori_loop(0, TILES * 3, place, 0)


def two_hops(ext, one, band, p_one, p_two):
    for p in range(4):
        one[:, p * PAIR : (p + 1) * PAIR] = dot(
            ext[:, p * PAIR : (p + 3) * PAIR],
            band[p * PAIR : (p + 3) * PAIR, (p + 1) * PAIR : (p + 2) * PAIR],
        ).astype(BF16)
    for p in range(2):
        p_two(
            p,
            dot(
                one[:, p * PAIR : (p + 3) * PAIR],
                band[(p + 1) * PAIR : (p + 4) * PAIR, (p + 2) * PAIR : (p + 3) * PAIR],
            ).astype(BF16),
        )


def coefs(coef, *which):
    return [coef[i * C : (i + 1) * C, :] for i in which]


def forward_kernel(x0, x1, coef, mix, bandt, res, zext, one, stack):
    def step(t, carry):
        a0f, a1f, cf, a0g, a1g, cg = coefs(coef, A0F, A1F, CF, A0G, A1G, CG)
        lanes = pl.ds(pl.multiple_of(t * TILE, TILE), TILE)
        for k in range(TG):
            p = x0[0, k : k + 1, lanes]
            q = x1[0, k : k + 1, lanes]
            f = jnp.tanh(a0f * p + a1f * q + cf)
            g = 0.5 * jnp.tanh(a0g * p + a1g * q + cg) + 0.5
            zext[k * C : (k + 1) * C, lanes] = (f * g).astype(BF16)
        return carry

    lax.fori_loop(0, 3 * TILES, step, 0)
    stack[0:ROWS, :] = zext[:, W : 2 * W]

    def put(p, v):
        stack[2 * ROWS : 3 * ROWS, p * PAIR : (p + 1) * PAIR] = v

    two_hops(zext, one, bandt, None, put)
    stack[ROWS : 2 * ROWS, :] = one[:, PAIR : PAIR + W]
    mixed = dot(mix[...], stack[...])
    ws, bs, bm = coefs(coef, WS, BS, BM)
    bb = bs + bm
    for k in range(TG):
        for t in range(TILES):
            q = x1[0, k : k + 1, W + t * TILE : W + (t + 1) * TILE]
            r, lanes = slice(k * C, (k + 1) * C), slice(t * TILE, (t + 1) * TILE)
            res[r, lanes] = (mixed[r, lanes] + (ws * q + bb)).astype(BF16)


def backward_kernel(
    x0, x1, coef, mixt, wsk, wskt, bsk, band, gl, go, gr, gs,
    skip, pay, ext, one, stack, zb, dzs, acc, dmx, dsk,
):
    i = pl.program_id(0)
    last = i % 4 == 3
    res_scale = 1.0 / math.sqrt(8 * TOUT * 16384)
    skip_scale = 1.0 / math.sqrt(8 * 16384)

    @pl.when(i == 0)
    def _():
        acc[...] = jnp.zeros_like(acc)
        dmx[...] = jnp.zeros_like(dmx)
        dsk[...] = jnp.zeros_like(dsk)

    ext[:, 0:W] = gl[...]
    ext[:, W : 2 * W] = go[...]
    ext[:, 2 * W : 3 * W] = gr[...]
    stack[0:ROWS, :] = go[...]

    def put(p, v):
        stack[2 * ROWS : 3 * ROWS, p * PAIR : (p + 1) * PAIR] = v

    two_hops(ext, one, band, None, put)
    stack[ROWS : 2 * ROWS, :] = one[:, PAIR : PAIR + W]
    dzs[...] = dot(mixt[...], stack[...]) * res_scale

    @pl.when(last)
    def _():
        dzs[ROWS - C : ROWS, :] += dot(wskt[...], gs[0]) * skip_scale

    a0f, a1f, cf, a0g, a1g, cg = coefs(coef, A0F, A1F, CF, A0G, A1G, CG)
    sums = [acc[j] for j in range(8)]
    for k in range(TG):
        for t in range(TILES):
            r, lanes = slice(k * C, (k + 1) * C), slice(t * TILE, (t + 1) * TILE)
            p = x0[0, k : k + 1, W + t * TILE : W + (t + 1) * TILE]
            q = x1[0, k : k + 1, W + t * TILE : W + (t + 1) * TILE]
            f = jnp.tanh(a0f * p + a1f * q + cf)
            g = 0.5 * jnp.tanh(a0g * p + a1g * q + cg) + 0.5
            zb[r, lanes] = (f * g).astype(BF16)
            dg = dzs[r, lanes] * g
            df = dg * (1.0 - f * f)
            dgt = dg * f * (1.0 - g)
            e = go[r, lanes].astype(F32)
            for j, term in enumerate((df * p, df * q, df, dgt * p, dgt * q, dgt, e * q, e)):
                sums[j] = sums[j] + term
    for j in range(8):
        acc[j] = sums[j]
    dmx[...] += dot_nt(stack[...], zb[...])

    @pl.when(last)
    def _():
        z31 = zb[ROWS - C : ROWS, :]
        ones = jnp.ones((16, W), BF16)
        dsk[...] += dot_nt(jnp.concatenate([z31, ones], axis=0), gs[0])
        skip[0] = (dot(wsk[...], z31) + bsk[...]).astype(BF16)

    @pl.when(i == 7)
    def _():
        r = lax.broadcasted_iota(jnp.int32, (ROWS, ROWS), 0) // C
        c = lax.broadcasted_iota(jnp.int32, (ROWS, ROWS), 1) // C
        lane = lax.broadcasted_iota(jnp.int32, (C, TILE), 1)
        packed = jnp.zeros((C, TILE), F32)
        for h in range(3):
            m = jnp.where(r == c, dmx[h * ROWS : (h + 1) * ROWS, :], 0.0)
            v = m[0:C]
            for k in range(1, TG):
                v = v + m[k * C : (k + 1) * C]
            v = v[:, :TILE] + v[:, TILE:]
            v = v + pltpu.roll(v, 64, 1)
            v = v + pltpu.roll(v, 32, 1)
            packed = jnp.where(lane // C == h, v, packed)
        for j in range(8):
            s = jnp.sum(acc[j], axis=1, keepdims=True)
            packed = jnp.where(lane == 96 + j, s, packed)
        pay[0:C, :] = packed
        pay[C : 2 * C, :] = dsk[0:C, 0:TILE]
        pay[2 * C : 3 * C, :] = dsk[0:C, TILE:]
        sub = lax.broadcasted_iota(jnp.int32, (8, TILE), 0)
        pay[3 * C : PAY, :] = jnp.where(sub == 0, dsk[C : C + 8, 0:TILE], dsk[C : C + 8, TILE:])


def finish_kernel(
    p0, p1, p2, p3, ws, bs, wf, wg,
    swg, dsb, dfil, dfb, dgat, dgb, dmix, dmixb, dskip, dskipb,
):
    res_scale = 1.0 / math.sqrt(8 * TOUT * 16384)
    skip_scale = 1.0 / math.sqrt(8 * 16384)
    v = (p0[...] + p1[...]) + (p2[...] + p3[...])
    wrow, brow = ws[...], bs[...]
    head = v[0:C]
    rows = head.T
    uf0, uf1, fb, ug0, ug1, gb = (head[:, 96 + j : 97 + j] for j in range(6))
    dmix[...] = head[:, 0:96] * res_scale
    dfil[0] = uf0 * wrow + fb * brow
    dfil[1] = uf1 * wrow + fb * brow
    dgat[0] = ug0 * wrow + gb * brow
    dgat[1] = ug1 * wrow + gb * brow
    dfb[...] = rows[98:99]
    dgb[...] = rows[101:102]
    mb = rows[103:104] * res_scale
    dmixb[...] = mb
    f0, f1, g0, g1 = wf[0].astype(F32), wf[1].astype(F32), wg[0].astype(F32), wg[1].astype(F32)
    swg[...] = (
        jnp.sum(f0 * uf0 + f1 * uf1 + g0 * ug0 + g1 * ug1, axis=0, keepdims=True)
        + rows[102:103] * res_scale
    )
    dsb[...] = jnp.sum((f0 + f1) * fb + (g0 + g1) * gb, axis=0, keepdims=True) + mb
    dskip[0:TILE, :] = v[C : 2 * C].T * skip_scale
    dskip[TILE:, :] = v[2 * C : 3 * C].T * skip_scale
    dskipb[:, 0:TILE] = v[3 * C : 3 * C + 1] * skip_scale
    dskipb[:, TILE:] = v[3 * C + 1 : 3 * C + 2] * skip_scale


def neighbour(value, steps):
    count = lax.axis_size("seg")
    pairs = [(i, i + steps) for i in range(max(0, -steps), min(count, count - steps))]
    return lax.ppermute(value, "seg", pairs)


def seg_ring(value, shift):
    return lax.ppermute(value, "seg", [(i, shift(i)) for i in range(lax.axis_size("seg"))])


def whole(shape):
    return pl.BlockSpec(shape, lambda *_: (0,) * len(shape))


def params(**kw):
    return pltpu.CompilerParams(vmem_limit_bytes=VMEM_LIMIT, **kw)


VMEM = pl.BlockSpec(memory_space=pltpu.VMEM)
SMEM = pl.BlockSpec(memory_space=pltpu.SMEM)


def body(
    speeds, w_start, b_start, w_filter, b_filter, w_gate, b_gate, adj_cols, adj_vals,
    w_mix, b_mix, w_skip, b_skip, grad_res, grad_skip,
):
    rows = BR * TOUT * C
    grad = grad_res.reshape(rows, W)
    x = lax.all_to_all(speeds.astype(BF16), "seg", split_axis=1, concat_axis=0, tiled=True)
    grad_l, grad_r = neighbour(grad, 1), neighbour(grad, -1)
    vals_l, vals_r = neighbour(adj_vals, 1), neighbour(adj_vals, -1)
    cols_l, cols_r = neighbour(adj_cols, 1), neighbour(adj_cols, -1)
    x_l, x_r = neighbour(x, 1), neighbour(x, -1)
    xs = jnp.concatenate([x_l, x, x_r], axis=1).astype(F32).reshape(BR * T_IN // TG, TG, 3 * W)

    ws, bs = w_start.reshape(1, C), b_start.reshape(1, C)
    coef, mix, mixt, band, bandt = pl.pallas_call(
        prep_kernel,
        out_shape=(
            jax.ShapeDtypeStruct((9 * C, TILE), F32),
            jax.ShapeDtypeStruct((ROWS, 3 * ROWS), BF16),
            jax.ShapeDtypeStruct((ROWS, 3 * ROWS), BF16),
            jax.ShapeDtypeStruct((3 * W, 3 * W), BF16),
            jax.ShapeDtypeStruct((3 * W, 3 * W), BF16),
        ),
        in_specs=[SMEM] * 3 + [VMEM] * 12,
        out_specs=(VMEM,) * 5,
        compiler_params=params(),
        name="prep",
    )(
        cols_l, adj_cols, cols_r, ws, bs, w_filter, b_filter.reshape(1, C), w_gate,
        b_gate.reshape(1, C), w_mix, b_mix.reshape(1, C), w_mix.T, vals_l, adj_vals, vals_r,
    )

    early = pl.BlockSpec((1, TG, 3 * W), lambda i: ((i // 4) * 6 + i % 4, 0, 0))
    late = pl.BlockSpec((1, TG, 3 * W), lambda i: ((i // 4) * 6 + i % 4 + 2, 0, 0))
    slab = pl.BlockSpec((ROWS, W), lambda i: (i, 0))
    res = pl.pallas_call(
        forward_kernel,
        grid=(8,),
        out_shape=jax.ShapeDtypeStruct((rows, W), BF16),
        in_specs=[early, late, whole((9 * C, TILE)), whole((ROWS, 3 * ROWS)), whole((3 * W, 3 * W))],
        out_specs=slab,
        scratch_shapes=[
            pltpu.VMEM((ROWS, 3 * W), BF16),
            pltpu.VMEM((ROWS, 2 * W), BF16),
            pltpu.VMEM((3 * ROWS, W), BF16),
        ],
        compiler_params=params(),
        name="forward",
    )(xs, xs, coef, mix, bandt)

    per_sample = pl.BlockSpec((1, SKIP, W), lambda i: (i // 4, 0, 0))
    skip, pay = pl.pallas_call(
        backward_kernel,
        grid=(8,),
        out_shape=(
            jax.ShapeDtypeStruct((BR, SKIP, W), BF16),
            jax.ShapeDtypeStruct((PAY, TILE), F32),
        ),
        in_specs=[
            early, late, whole((9 * C, TILE)), whole((ROWS, 3 * ROWS)), whole((SKIP, C)),
            whole((C, SKIP)), whole((SKIP, 1)), whole((3 * W, 3 * W)), slab, slab, slab, per_sample,
        ],
        out_specs=(per_sample, whole((PAY, TILE))),
        scratch_shapes=[
            pltpu.VMEM((ROWS, 3 * W), BF16),
            pltpu.VMEM((ROWS, 2 * W), BF16),
            pltpu.VMEM((3 * ROWS, W), BF16),
            pltpu.VMEM((ROWS, W), BF16),
            pltpu.VMEM((ROWS, W), F32),
            pltpu.VMEM((8, C, TILE), F32),
            pltpu.VMEM((3 * ROWS, ROWS), F32),
            pltpu.VMEM((C + 16, SKIP), F32),
        ],
        compiler_params=params(),
        name="backward",
    )(
        xs, xs, coef, mixt, w_skip, w_skip.T, b_skip.reshape(SKIP, 1), band,
        grad_l, grad, grad_r, grad_skip,
    )

    v = pay
    v = v + seg_ring(v, lambda i: i ^ 1)
    v = v + sum(seg_ring(v, lambda i, k=k: (i // 8) * 8 + ((i // 2 + k) % 4) * 2 + i % 2) for k in (1, 2, 3))
    v = v + sum(seg_ring(v, lambda i, k=k: (i + 8 * k) % 32) for k in (1, 2, 3))
    others = [lax.ppermute(v, "rep", [(i, (i + k) % 4) for i in range(4)]) for k in (1, 2, 3)]

    row = jax.ShapeDtypeStruct((1, C), F32)
    taps = jax.ShapeDtypeStruct((2, C, C), F32)
    swg, dsb, dfil, dfb, dgat, dgb, dmix, dmixb, dskip, dskipb = pl.pallas_call(
        finish_kernel,
        out_shape=(
            row, row, taps, row, taps, row, jax.ShapeDtypeStruct((C, 3 * C), F32), row,
            jax.ShapeDtypeStruct((SKIP, C), F32), jax.ShapeDtypeStruct((1, SKIP), F32),
        ),
        in_specs=[VMEM] * 8,
        out_specs=(VMEM,) * 10,
        compiler_params=params(),
        name="finish",
    )(v, *others, ws, bs, w_filter, w_gate)
    vec = lambda a: a.reshape(-1)
    return (
        res.reshape(BR, TOUT, C, W), skip, vec(swg), vec(dsb), dfil, vec(dfb), dgat, vec(dgb),
        dmix, vec(dmixb), dskip, vec(dskipb),
    )


def solution(mesh):
    placed = (
        P(("rep", "seg"), None), P(), P(), P(), P(), P(), P(), P("seg", None),
        P("seg", None, None, None), P(), P(), P(), P(), P("rep", None, None, "seg"),
        P("rep", None, "seg"),
    )
    return jax.shard_map(
        body,
        mesh=mesh,
        in_specs=placed,
        out_specs=(P("rep", None, None, "seg"), P("rep", None, "seg")) + (P(),) * 10,
        check_vma=False,
    )
```

time: 427 us -> 146 us (0.34); the launches traced: 418 us -> 145 us
  local copies, waits for them, and re-layouts: 132 us -> 16.7 us
  other arithmetic: 85.4 us -> 1.09 us
  matrix products: 74.6 us -> 0 us
  blocking collectives: 72.6 us -> 30.2 us
  Pallas kernels: 0 us -> 40.1 us
    dot_general x34 -> x0, matrix products: 74.6 us -> none  [the longest x6 17.7 us: spread_back(): jnp.einsum('htg,tgd->htd', receptive_input, block_list[:, column_vector],...]
    psum x1 -> x0, blocking collectives: 72.6 us -> none  [body(): lax.psum((start_weight_gradient, d_start_b, d_filter, d_filter_b, d_gate,...]
    scatter-add x6 -> x0, other arithmetic: 54.2 us -> none  [spread_back(): widened = widened.at[:, targets[:, column_vector]].add(matrix_product)]
    reshape x9 -> x1, local copies, waits for them, and re-layouts: 42.7 us -> 1.47 us  [body(): b_skip.reshape(SKIP, 1)]
    pallas_call x0 -> x4, Pallas kernels: none -> 40.1 us  [the longest x1 19.2 us: body(): pl.pallas_call(backward_kernel, grid=(8,), out_shape=(jax.ShapeDtypeStruc...]
    all_to_all x0 -> x1, blocking collectives: none -> 30.2 us  [body(): lax.all_to_all(speeds.astype(BF16), 'seg', split_axis=1, concat_axis=0, t...]
    gather x6 -> x0, local copies, waits for them, and re-layouts: 26.1 us -> none  [diffuse(): selected_entries = jnp.take(source, places[:, column_vector], axis=1)]
    concatenate x2 -> x1, local copies, waits for them, and re-layouts: 20 us -> 0.08 us  [body(): jnp.concatenate([x_l, x, x_r], axis=1).astype(F32)]
  transfers between devices with their start and end apart: 9 -> 18, of which waited for: 1 -> 7; matrix products, arithmetic and copies ran while one was open for 8% -> 3% of each run, Pallas kernels for 0% -> 14%
where the time goes in v1:
time: 146 us; the launch traced here: 145 us
  starting transfers between devices  44.2 us (30%)
  Pallas kernels  40.1 us (27%)
  blocking collectives  30.2 us (21%)
  local copies, waits for them, and re-layouts  16.7 us (11%)
  waiting for transfers between devices  11.7 us (8%)
    all_to_all x1, blocking collectives, body(): lax.all_to_all(speeds.astype(BF16), 'seg', split_axis=1, concat_axis=0, t...  30.2 us
    ppermute x7, starting transfers between devices, seg_ring(): lax.ppermute(value, 'seg', [(i, shift(i)) for i in range(lax.axis_size('s...  19.6 us
    pallas_call x1, Pallas kernels, body(): pl.pallas_call(backward_kernel, grid=(8,), out_shape=(jax.ShapeDtypeStruc...  19.2 us
    ppermute x8, starting transfers between devices, neighbour(): return lax.ppermute(value, 'seg', pairs)  18.9 us
    pallas_call x1, Pallas kernels, body(): pl.pallas_call(forward_kernel, grid=(8,), out_shape=jax.ShapeDtypeStruct(...  15.6 us
    unnamed x49, local copies, waits for them, and re-layouts  15.1 us
    ppermute x7, waiting for transfers between devices, seg_ring(): lax.ppermute(value, 'seg', [(i, shift(i)) for i in range(lax.axis_size('s...  8.71 us
    ppermute x3, starting transfers between devices, body(): lax.ppermute(v, 'rep', [(i, (i + k) % 4) for i in range(4)])  5.72 us
  transfers between devices with their start and end apart: 18, of which 7 were waited for; matrix products, arithmetic and copies ran while one was open for 3% of the time, Pallas kernels for 14%

profile of v1, /device:TPU:0, one launch (start us, length us, event | category | flops | bytes accessed | tf_op | source)
XLA Modules:
  0.0 144.8 jit_solution(7224640983402387972)
XLA Ops:
  0.7 2.8 %collective-permute-start.6 = (bf16[2048,512]{1,0:T(8,128)(2,1)}, bf16[2048,512]{1,0:T(8,128)(2,1)}, u32[]{:S(2)}, u32[]{:S(2)}) collective-permute-start(bf16[2048,512]{1,0:T(8,128)(2,1)} %bitcast.20), channel_id=1, source_target_pairs={{0,4},{4,8},{8,12},{12,16},{16,20},{20,24},{24,28},{28,32},{32,36}... | collective-permute-start | bytes 6291464 | tf_op jit(solution)/shard_map/ppermute | solution.py:269
  3.4 1.3 collective-permute-start.7
  4.7 1.0 convert_element_type.7
  5.7 30.2 %all_to_all.19 = bf16[3,32,512]{2,0,1:T(4,128)(2,1)S(1)} all-to-all(bf16[3,32,512]{2,0,1:T(4,128)(2,1)S(1)} %bitcast.35), channel_id=1, replica_groups=mesh['seg'=32,'rep'=4] {'seg'}, dimensions={1} | all-to-all | bytes 196608 | tf_op jit(solution)/shard_map/all_to_all | solution.py:294
  35.9 0.1 all_to_all.17
  36.0 1.3 collective-permute-start.1
  37.3 3.1 %collective-permute-start.4 = (bf16[4,3,128,128]{3,2,1,0:T(8,128)(2,1)}, bf16[4,3,128,128]{3,2,1,0:T(8,128)(2,1)S(1)}, u32[]{:S(2)}, u32[]{:S(2)}) collective-permute-start(bf16[4,3,128,128]{3,2,1,0:T(8,128)(2,1)} %vo.1), channel_id=1, source_target_pairs={{0,4},{4,8},{8,12},{12,16},{16,20},{20,24},{24,28},{28,32},{32,36}... | collective-permute-start | bytes 1179656 | tf_op jit(solution)/shard_map/ppermute | solution.py:269
  40.4 1.3 collective-permute-start.5
  41.7 0.0 collective-permute-done.1
  41.7 4.1 %collective-permute-start = (bf16[96,512]{1,0:T(8,128)(2,1)S(1)}, bf16[96,512]{1,0:T(8,128)(2,1)S(1)}, u32[]{:S(2)}, u32[]{:S(2)}) collective-permute-start(bf16[96,512]{1,0:T(8,128)(2,1)S(1)} %all_to_all.17), channel_id=1, source_target_pairs={{0,4},{4,8},{8,12},{12,16},{16,20},{20,24},{24,28},{28,32},{32,36}... | collective-permute-start | bytes 294920 | tf_op jit(solution)/shard_map/ppermute | solution.py:269
  45.8 0.8 copy.32
  46.6 1.4 copy.33.wsk
  48.0 1.5 %copy.34.bsk = f32[256,1]{1,0:T(8,128)} copy(f32[256,1]{0,1:T(1,128)} %bitcast.38) | data formatting | bytes 2048 | tf_op jit(solution)/shard_map/reshape | solution.py:364
  49.5 0.1 concatenate.11
  49.6 0.0 copy-start.2
  49.6 0.0 collective-permute-done
  49.6 3.8 %collective-permute-start.2 = (s32[4,3]{1,0:T(4,128)}, s32[4,3]{1,0:T(4,128)S(1)}, u32[]{:S(2)}, u32[]{:S(2)}) collective-permute-start(s32[4,3]{1,0:T(4,128)} %co.1), channel_id=1, source_target_pairs={{0,4},{4,8},{8,12},{12,16},{16,20},{20,24},{24,28},{28,32},{32,36}... | collective-permute-start | bytes 152 | tf_op jit(solution)/shard_map/ppermute | solution.py:269
  53.5 1.0 collective-permute-done.2.cl
  54.4 1.3 collective-permute-start.3
  55.7 2.0 %collective-permute-done.3.cr = s32[4,3]{1,0:T(4,128)S(1)} collective-permute-done((s32[4,3]{1,0:T(4,128)}, s32[4,3]{1,0:T(4,128)S(1)}, u32[]{:S(2)}, u32[]{:S(2)}) %collective-permute-start.3) | collective-permute-done | bytes 80 | tf_op jit(solution)/shard_map/ppermute | solution.py:269
  57.7 0.0 collective-permute-done.4.vl
  57.7 0.7 copy-done.4
  58.4 0.0 collective-permute-done.5.vr
  58.4 0.7 copy-done.6
  59.2 1.0 copy-done.3
  60.2 1.0 copy-done.5
  61.2 1.0 copy-done.7
  62.2 0.7 copy-done.10
  62.9 0.7 copy-done.12
  63.6 0.7 copy-done.14
  64.3 0.7 copy-done.15
  65.0 0.7 copy-done.16
  65.6 0.7 copy-done.18
  66.3 0.7 copy-done.20
  66.9 0.7 copy-done.21
  67.6 0.7 copy-done.22
  68.3 4.5 %prep.1 = (f32[288,128]{1,0:T(8,128)S(1)}, bf16[256,768]{1,0:T(8,128)(2,1)S(1)}, bf16[256,768]{1,0:T(8,128)(2,1)S(1)}, bf16[1536,1536]{1,0:T(8,128)(2,1)S(1)}, bf16[1536,1536]{1,0:T(8,128)(2,1)S(1)}) custom-call(s32[4,3]{1,0:T(4,128)S(1)} %collective-permute-done.2.cl, s32[4,3]{1,0:T(4,128)S(1)} %copy-done.15, s32[4,3]{1,0:T(4,128)S(1)} %collective-permute-done.3.cr, ...), custom_call_target="tpu_custom_call" | custom-call | tf_op jit(solution)/shard_map/prep/pallas_call | solution.py:302
  72.8 0.0 collective-permute-done.6.gl
  72.8 0.0 collective-permute-done.7.gr
  72.9 0.8 copy-done.8
  73.7 0.7 copy-done.9
  74.4 19.2 %backward.1 = (bf16[2,256,512]{2,1,0:T(8,128)(2,1)}, f32[104,128]{1,0:T(8,128)S(1)}) custom-call(f32[12,8,1536]{2,1,0:T(8,128)S(1)} %maximum_convert_fusion.x0.x1, f32[12,8,1536]{2,1,0:T(8,128)S(1)} %maximum_convert_fusion.x0.x1, f32[288,128]{1,0:T(8,128)S(1)} %get-tuple-element.29.coef, bf16[256,768]{1,0:T(8,128)(2,1)S(1)} %get-tuple-element.32.mixt, ...), custom_call_target="tpu_custom_call" | custom-call | tf_op jit(solution)/shard_map/backward/pallas_call | solution.py:339
  93.6 2.5 %collective-permute-start.8 = (f32[104,128]{1,0:T(8,128)S(1)}, f32[104,128]{1,0:T(8,128)S(1)}, u32[]{:S(2)}, u32[]{:S(2)}) collective-permute-start(f32[104,128]{1,0:T(8,128)S(1)} %get-tuple-element.35), channel_id=1, source_target_pairs={{0,4},{4,0},{8,12},{12,8},{16,20},{20,16},{24,28},{28,24},{32,36},... | collective-permute-start | bytes 159752 | tf_op jit(solution)/shard_map/ppermute | solution.py:273
  96.1 0.9 collective-permute-done.8
  97.0 10.8 %collective-permute-start.11 = (f32[104,128]{1,0:T(8,128)S(1)}, f32[104,128]{1,0:T(8,128)S(1)}, u32[]{:S(2)}, u32[]{:S(2)}) collective-permute-start(f32[104,128]{1,0:T(8,128)S(1)} %add.21), channel_id=1, source_target_pairs={{0,24},{4,28},{8,0},{12,4},{16,8},{20,12},{24,16},{28,20},{32,56},... | collective-permute-start | bytes 159752 | tf_op jit(solution)/shard_map/ppermute | solution.py:273
  107.9 0.0 collective-permute-start.9
  107.9 1.5 %collective-permute-start.10 = (f32[104,128]{1,0:T(8,128)S(1)}, f32[104,128]{1,0:T(8,128)S(1)}, u32[]{:S(2)}, u32[]{:S(2)}) collective-permute-start(f32[104,128]{1,0:T(8,128)S(1)} %add.21), channel_id=1, source_target_pairs={{0,16},{4,20},{8,24},{12,28},{16,0},{20,4},{24,8},{28,12},{32,48},... | collective-permute-start | bytes 159752 | tf_op jit(solution)/shard_map/ppermute | solution.py:273
  109.4 0.2 collective-permute-done.11
  109.6 4.4 %collective-permute-done.9 = f32[104,128]{1,0:T(8,128)S(1)} collective-permute-done((f32[104,128]{1,0:T(8,128)S(1)}, f32[104,128]{1,0:T(8,128)S(1)}, u32[]{:S(2)}, u32[]{:S(2)}) %collective-permute-start.9) | collective-permute-done | bytes 53280 | tf_op jit(solution)/shard_map/ppermute | solution.py:273
  114.1 0.0 collective-permute-done.10
  114.1 0.4 collective-permute-start.14
  114.5 1.8 %collective-permute-start.12 = (f32[104,128]{1,0:T(8,128)S(1)}, f32[104,128]{1,0:T(8,128)S(1)}, u32[]{:S(2)}, u32[]{:S(2)}) collective-permute-start(f32[104,128]{1,0:T(8,128)S(1)} %add_add_fusion.1), channel_id=1, source_target_pairs={{0,32},{4,36},{8,40},{12,44},{16,48},{20,52},{24,56},{28,60},{32,6... | collective-permute-start | bytes 159752 | tf_op jit(solution)/shard_map/ppermute | solution.py:273
  116.3 2.5 %collective-permute-start.13 = (f32[104,128]{1,0:T(8,128)S(1)}, f32[104,128]{1,0:T(8,128)S(1)}, u32[]{:S(2)}, u32[]{:S(2)}) collective-permute-start(f32[104,128]{1,0:T(8,128)S(1)} %add_add_fusion.1), channel_id=1, source_target_pairs={{0,64},{4,68},{8,72},{12,76},{16,80},{20,84},{24,88},{28,92},{32,9... | collective-permute-start | bytes 159752 | tf_op jit(solution)/shard_map/ppermute | solution.py:273
  118.8 0.0 collective-permute-done.14
  118.8 1.0 collective-permute-done.12
  119.8 2.1 %collective-permute-done.13 = f32[104,128]{1,0:T(8,128)S(1)} collective-permute-done((f32[104,128]{1,0:T(8,128)S(1)}, f32[104,128]{1,0:T(8,128)S(1)}, u32[]{:S(2)}, u32[]{:S(2)}) %collective-permute-start.13) | collective-permute-done | bytes 53280 | tf_op jit(solution)/shard_map/ppermute | solution.py:273
  122.0 1.6 %collective-permute-start.15 = (f32[104,128]{1,0:T(8,128)S(1)}, f32[104,128]{1,0:T(8,128)S(1)}, u32[]{:S(2)}, u32[]{:S(2)}) collective-permute-start(f32[104,128]{1,0:T(8,128)S(1)} %add_add_fusion.p0), channel_id=1, source_target_pairs={{0,1},{1,2},{2,3},{3,0},{4,5},{5,6},{6,7},{7,4},{8,9},{9,10},{10,1... | collective-permute-start | bytes 159752 | tf_op jit(solution)/shard_map/ppermute | solution.py:372
  123.5 2.7 %collective-permute-start.16 = (f32[104,128]{1,0:T(8,128)S(1)}, f32[104,128]{1,0:T(8,128)S(1)}, u32[]{:S(2)}, u32[]{:S(2)}) collective-permute-start(f32[104,128]{1,0:T(8,128)S(1)} %add_add_fusion.p0), channel_id=1, source_target_pairs={{0,2},{1,3},{2,0},{3,1},{4,6},{5,7},{6,4},{7,5},{8,10},{9,11},{10,... | collective-permute-start | bytes 159752 | tf_op jit(solution)/shard_map/ppermute | solution.py:372
  126.3 1.4 collective-permute-start.17
  127.7 15.6 %forward.1 = bf16[2048,512]{1,0:T(8,128)(2,1)} custom-call(f32[12,8,1536]{2,1,0:T(8,128)S(1)} %maximum_convert_fusion.x0.x1, f32[12,8,1536]{2,1,0:T(8,128)S(1)} %maximum_convert_fusion.x0.x1, f32[288,128]{1,0:T(8,128)S(1)} %get-tuple-element.29.coef, bf16[256,768]{1,0:T(8,128)(2,1)S(1)} %get-tuple-element.30.mix, bf16[1536,1536]{1,0:T(8,128)(2,1)S(1)} %get-tuple-element.31.bandt), custom_call_target="tpu_custom_call" | custom-call | tf_op jit(solution)/shard_map/forward/pallas_call | solution.py:323
  143.3 0.0 collective-permute-done.15.p1
  143.3 0.0 collective-permute-done.16.p2
  143.3 0.8 finish.1
  144.1 0.7 copy.35
  (34 shorter events, 0.1 us)
Async XLA Ops:
  0.6 72.2 %copy-start = (bf16[2,32,32,512]{3,2,1,0:T(8,128)(2,1)S(1)}, bf16[2,32,32,512]{3,2,1,0:T(8,128)(2,1)}, u32[]{:S(2)}) copy-start(bf16[2,32,32,512]{3,2,1,0:T(8,128)(2,1)} %param.28) | copy-start | bytes 6291460
  0.7 72.2 %collective-permute-start.6 = (bf16[2048,512]{1,0:T(8,128)(2,1)}, bf16[2048,512]{1,0:T(8,128)(2,1)}, u32[]{:S(2)}, u32[]{:S(2)}) collective-permute-start(bf16[2048,512]{1,0:T(8,128)(2,1)} %bitcast.20), channel_id=1, source_target_pairs={{0,4},{4,8},{8,12},{12,16},{16,20},{20,24},{24,28},{28,32},{32,36}... | collective-permute-start | bytes 6291464 | tf_op jit(solution)/shard_map/ppermute | solution.py:269
  3.4 69.4 %collective-permute-start.7 = (bf16[2048,512]{1,0:T(8,128)(2,1)}, bf16[2048,512]{1,0:T(8,128)(2,1)}, u32[]{:S(2)}, u32[]{:S(2)}) collective-permute-start(bf16[2048,512]{1,0:T(8,128)(2,1)} %bitcast.21), channel_id=1, source_target_pairs={{4,0},{8,4},{12,8},{16,12},{20,16},{24,20},{28,24},{32,28},{36,32}... | collective-permute-start | bytes 6291464 | tf_op jit(solution)/shard_map/ppermute | solution.py:269
  36.0 5.7 %collective-permute-start.1 = (bf16[96,512]{1,0:T(8,128)(2,1)S(1)}, bf16[96,512]{1,0:T(8,128)(2,1)S(1)}, u32[]{:S(2)}, u32[]{:S(2)}) collective-permute-start(bf16[96,512]{1,0:T(8,128)(2,1)S(1)} %all_to_all.17), channel_id=1, source_target_pairs={{4,0},{8,4},{12,8},{16,12},{20,16},{24,20},{28,24},{32,28},{36,32}... | collective-permute-start | bytes 294920 | tf_op jit(solution)/shard_map/ppermute | solution.py:269
  37.3 20.4 %collective-permute-start.4 = (bf16[4,3,128,128]{3,2,1,0:T(8,128)(2,1)}, bf16[4,3,128,128]{3,2,1,0:T(8,128)(2,1)S(1)}, u32[]{:S(2)}, u32[]{:S(2)}) collective-permute-start(bf16[4,3,128,128]{3,2,1,0:T(8,128)(2,1)} %vo.1), channel_id=1, source_target_pairs={{0,4},{4,8},{8,12},{12,16},{16,20},{20,24},{24,28},{28,32},{32,36}... | collective-permute-start | bytes 1179656 | tf_op jit(solution)/shard_map/ppermute | solution.py:269
  40.4 18.1 %collective-permute-start.5 = (bf16[4,3,128,128]{3,2,1,0:T(8,128)(2,1)}, bf16[4,3,128,128]{3,2,1,0:T(8,128)(2,1)S(1)}, u32[]{:S(2)}, u32[]{:S(2)}) collective-permute-start(bf16[4,3,128,128]{3,2,1,0:T(8,128)(2,1)} %vo.1), channel_id=1, source_target_pairs={{4,0},{8,4},{12,8},{16,12},{20,16},{24,20},{28,24},{32,28},{36,32}... | collective-permute-start | bytes 1179656 | tf_op jit(solution)/shard_map/ppermute | solution.py:269
  41.7 8.0 %collective-permute-start = (bf16[96,512]{1,0:T(8,128)(2,1)S(1)}, bf16[96,512]{1,0:T(8,128)(2,1)S(1)}, u32[]{:S(2)}, u32[]{:S(2)}) collective-permute-start(bf16[96,512]{1,0:T(8,128)(2,1)S(1)} %all_to_all.17), channel_id=1, source_target_pairs={{0,4},{4,8},{8,12},{12,16},{16,20},{20,24},{24,28},{28,32},{32,36}... | collective-permute-start | bytes 294920 | tf_op jit(solution)/shard_map/ppermute | solution.py:269
  49.6 23.2 %copy-start.1 = (f32[256,1]{1,0:T(8,128)S(1)}, f32[256,1]{1,0:T(8,128)}, u32[]{:S(2)}) copy-start(f32[256,1]{1,0:T(8,128)} %copy.34.bsk) | copy-start | bytes 3076
  49.6 23.2 %copy-start.2 = (bf16[2,256,512]{2,1,0:T(8,128)(2,1)S(1)}, bf16[2,256,512]{2,1,0:T(8,128)(2,1)}, u32[]{:S(2)}) copy-start(bf16[2,256,512]{2,1,0:T(8,128)(2,1)} %gs.1) | copy-start | bytes 1572868
  49.6 4.8 %collective-permute-start.2 = (s32[4,3]{1,0:T(4,128)}, s32[4,3]{1,0:T(4,128)S(1)}, u32[]{:S(2)}, u32[]{:S(2)}) collective-permute-start(s32[4,3]{1,0:T(4,128)} %co.1), channel_id=1, source_target_pairs={{0,4},{4,8},{8,12},{12,16},{16,20},{20,24},{24,28},{28,32},{32,36}... | collective-permute-start | bytes 152 | tf_op jit(solution)/shard_map/ppermute | solution.py:269
  54.4 3.3 %collective-permute-start.3 = (s32[4,3]{1,0:T(4,128)}, s32[4,3]{1,0:T(4,128)S(1)}, u32[]{:S(2)}, u32[]{:S(2)}) collective-permute-start(s32[4,3]{1,0:T(4,128)} %co.1), channel_id=1, source_target_pairs={{4,0},{8,4},{12,8},{16,12},{20,16},{24,20},{28,24},{32,28},{36,32}... | collective-permute-start | bytes 152 | tf_op jit(solution)/shard_map/ppermute | solution.py:269
  57.7 0.7 copy-start.4
  58.4 0.7 copy-start.6
  59.2 1.0 copy-start.3
  60.2 1.0 copy-start.5
  61.2 1.0 copy-start.7
  62.2 0.7 copy-start.10
  62.9 0.7 copy-start.12
  63.6 0.7 copy-start.14
  64.3 0.7 copy-start.15
  65.0 0.7 copy-start.16
  65.6 0.7 copy-start.18
  66.3 0.7 copy-start.20
  66.9 0.7 copy-start.21
  67.6 0.7 copy-start.22
  72.9 0.8 copy-start.8
  73.7 0.7 copy-start.9
  93.6 3.4 %collective-permute-start.8 = (f32[104,128]{1,0:T(8,128)S(1)}, f32[104,128]{1,0:T(8,128)S(1)}, u32[]{:S(2)}, u32[]{:S(2)}) collective-permute-start(f32[104,128]{1,0:T(8,128)S(1)} %get-tuple-element.35), channel_id=1, source_target_pairs={{0,4},{4,0},{8,12},{12,8},{16,20},{20,16},{24,28},{28,24},{32,36},... | collective-permute-start | bytes 159752 | tf_op jit(solution)/shard_map/ppermute | solution.py:273
  97.0 12.6 %collective-permute-start.11 = (f32[104,128]{1,0:T(8,128)S(1)}, f32[104,128]{1,0:T(8,128)S(1)}, u32[]{:S(2)}, u32[]{:S(2)}) collective-permute-start(f32[104,128]{1,0:T(8,128)S(1)} %add.21), channel_id=1, source_target_pairs={{0,24},{4,28},{8,0},{12,4},{16,8},{20,12},{24,16},{28,20},{32,56},... | collective-permute-start | bytes 159752 | tf_op jit(solution)/shard_map/ppermute | solution.py:273
  107.9 6.2 %collective-permute-start.9 = (f32[104,128]{1,0:T(8,128)S(1)}, f32[104,128]{1,0:T(8,128)S(1)}, u32[]{:S(2)}, u32[]{:S(2)}) collective-permute-start(f32[104,128]{1,0:T(8,128)S(1)} %add.21), channel_id=1, source_target_pairs={{0,8},{4,12},{8,16},{12,20},{16,24},{20,28},{24,0},{28,4},{32,40},... | collective-permute-start | bytes 159752 | tf_op jit(solution)/shard_map/ppermute | solution.py:273
  107.9 6.2 %collective-permute-start.10 = (f32[104,128]{1,0:T(8,128)S(1)}, f32[104,128]{1,0:T(8,128)S(1)}, u32[]{:S(2)}, u32[]{:S(2)}) collective-permute-start(f32[104,128]{1,0:T(8,128)S(1)} %add.21), channel_id=1, source_target_pairs={{0,16},{4,20},{8,24},{12,28},{16,0},{20,4},{24,8},{28,12},{32,48},... | collective-permute-start | bytes 159752 | tf_op jit(solution)/shard_map/ppermute | solution.py:273
  114.1 4.7 %collective-permute-start.14 = (f32[104,128]{1,0:T(8,128)S(1)}, f32[104,128]{1,0:T(8,128)S(1)}, u32[]{:S(2)}, u32[]{:S(2)}) collective-permute-start(f32[104,128]{1,0:T(8,128)S(1)} %add_add_fusion.1), channel_id=1, source_target_pairs={{0,96},{4,100},{8,104},{12,108},{16,112},{20,116},{24,120},{28,124... | collective-permute-start | bytes 159752 | tf_op jit(solution)/shard_map/ppermute | solution.py:273
  114.5 5.3 %collective-permute-start.12 = (f32[104,128]{1,0:T(8,128)S(1)}, f32[104,128]{1,0:T(8,128)S(1)}, u32[]{:S(2)}, u32[]{:S(2)}) collective-permute-start(f32[104,128]{1,0:T(8,128)S(1)} %add_add_fusion.1), channel_id=1, source_target_pairs={{0,32},{4,36},{8,40},{12,44},{16,48},{20,52},{24,56},{28,60},{32,6... | collective-permute-start | bytes 159752 | tf_op jit(solution)/shard_map/ppermute | solution.py:273
  116.3 5.6 %collective-permute-start.13 = (f32[104,128]{1,0:T(8,128)S(1)}, f32[104,128]{1,0:T(8,128)S(1)}, u32[]{:S(2)}, u32[]{:S(2)}) collective-permute-start(f32[104,128]{1,0:T(8,128)S(1)} %add_add_fusion.1), channel_id=1, source_target_pairs={{0,64},{4,68},{8,72},{12,76},{16,80},{20,84},{24,88},{28,92},{32,9... | collective-permute-start | bytes 159752 | tf_op jit(solution)/shard_map/ppermute | solution.py:273
  122.0 21.3 %collective-permute-start.15 = (f32[104,128]{1,0:T(8,128)S(1)}, f32[104,128]{1,0:T(8,128)S(1)}, u32[]{:S(2)}, u32[]{:S(2)}) collective-permute-start(f32[104,128]{1,0:T(8,128)S(1)} %add_add_fusion.p0), channel_id=1, source_target_pairs={{0,1},{1,2},{2,3},{3,0},{4,5},{5,6},{6,7},{7,4},{8,9},{9,10},{10,1... | collective-permute-start | bytes 159752 | tf_op jit(solution)/shard_map/ppermute | solution.py:372
  123.5 19.8 %collective-permute-start.16 = (f32[104,128]{1,0:T(8,128)S(1)}, f32[104,128]{1,0:T(8,128)S(1)}, u32[]{:S(2)}, u32[]{:S(2)}) collective-permute-start(f32[104,128]{1,0:T(8,128)S(1)} %add_add_fusion.p0), channel_id=1, source_target_pairs={{0,2},{1,3},{2,0},{3,1},{4,6},{5,7},{6,4},{7,5},{8,10},{9,11},{10,... | collective-permute-start | bytes 159752 | tf_op jit(solution)/shard_map/ppermute | solution.py:372
  126.3 17.0 %collective-permute-start.17 = (f32[104,128]{1,0:T(8,128)S(1)}, f32[104,128]{1,0:T(8,128)S(1)}, u32[]{:S(2)}, u32[]{:S(2)}) collective-permute-start(f32[104,128]{1,0:T(8,128)S(1)} %add_add_fusion.p0), channel_id=1, source_target_pairs={{0,3},{1,0},{2,1},{3,2},{4,7},{5,4},{6,5},{7,6},{8,11},{9,8},{10,9... | collective-permute-start | bytes 159752 | tf_op jit(solution)/shard_map/ppermute | solution.py:372
  127.7 15.6 %copy-start.11 = (bf16[2,32,32]{2,1,0:T(8,128)(2,1)S(1)}, bf16[2,32,32]{2,1,0:T(8,128)(2,1)}, u32[]{:S(2)}) copy-start(bf16[2,32,32]{2,1,0:T(8,128)(2,1)} %wf.3) | copy-start | bytes 12292
  127.7 15.6 %copy-start.13 = (bf16[2,32,32]{2,1,0:T(8,128)(2,1)S(1)}, bf16[2,32,32]{2,1,0:T(8,128)(2,1)}, u32[]{:S(2)}) copy-start(bf16[2,32,32]{2,1,0:T(8,128)(2,1)} %wg.3) | copy-start | bytes 12292
  127.7 15.6 %copy-start.17 = (f32[32]{0:T(128)S(1)}, f32[32]{0:T(128)}, u32[]{:S(2)}) copy-start(f32[32]{0:T(128)} %param.16) | copy-start | bytes 388
  127.7 15.6 %copy-start.19 = (f32[32]{0:T(128)S(1)}, f32[32]{0:T(128)}, u32[]{:S(2)}) copy-start(f32[32]{0:T(128)} %param.17) | copy-start | bytes 388

commit v2 on v1

v2 whole, which is shorter than its diff:
```python
import functools
import math

import jax
import jax.numpy as jnp
from jax import lax
from jax.experimental import pallas as pl
from jax.experimental.pallas import tpu as pltpu
from jax.sharding import PartitionSpec as P

C = 32
SKIP = 256
TILE = 128
DIL = 16
TOUT = 32
T_IN = 48
BR = 2
TILES = 4
W = TILES * TILE
PAIR = 2 * TILE
TG = 8
ROWS = TG * C
F32 = jnp.float32
BF16 = jnp.bfloat16
A0F, A1F, CF, A0G, A1G, CG, WS, BS, BM = range(9)
PAY = 104
VMEM_LIMIT = 40 * 1024 * 1024


def dot(a, b):
    return jnp.dot(a, b, preferred_element_type=F32)


def dot_nt(a, b):
    return lax.dot_general(a, b, (((1,), (1,)), ((), ())), preferred_element_type=F32)


def column(row):
    n = row.shape[1]
    r = lax.broadcasted_iota(jnp.int32, (n, n), 0)
    c = lax.broadcasted_iota(jnp.int32, (n, n), 1)
    return jnp.sum(jnp.where(r == c, jnp.broadcast_to(row, (n, n)), 0.0), axis=1, keepdims=True)


def block_diag(w):
    row = jnp.concatenate([w] * TG, axis=1)
    full = jnp.concatenate([row] * TG, axis=0)
    r = lax.broadcasted_iota(jnp.int32, (ROWS, ROWS), 0) // C
    c = lax.broadcasted_iota(jnp.int32, (ROWS, ROWS), 1) // C
    return jnp.where(r == c, full, 0.0)


def message_kernel(cols, speeds, msg, wide):
    wide[:, 0:W] = jnp.zeros((4, W), F32)
    wide[:, W + 16384 :] = jnp.zeros((4, W), F32)
    wide[0:3, W : W + 16384] = speeds[...]
    first = lax.axis_index("seg") * TILES
    offsets = jnp.concatenate(
        [
            jnp.broadcast_to((cols[t, k] - (first + t)).astype(F32), (4, TILE))
            for t in range(TILES)
            for k in range(3)
        ],
        axis=1,
    )
    row = lax.broadcasted_iota(jnp.int32, (4, 3 * W), 0)
    for d in range(32):
        msg[d] = jnp.where(row == 3, offsets, wide[:, d * W : (d + 3) * W]).astype(BF16)


def prep_kernel(
    ws, bs, wf, bf, wg, bg, wm, bm, wskt, bsk, vl, vo, vr, msg,
    coef, mix, mixt, wsk, bskc, band, bandt, xs,
):
    wrow, brow = ws[...], bs[...]

    def put(i, col):
        coef[i * C : (i + 1) * C, :] = jnp.broadcast_to(col, (C, TILE))

    def lane_sum(m):
        return jnp.sum(m, axis=1, keepdims=True)

    for w, bias, base, scale in ((wf, bf, A0F, 1.0), (wg, bg, A0G, 0.5)):
        w0, w1 = w[0].astype(F32), w[1].astype(F32)
        put(base, lane_sum(w0 * wrow) * scale)
        put(base + 1, lane_sum(w1 * wrow) * scale)
        put(base + 2, (lane_sum((w0 + w1) * brow) + column(bias[...])) * scale)
    put(WS, column(wrow))
    put(BS, column(brow))
    put(BM, column(bm[...]))
    for h in range(3):
        w = wm[:, h * C : (h + 1) * C].astype(F32)
        mix[:, h * ROWS : (h + 1) * ROWS] = block_diag(w).astype(BF16)
        mixt[:, h * ROWS : (h + 1) * ROWS] = block_diag(w.T).astype(BF16)
    wsk[...] = wskt[...].astype(F32).T.astype(BF16)
    bskc[...] = jnp.broadcast_to(column(bsk[...]), (SKIP, TILE))

    for i in range(32):
        xs[3 * i : 3 * i + 3, :] = msg[i].astype(F32)[0:3]

    def store(dst, row, col, v):
        j = col // 2 - 1
        at = row - 2 * j
        if 0 <= j < 4 and 0 <= at < 6:
            dst[j, at * TILE : (at + 1) * TILE, (col % 2) * TILE : (col % 2 + 1) * TILE] = v

    zero = jnp.zeros((TILE, TILE), BF16)
    for dst in (band, bandt):
        for j in range(4):
            dst[j, 0:TILE, TILE:] = zero
            dst[j, 5 * TILE :, 0:TILE] = zero
    seg = lax.axis_index("seg")
    for src, vals in enumerate((vl, vo, vr)):
        sender = jnp.clip(seg + src - 1, 0, 31)
        for t in range(TILES):
            m = src * TILES + t
            v0, v1, v2 = (vals[t, k] for k in range(3))
            u0, u1, u2 = v0.T, v1.T, v2.T

            def off(k, t=t, sender=sender):
                return msg[sender, :, (t * 3 + k) * TILE : (t * 3 + k + 1) * TILE].astype(F32)[3:4]

            o1, o2 = off(1), off(2)
            store(band, m, m, v0)
            store(bandt, m, m, u0)
            for o in (-2, -1, 1, 2):
                q = m + o
                if not 0 <= q < 12:
                    continue
                c2 = jnp.broadcast_to(jnp.where(o2 == o, 1.0, 0.0).astype(BF16), (TILE, TILE))
                v, u = c2 * v2, c2 * u2
                if abs(o) == 2:
                    c1 = jnp.broadcast_to(jnp.where(o1 == o, 1.0, 0.0).astype(BF16), (TILE, TILE))
                    v, u = v + c1 * v1, u + c1 * u1
                store(band, m, q, v)
                store(bandt, q, m, u)


def two_hops(ext, one, band, p_two):
    for p in range(4):
        one[:, p * PAIR : (p + 1) * PAIR] = dot(
            ext[:, p * PAIR : (p + 3) * PAIR], band[p]
        ).astype(BF16)
    for p in range(2):
        p_two(p, dot(one[:, p * PAIR : (p + 3) * PAIR], band[p + 1]).astype(BF16))


def coefs(coef, *which):
    return [coef[i * C : (i + 1) * C, :] for i in which]


def forward_kernel(base, xs, coef, mix, bandt, *refs):
    res, zext, one, stack = refs[-4:]
    i = pl.program_id(0) + base
    at = ((i // 4) * 6 + i % 4) * TG
    x0 = xs.at[pl.ds(pl.multiple_of(at, TG), TG)]
    x1 = xs.at[pl.ds(pl.multiple_of(at + DIL, TG), TG)]

    def step(t, carry):
        a0f, a1f, cf, a0g, a1g, cg = coefs(coef, A0F, A1F, CF, A0G, A1G, CG)
        lanes = pl.ds(pl.multiple_of(t * TILE, TILE), TILE)
        for k in range(TG):
            p = x0[k : k + 1, lanes]
            q = x1[k : k + 1, lanes]
            f = jnp.tanh(a0f * p + a1f * q + cf)
            g = 0.5 * jnp.tanh(a0g * p + a1g * q + cg) + 0.5
            zext[k * C : (k + 1) * C, lanes] = (f * g).astype(BF16)
        return carry

    lax.fori_loop(0, 3 * TILES, step, 0)
    stack[0:ROWS, :] = zext[:, W : 2 * W]

    def put(p, v):
        stack[2 * ROWS : 3 * ROWS, p * PAIR : (p + 1) * PAIR] = v

    two_hops(zext, one, bandt, put)
    stack[ROWS : 2 * ROWS, :] = one[:, PAIR : PAIR + W]
    mixed = dot(mix[...], stack[...])
    ws, bs, bm = coefs(coef, WS, BS, BM)
    bb = bs + bm
    for k in range(TG):
        for t in range(TILES):
            q = x1[k : k + 1, W + t * TILE : W + (t + 1) * TILE]
            r, lanes = slice(k * C, (k + 1) * C), slice(t * TILE, (t + 1) * TILE)
            res[r, lanes] = (mixed[r, lanes] + (ws * q + bb)).astype(BF16)


def backward_kernel(sample, xs, coef, mixt, wsk, wskt, bsk, band, gl, go, gr, gs, *refs):
    skip, pay, ext, one, stack, zb, dzs, acc, dmx, dsk = refs[-10:]
    i = pl.program_id(0)
    last = i == 3
    at = (sample * 6 + i) * TG
    x0 = xs.at[pl.ds(pl.multiple_of(at, TG), TG)]
    x1 = xs.at[pl.ds(pl.multiple_of(at + DIL, TG), TG)]
    res_scale = 1.0 / math.sqrt(8 * TOUT * 16384)
    skip_scale = 1.0 / math.sqrt(8 * 16384)

    @pl.when(i == 0)
    def _():
        acc[...] = jnp.zeros_like(acc)
        dmx[...] = jnp.zeros_like(dmx)
        dsk[...] = jnp.zeros_like(dsk)

    ext[:, 0:W] = gl[...]
    ext[:, W : 2 * W] = go[...]
    ext[:, 2 * W : 3 * W] = gr[...]
    stack[0:ROWS, :] = go[...]

    def put(p, v):
        stack[2 * ROWS : 3 * ROWS, p * PAIR : (p + 1) * PAIR] = v

    two_hops(ext, one, band, put)
    stack[ROWS : 2 * ROWS, :] = one[:, PAIR : PAIR + W]
    dzs[...] = dot(mixt[...], stack[...]) * res_scale

    @pl.when(last)
    def _():
        dzs[ROWS - C : ROWS, :] += dot(wskt[...], gs[0]) * skip_scale

    a0f, a1f, cf, a0g, a1g, cg = coefs(coef, A0F, A1F, CF, A0G, A1G, CG)
    sums = [acc[j] for j in range(8)]
    for k in range(TG):
        for t in range(TILES):
            r, lanes = slice(k * C, (k + 1) * C), slice(t * TILE, (t + 1) * TILE)
            p = x0[k : k + 1, W + t * TILE : W + (t + 1) * TILE]
            q = x1[k : k + 1, W + t * TILE : W + (t + 1) * TILE]
            f = jnp.tanh(a0f * p + a1f * q + cf)
            g = 0.5 * jnp.tanh(a0g * p + a1g * q + cg) + 0.5
            zb[r, lanes] = (f * g).astype(BF16)
            dg = dzs[r, lanes] * g
            df = dg * (1.0 - f * f)
            dgt = dg * f * (1.0 - g)
            e = go[r, lanes].astype(F32)
            for j, term in enumerate((df * p, df * q, df, dgt * p, dgt * q, dgt, e * q, e)):
                sums[j] = sums[j] + term
    for j in range(8):
        acc[j] = sums[j]
    dmx[...] += dot_nt(stack[...], zb[...])

    @pl.when(last)
    def _():
        z31 = zb[ROWS - C : ROWS, :]
        ones = jnp.ones((16, W), BF16)
        dsk[...] += dot_nt(jnp.concatenate([z31, ones], axis=0), gs[0])
        bias = jnp.concatenate([bsk[...]] * TILES, axis=1)
        skip[0] = (dot(wsk[...], z31) + bias).astype(BF16)

    @pl.when(last)
    def _():
        r = lax.broadcasted_iota(jnp.int32, (ROWS, ROWS), 0) // C
        c = lax.broadcasted_iota(jnp.int32, (ROWS, ROWS), 1) // C
        lane = lax.broadcasted_iota(jnp.int32, (C, TILE), 1)
        packed = jnp.zeros((C, TILE), F32)
        for h in range(3):
            m = jnp.where(r == c, dmx[h * ROWS : (h + 1) * ROWS, :], 0.0)
            v = m[0:C]
            for k in range(1, TG):
                v = v + m[k * C : (k + 1) * C]
            v = v[:, :TILE] + v[:, TILE:]
            v = v + pltpu.roll(v, 64, 1)
            v = v + pltpu.roll(v, 32, 1)
            packed = jnp.where(lane // C == h, v, packed)
        for j in range(8):
            s = jnp.sum(acc[j], axis=1, keepdims=True)
            packed = jnp.where(lane == 96 + j, s, packed)
        pay[0:C, :] = packed
        pay[C : 2 * C, :] = dsk[0:C, 0:TILE]
        pay[2 * C : 3 * C, :] = dsk[0:C, TILE:]
        sub = lax.broadcasted_iota(jnp.int32, (8, TILE), 0)
        pay[3 * C : PAY, :] = jnp.where(sub == 0, dsk[C : C + 8, 0:TILE], dsk[C : C + 8, TILE:])


def finish_kernel(
    p0, p1, p2, p3, ws, bs, wf, wg,
    swg, dsb, dfil, dfb, dgat, dgb, dmix, dmixb, dskip, dskipb,
):
    res_scale = 1.0 / math.sqrt(8 * TOUT * 16384)
    skip_scale = 1.0 / math.sqrt(8 * 16384)
    v = (p0[...] + p1[...]) + (p2[...] + p3[...])
    wrow, brow = ws[...], bs[...]
    head = v[0:C]
    rows = head.T
    uf0, uf1, fb, ug0, ug1, gb = (head[:, 96 + j : 97 + j] for j in range(6))
    dmix[...] = head[:, 0:96] * res_scale
    dfil[0] = uf0 * wrow + fb * brow
    dfil[1] = uf1 * wrow + fb * brow
    dgat[0] = ug0 * wrow + gb * brow
    dgat[1] = ug1 * wrow + gb * brow
    dfb[...] = rows[98:99]
    dgb[...] = rows[101:102]
    mb = rows[103:104] * res_scale
    dmixb[...] = mb
    f0, f1, g0, g1 = wf[0].astype(F32), wf[1].astype(F32), wg[0].astype(F32), wg[1].astype(F32)
    swg[...] = (
        jnp.sum(f0 * uf0 + f1 * uf1 + g0 * ug0 + g1 * ug1, axis=0, keepdims=True)
        + rows[102:103] * res_scale
    )
    dsb[...] = jnp.sum((f0 + f1) * fb + (g0 + g1) * gb, axis=0, keepdims=True) + mb
    dskip[:, 0:TILE] = v[C : 2 * C] * skip_scale
    dskip[:, TILE:] = v[2 * C : 3 * C] * skip_scale
    dskipb[:, 0:TILE] = v[3 * C : 3 * C + 1] * skip_scale
    dskipb[:, TILE:] = v[3 * C + 1 : 3 * C + 2] * skip_scale


def neighbour(value, steps):
    count = lax.axis_size("seg")
    pairs = [(i, i + steps) for i in range(max(0, -steps), min(count, count - steps))]
    return lax.ppermute(value, "seg", pairs)


def seg_ring(value, shift):
    return lax.ppermute(value, "seg", [(i, shift(i)) for i in range(lax.axis_size("seg"))])


def whole(shape):
    return pl.BlockSpec(shape, lambda *_: (0,) * len(shape))


def params(**kw):
    return pltpu.CompilerParams(vmem_limit_bytes=VMEM_LIMIT, **kw)


VMEM = pl.BlockSpec(memory_space=pltpu.VMEM)
ANY = pl.BlockSpec(memory_space=pl.ANY)


def forward_call(base, count, xs, coef, mix, bandt, before):
    more = [] if before is None else [before]
    return pl.pallas_call(
        functools.partial(forward_kernel, base),
        grid=(count,),
        out_shape=jax.ShapeDtypeStruct((BR * TOUT * C, W), BF16),
        in_specs=[VMEM] * 4 + [ANY] * len(more),
        out_specs=pl.BlockSpec((ROWS, W), lambda i: (i + base, 0)),
        scratch_shapes=[
            pltpu.VMEM((ROWS, 3 * W), BF16),
            pltpu.VMEM((ROWS, 2 * W), BF16),
            pltpu.VMEM((3 * ROWS, W), BF16),
        ],
        input_output_aliases={4: 0} if more else {},
        compiler_params=params(),
        name="forward",
    )(xs, coef, mix, bandt, *more)


def backward_call(sample, xs, coef, mixt, wsk, wskt, bsk, band, gl, go, gr, gs, before):
    more = [] if before is None else [before]
    slab = pl.BlockSpec((ROWS, W), lambda i: (i, 0))
    own = pl.BlockSpec((ROWS, W), lambda i: (i + 4 * sample, 0))
    per_sample = pl.BlockSpec((1, SKIP, W), lambda i: (sample, 0, 0))
    return pl.pallas_call(
        functools.partial(backward_kernel, sample),
        grid=(4,),
        out_shape=(
            jax.ShapeDtypeStruct((BR, SKIP, W), BF16),
            jax.ShapeDtypeStruct((PAY, TILE), F32),
        ),
        in_specs=[VMEM] * 7 + [slab, own, slab, per_sample] + [ANY] * len(more),
        out_specs=(per_sample, whole((PAY, TILE))),
        scratch_shapes=[
            pltpu.VMEM((ROWS, 3 * W), BF16),
            pltpu.VMEM((ROWS, 2 * W), BF16),
            pltpu.VMEM((3 * ROWS, W), BF16),
            pltpu.VMEM((ROWS, W), BF16),
            pltpu.VMEM((ROWS, W), F32),
            pltpu.VMEM((8, C, TILE), F32),
            pltpu.VMEM((3 * ROWS, ROWS), F32),
            pltpu.VMEM((C + 16, SKIP), F32),
        ],
        input_output_aliases={11: 0} if more else {},
        compiler_params=params(),
        name="backward",
    )(xs, coef, mixt, wsk, wskt, bsk, band, gl, go, gr, gs, *more)


def send(speeds, cols):
    return pl.pallas_call(
        message_kernel,
        grid=(1,),
        out_shape=jax.ShapeDtypeStruct((32, 4, 3 * W), BF16),
        in_specs=[
            pl.BlockSpec((TILES, 3), lambda i: (0, 0), memory_space=pltpu.SMEM),
            whole((3, 16384)),
        ],
        out_specs=VMEM,
        scratch_shapes=[pltpu.VMEM((4, 16384 + 2 * W), F32)],
        compiler_params=params(),
        name="message",
    )(cols, speeds)


def prepare(msg, vals, w_start, b_start, w_filter, b_filter, w_gate, b_gate, w_mix, b_mix, w_skip, b_skip):
    row = lambda a: a.reshape(1, -1)
    small = [
        row(w_start), row(b_start), w_filter, row(b_filter), w_gate, row(b_gate), w_mix, row(b_mix),
        w_skip.T, row(b_skip), *vals,
    ]
    return pl.pallas_call(
        prep_kernel,
        grid=(1,),
        out_shape=(
            jax.ShapeDtypeStruct((9 * C, TILE), F32),
            jax.ShapeDtypeStruct((ROWS, 3 * ROWS), BF16),
            jax.ShapeDtypeStruct((ROWS, 3 * ROWS), BF16),
            jax.ShapeDtypeStruct((SKIP, C), BF16),
            jax.ShapeDtypeStruct((SKIP, TILE), F32),
            jax.ShapeDtypeStruct((4, 3 * PAIR, PAIR), BF16),
            jax.ShapeDtypeStruct((4, 3 * PAIR, PAIR), BF16),
            jax.ShapeDtypeStruct((BR * T_IN, 3 * W), F32),
        ),
        in_specs=[whole(a.shape) for a in small] + [VMEM],
        out_specs=(VMEM,) * 8,
        compiler_params=params(),
        name="prep",
    )(*small, msg)


def body(
    speeds, w_start, b_start, w_filter, b_filter, w_gate, b_gate, adj_cols, adj_vals,
    w_mix, b_mix, w_skip, b_skip, grad_res, grad_skip,
):
    barrier = lax.optimization_barrier
    half = TOUT * C
    grad = grad_res.reshape(BR * half, W)
    vals = (neighbour(adj_vals, 1), adj_vals, neighbour(adj_vals, -1))
    msg = lax.all_to_all(send(speeds, adj_cols), "seg", split_axis=0, concat_axis=0, tiled=True)
    first = grad[:half]
    msg, first = barrier((msg, first))
    halo0 = neighbour(first, 1), neighbour(first, -1)
    coef, mix, mixt, wsk, bsk, band, bandt, xs = prepare(
        msg, vals, w_start, b_start, w_filter, b_filter, w_gate, b_gate, w_mix, b_mix, w_skip, b_skip
    )
    xs, second = barrier((xs, grad[half:]))
    halo1 = neighbour(second, 1), neighbour(second, -1)

    common = (coef, mixt, wsk, w_skip.T, bsk, band)
    skip, pay0 = backward_call(0, xs, *common, halo0[0], grad, halo0[1], grad_skip, None)
    pay0, xs = barrier((pay0, xs))
    res = forward_call(0, 3, xs, coef, mix, bandt, None)
    res, xs = barrier((res, xs))
    skip, pay1 = backward_call(1, xs, *common, halo1[0], grad, halo1[1], grad_skip, skip)

    v = pay0 + pay1
    v = v + seg_ring(v, lambda i: i ^ 1)

    def forward(base, count, v, before):
        v, xs_now = barrier((v, xs))
        return v, forward_call(base, count, xs_now, coef, mix, bandt, before)

    v, res = forward(3, 2, v, res)
    v = v + sum(seg_ring(v, lambda i, k=k: (i // 8) * 8 + ((i // 2 + k) % 4) * 2 + i % 2) for k in (1, 2, 3))
    v, res = barrier((v, res))
    v, res = forward(5, 2, v, res)
    v = v + sum(seg_ring(v, lambda i, k=k: (i + 8 * k) % 32) for k in (1, 2, 3))
    v, res = barrier((v, res))
    v, res = forward(7, 1, v, res)
    others = [lax.ppermute(v, "rep", [(i, (i + k) % 4) for i in range(4)]) for k in (1, 2, 3)]

    row = jax.ShapeDtypeStruct((1, C), F32)
    taps = jax.ShapeDtypeStruct((2, C, C), F32)
    small = (v, *others, w_start.reshape(1, C), b_start.reshape(1, C), w_filter, w_gate)
    swg, dsb, dfil, dfb, dgat, dgb, dmix, dmixb, dskip, dskipb = pl.pallas_call(
        finish_kernel,
        grid=(1,),
        out_shape=(
            row, row, taps, row, taps, row, jax.ShapeDtypeStruct((C, 3 * C), F32), row,
            jax.ShapeDtypeStruct((C, SKIP), F32), jax.ShapeDtypeStruct((1, SKIP), F32),
        ),
        in_specs=[whole(a.shape) for a in small],
        out_specs=(whole((1, C)), whole((1, C)), whole((2, C, C)), whole((1, C)), whole((2, C, C)),
                   whole((1, C)), whole((C, 3 * C)), whole((1, C)), whole((C, SKIP)), whole((1, SKIP))),
        compiler_params=params(),
        name="finish",
    )(*small)
    vec = lambda a: a.reshape(-1)
    return (
        res.reshape(BR, TOUT, C, W), skip, vec(swg), vec(dsb), dfil, vec(dfb), dgat, vec(dgb),
        dmix, vec(dmixb), dskip.T, vec(dskipb),
    )


def solution(mesh):
    placed = (
        P(("rep", "seg"), None), P(), P(), P(), P(), P(), P(), P("seg", None),
        P("seg", None, None, None), P(), P(), P(), P(), P("rep", None, None, "seg"),
        P("rep", None, "seg"),
    )
    return jax.shard_map(
        body,
        mesh=mesh,
        in_specs=placed,
        out_specs=(P("rep", None, None, "seg"), P("rep", None, "seg")) + (P(),) * 10,
        check_vma=False,
    )
```

time: 146 us -> 102 us (0.70)
  blocking collectives: 30.2 us -> 0 us
  local copies, waits for them, and re-layouts: 16.7 us -> 4.96 us
    all_to_all x1 -> x0, blocking collectives: 30.2 us -> none  [body(): lax.all_to_all(speeds.astype(BF16), 'seg', split_axis=1, concat_axis=0, t...]
    unnamed x49 -> x30, local copies, waits for them, and re-layouts: 15.1 us -> 1.71 us
    all_to_all x0 -> x1, starting transfers between devices: none -> 10.7 us  [body(): lax.all_to_all(send(speeds, adj_cols), 'seg', split_axis=0, concat_axis=0...]
    all_to_all x0 -> x1, waiting for transfers between devices: none -> 6.53 us  [body(): lax.all_to_all(send(speeds, adj_cols), 'seg', split_axis=0, concat_axis=0...]
    ppermute x7, waiting for transfers between devices: 8.71 us -> 2.66 us  [seg_ring(): lax.ppermute(value, 'seg', [(i, shift(i)) for i in range(lax.axis_size('s...]
    ppermute x8 -> x6, starting transfers between devices: 18.9 us -> 13.4 us  [neighbour(): return lax.ppermute(value, 'seg', pairs)]
    ppermute x7, starting transfers between devices: 19.6 us -> 14.9 us  [seg_ring(): lax.ppermute(value, 'seg', [(i, shift(i)) for i in range(lax.axis_size('s...]
    slice x0 -> x1, local copies, waits for them, and re-layouts: none -> 3.26 us  [body(): xs, second = barrier((xs, grad[half:]))]
  transfers between devices with their start and end apart: 18 -> 17, of which waited for: 7 -> 7; matrix products, arithmetic and copies ran while one was open for 3% -> 3% of each run, Pallas kernels for 14% -> 30%
where the time goes in v2:
time: 102 us; the launch traced here: 101 us
  starting transfers between devices  43.5 us (43%)
  Pallas kernels  40.6 us (40%)
  waiting for transfers between devices  11.2 us (11%)
  local copies, waits for them, and re-layouts  4.96 us (5%)
    pallas_call x2, Pallas kernels, backward_call(): pl.pallas_call(functools.partial(backward_kernel, sample), grid=(4,), out...  18.4 us
    pallas_call x4, Pallas kernels, forward_call(): pl.pallas_call(functools.partial(forward_kernel, base), grid=(count,), ou...  17.8 us
    ppermute x7, starting transfers between devices, seg_ring(): lax.ppermute(value, 'seg', [(i, shift(i)) for i in range(lax.axis_size('s...  14.9 us
    ppermute x6, starting transfers between devices, neighbour(): return lax.ppermute(value, 'seg', pairs)  13.4 us
    all_to_all x1, starting transfers between devices, body(): lax.all_to_all(send(speeds, adj_cols), 'seg', split_axis=0, concat_axis=0...  10.7 us
    all_to_all x1, waiting for transfers between devices, body(): lax.all_to_all(send(speeds, adj_cols), 'seg', split_axis=0, concat_axis=0...  6.53 us
    ppermute x3, starting transfers between devices, body(): lax.ppermute(v, 'rep', [(i, (i + k) % 4) for i in range(4)])  4.51 us
    slice x1, local copies, waits for them, and re-layouts, body(): xs, second = barrier((xs, grad[half:]))  3.26 us
  transfers between devices with their start and end apart: 17, of which 7 were waited for; matrix products, arithmetic and copies ran while one was open for 3% of the time, Pallas kernels for 30%

profile of v2, /device:TPU:0, one launch (start us, length us, event | category | flops | bytes accessed | tf_op | source)
XLA Modules:
  0.0 101.3 jit_solution(8718003472927263466)
XLA Ops:
  0.6 2.0 %collective-permute-start = (bf16[4,3,128,128]{3,2,1,0:T(8,128)(2,1)}, bf16[4,3,128,128]{3,2,1,0:T(8,128)(2,1)}, u32[]{:S(2)}, u32[]{:S(2)}) collective-permute-start(bf16[4,3,128,128]{3,2,1,0:T(8,128)(2,1)} %vo.1), channel_id=1, source_target_pairs={{0,4},{4,8},{8,12},{12,16},{16,20},{20,24},{24,28},{28,32},{32,36}... | collective-permute-start | bytes 1179656 | tf_op jit(solution)/shard_map/ppermute | solution.py:308
  2.7 1.3 %collective-permute-start.1 = (bf16[4,3,128,128]{3,2,1,0:T(8,128)(2,1)}, bf16[4,3,128,128]{3,2,1,0:T(8,128)(2,1)}, u32[]{:S(2)}, u32[]{:S(2)}) collective-permute-start(bf16[4,3,128,128]{3,2,1,0:T(8,128)(2,1)} %vo.1), channel_id=1, source_target_pairs={{4,0},{8,4},{12,8},{16,12},{20,16},{24,20},{28,24},{32,28},{36,32}... | collective-permute-start | bytes 1179656 | tf_op jit(solution)/shard_map/ppermute | solution.py:308
  4.0 0.0 copy-start.3
  4.0 0.9 copy-done.3
  4.9 0.7 copy-done.8
  5.6 1.5 %message.1 = bf16[32,4,1536]{2,1,0:T(4,128)(2,1)} custom-call(s32[4,3]{1,0:T(4,128)S(1)} %copy-done.8, f32[3,16384]{1,0:T(4,128)S(1)} %copy-done.3), custom_call_target="tpu_custom_call" | custom-call | tf_op jit(solution)/shard_map/message/pallas_call | solution.py:377
  7.1 10.7 %all-to-all-start = ((bf16[32,4,1536]{2,1,0:T(4,128)(2,1)}), bf16[32,4,1536]{2,1,0:T(4,128)(2,1)S(1)}, u32[]{:S(2)}, u32[]{:S(2)}) async-start(bf16[32,4,1536]{2,1,0:T(4,128)(2,1)} %message.1), calls=%async_computation | async-start | bytes 786432 | tf_op jit(solution)/shard_map/all_to_all | solution.py:426
  17.8 0.0 copy-start.2
  17.8 0.0 copy-start.4
  17.8 0.0 copy-start.5
  17.8 0.0 copy-start.6
  17.8 0.0 copy-start.7
  17.8 0.0 copy-start.9
  17.8 0.0 copy-start.10
  17.8 0.0 copy-start.11
  17.9 0.0 copy-start.12
  17.9 0.0 copy-start.13
  17.9 0.0 copy-start.14
  17.9 0.0 copy-start
  17.9 0.0 copy-start.1
  17.9 3.3 %fusion = (bf16[1,32,32,512]{3,2,1,0:T(8,128)(2,1)}, bf16[1,32,32,512]{3,2,1,0:T(8,128)(2,1)}) fusion(bf16[2,32,32,512]{3,2,1,0:T(8,128)(2,1)} %param.28), kind=kLoop, calls=%fused_computation.2 | loop fusion | bytes 4194304 | tf_op jit(solution)/shard_map/slice | solution.py:433
  21.2 6.5 %all-to-all-done.msg = bf16[32,4,1536]{2,1,0:T(4,128)(2,1)S(1)} async-done(((bf16[32,4,1536]{2,1,0:T(4,128)(2,1)}), bf16[32,4,1536]{2,1,0:T(4,128)(2,1)S(1)}, u32[]{:S(2)}, u32[]{:S(2)}) %all-to-all-start) | async-done | bytes 393248 | tf_op jit(solution)/shard_map/all_to_all | solution.py:426
  27.7 1.3 %collective-permute-start.3 = (bf16[1024,512]{1,0:T(8,128)(2,1)}, bf16[1024,512]{1,0:T(8,128)(2,1)S(1)}, u32[]{:S(2)}, u32[]{:S(2)}) collective-permute-start(bf16[1024,512]{1,0:T(8,128)(2,1)} %bitcast.34), channel_id=1, source_target_pairs={{4,0},{8,4},{12,8},{16,12},{20,16},{24,20},{28,24},{32,28},{36,32}... | collective-permute-start | bytes 3145736 | tf_op jit(solution)/shard_map/ppermute | solution.py:308
  29.0 3.2 %collective-permute-start.2 = (bf16[1024,512]{1,0:T(8,128)(2,1)}, bf16[1024,512]{1,0:T(8,128)(2,1)S(1)}, u32[]{:S(2)}, u32[]{:S(2)}) collective-permute-start(bf16[1024,512]{1,0:T(8,128)(2,1)} %bitcast.35), channel_id=1, source_target_pairs={{0,4},{4,8},{8,12},{12,16},{16,20},{20,24},{24,28},{28,32},{32,36}... | collective-permute-start | bytes 3145736 | tf_op jit(solution)/shard_map/ppermute | solution.py:308
  32.2 0.0 collective-permute-done.vl
  32.2 0.0 collective-permute-done.1.vr
  32.2 0.0 copy-done.2
  32.3 0.0 copy-done.4
  32.3 0.0 copy-done.5
  32.3 0.0 copy-done.6
  32.4 2.2 %prep.1 = (f32[288,128]{1,0:T(8,128)S(1)}, bf16[256,768]{1,0:T(8,128)(2,1)S(1)}, bf16[256,768]{1,0:T(8,128)(2,1)S(1)}, bf16[256,32]{1,0:T(8,128)(2,1)S(1)}, f32[...) custom-call(f32[1,32]{1,0:T(1,128)S(1)} %bitcast.23, ...), custom_call_target="tpu_custom_call" | custom-call | tf_op jit(solution)/shard_map/prep/pallas_call | solution.py:398
  34.6 1.3 %collective-permute-start.5 = (bf16[1024,512]{1,0:T(8,128)(2,1)}, bf16[1024,512]{1,0:T(8,128)(2,1)S(1)}, u32[]{:S(2)}, u32[]{:S(2)}) collective-permute-start(bf16[1024,512]{1,0:T(8,128)(2,1)} %bitcast.32), channel_id=1, source_target_pairs={{4,0},{8,4},{12,8},{16,12},{20,16},{24,20},{28,24},{32,28},{36,32}... | collective-permute-start | bytes 3145736 | tf_op jit(solution)/shard_map/ppermute | solution.py:308
  35.9 4.3 %collective-permute-start.4 = (bf16[1024,512]{1,0:T(8,128)(2,1)}, bf16[1024,512]{1,0:T(8,128)(2,1)S(1)}, u32[]{:S(2)}, u32[]{:S(2)}) collective-permute-start(bf16[1024,512]{1,0:T(8,128)(2,1)} %bitcast.33), channel_id=1, source_target_pairs={{0,4},{4,8},{8,12},{12,16},{16,20},{20,24},{24,28},{28,32},{32,36}... | collective-permute-start | bytes 3145736 | tf_op jit(solution)/shard_map/ppermute | solution.py:308
  40.1 0.0 collective-permute-done.3.gr
  40.1 0.0 collective-permute-done.2.gl
  40.2 9.2 %backward.2 = (bf16[2,256,512]{2,1,0:T(8,128)(2,1)}, f32[104,128]{1,0:T(8,128)S(1)}) custom-call(f32[96,1536]{1,0:T(8,128)S(1)} %get-tuple-element.78.xs, f32[288,128]{1,0:T(8,128)S(1)} %get-tuple-element.55.coef, bf16[256,768]{1,0:T(8,128)(2,1)S(1)} %get-tuple-element.56.mixt, bf16[256,32]{1,0:T(8,128)(2,1)S(1)} %get-tuple-element.57.wsk, ...), custom_call_target="tpu_custom_call" | custom-call | tf_op jit(solution)/shard_map/backward/pallas_call | solution.py:351
  49.4 6.3 %forward.4.refs_0_ = bf16[2048,512]{1,0:T(8,128)(2,1)} custom-call(f32[96,1536]{1,0:T(8,128)S(1)} %get-tuple-element.78.xs, f32[288,128]{1,0:T(8,128)S(1)} %get-tuple-element.55.coef, bf16[256,768]{1,0:T(8,128)(2,1)S(1)} %get-tuple-element.64.mix, bf16[4,768,256]{2,1,0:T(8,128)(2,1)S(1)} %get-tuple-element.65.bandt), custom_call_target="tpu_custom_call" | custom-call | tf_op jit(solution)/shard_map/forward/pallas_call | solution.py:329
  55.7 0.0 collective-permute-done.5.gr
  55.7 0.0 collective-permute-done.4.gl
  55.7 9.2 %backward.3 = (bf16[2,256,512]{2,1,0:T(8,128)(2,1)}, f32[104,128]{1,0:T(8,128)S(1)}) custom-call(f32[96,1536]{1,0:T(8,128)S(1)} %get-tuple-element.78.xs, f32[288,128]{1,0:T(8,128)S(1)} %get-tuple-element.55.coef, bf16[256,768]{1,0:T(8,128)(2,1)S(1)} %get-tuple-element.56.mixt, ...), custom_call_target="tpu_custom_call", output_to_operand_aliasing={{0}: (11, {})} | custom-call | tf_op jit(solution)/shard_map/backward/pallas_call | solution.py:351
  64.9 5.8 %collective-permute-start.6 = (f32[104,128]{1,0:T(8,128)S(1)}, f32[104,128]{1,0:T(8,128)S(1)}, u32[]{:S(2)}, u32[]{:S(2)}) collective-permute-start(f32[104,128]{1,0:T(8,128)S(1)} %add.24), channel_id=1, source_target_pairs={{0,4},{4,0},{8,12},{12,8},{16,20},{20,16},{24,28},{28,24},{32,36},... | collective-permute-start | bytes 159752 | tf_op jit(solution)/shard_map/ppermute | solution.py:312
  70.7 0.9 collective-permute-done.6
  71.6 3.4 %collective-permute-start.9 = (f32[104,128]{1,0:T(8,128)S(1)}, f32[104,128]{1,0:T(8,128)S(1)}, u32[]{:S(2)}, u32[]{:S(2)}) collective-permute-start(f32[104,128]{1,0:T(8,128)S(1)} %add.25), channel_id=1, source_target_pairs={{0,24},{4,28},{8,0},{12,4},{16,8},{20,12},{24,16},{28,20},{32,56},... | collective-permute-start | bytes 159752 | tf_op jit(solution)/shard_map/ppermute | solution.py:312
  75.0 1.3 %collective-permute-start.8 = (f32[104,128]{1,0:T(8,128)S(1)}, f32[104,128]{1,0:T(8,128)S(1)}, u32[]{:S(2)}, u32[]{:S(2)}) collective-permute-start(f32[104,128]{1,0:T(8,128)S(1)} %add.25), channel_id=1, source_target_pairs={{0,16},{4,20},{8,24},{12,28},{16,0},{20,4},{24,8},{28,12},{32,48},... | collective-permute-start | bytes 159752 | tf_op jit(solution)/shard_map/ppermute | solution.py:312
  76.4 0.0 collective-permute-start.7
  76.4 4.5 %forward.5.refs_0_ = bf16[2048,512]{1,0:T(8,128)(2,1)} custom-call(f32[96,1536]{1,0:T(8,128)S(1)} %get-tuple-element.78.xs, f32[288,128]{1,0:T(8,128)S(1)} %get-tuple-element.55.coef, bf16[256,768]{1,0:T(8,128)(2,1)S(1)} %get-tuple-element.64.mix, bf16[4,768,256]{2,1,0:T(8,128)(2,1)S(1)} %get-tuple-element.65.bandt, ...), custom_call_target="tpu_custom_call", output_to_operand_aliasing={{}: (4, {})} | custom-call | tf_op jit(solution)/shard_map/forward/pallas_call | solution.py:329
  80.8 0.0 collective-permute-done.9
  80.8 0.2 collective-permute-done.8
  81.0 0.7 collective-permute-done.7
  81.7 1.5 %collective-permute-start.12 = (f32[104,128]{1,0:T(8,128)S(1)}, f32[104,128]{1,0:T(8,128)S(1)}, u32[]{:S(2)}, u32[]{:S(2)}) collective-permute-start(f32[104,128]{1,0:T(8,128)S(1)} %add_add_fusion.1), channel_id=1, source_target_pairs={{0,96},{4,100},{8,104},{12,108},{16,112},{20,116},{24,120},{28,124... | collective-permute-start | bytes 159752 | tf_op jit(solution)/shard_map/ppermute | solution.py:312
  83.3 2.8 %collective-permute-start.11 = (f32[104,128]{1,0:T(8,128)S(1)}, f32[104,128]{1,0:T(8,128)S(1)}, u32[]{:S(2)}, u32[]{:S(2)}) collective-permute-start(f32[104,128]{1,0:T(8,128)S(1)} %add_add_fusion.1), channel_id=1, source_target_pairs={{0,64},{4,68},{8,72},{12,76},{16,80},{20,84},{24,88},{28,92},{32,9... | collective-permute-start | bytes 159752 | tf_op jit(solution)/shard_map/ppermute | solution.py:312
  86.1 0.0 collective-permute-start.10
  86.1 4.4 %forward.6.refs_0_ = bf16[2048,512]{1,0:T(8,128)(2,1)} custom-call(f32[96,1536]{1,0:T(8,128)S(1)} %get-tuple-element.78.xs, f32[288,128]{1,0:T(8,128)S(1)} %get-tuple-element.55.coef, bf16[256,768]{1,0:T(8,128)(2,1)S(1)} %get-tuple-element.64.mix, bf16[4,768,256]{2,1,0:T(8,128)(2,1)S(1)} %get-tuple-element.65.bandt, ...), custom_call_target="tpu_custom_call", output_to_operand_aliasing={{}: (4, {})} | custom-call | tf_op jit(solution)/shard_map/forward/pallas_call | solution.py:329
  90.6 0.0 collective-permute-done.12
  90.6 0.0 collective-permute-done.11
  90.6 0.9 collective-permute-done.10
  91.5 2.8 %collective-permute-start.15 = (f32[104,128]{1,0:T(8,128)S(1)}, f32[104,128]{1,0:T(8,128)S(1)}, u32[]{:S(2)}, u32[]{:S(2)}) collective-permute-start(f32[104,128]{1,0:T(8,128)S(1)} %add_add_fusion.p0), channel_id=1, source_target_pairs={{0,3},{1,0},{2,1},{3,2},{4,7},{5,4},{6,5},{7,6},{8,11},{9,8},{10,9... | collective-permute-start | bytes 159752 | tf_op jit(solution)/shard_map/ppermute | solution.py:457
  94.3 0.8 collective-permute-start.14
  95.1 0.9 collective-permute-start.13
  96.0 2.5 %forward.7 = bf16[2048,512]{1,0:T(8,128)(2,1)} custom-call(f32[96,1536]{1,0:T(8,128)S(1)} %get-tuple-element.78.xs, f32[288,128]{1,0:T(8,128)S(1)} %get-tuple-element.55.coef, bf16[256,768]{1,0:T(8,128)(2,1)S(1)} %get-tuple-element.64.mix, bf16[4,768,256]{2,1,0:T(8,128)(2,1)S(1)} %get-tuple-element.65.bandt, ...), custom_call_target="tpu_custom_call", output_to_operand_aliasing={{}: (4, {})} | custom-call | tf_op jit(solution)/shard_map/forward/pallas_call | solution.py:329
  98.5 0.0 collective-permute-done.15.p3
  98.5 1.4 %collective-permute-done.14.p2 = f32[104,128]{1,0:T(8,128)S(1)} collective-permute-done((f32[104,128]{1,0:T(8,128)S(1)}, f32[104,128]{1,0:T(8,128)S(1)}, u32[]{:S(2)}, u32[]{:S(2)}) %collective-permute-start.14) | collective-permute-done | bytes 53280 | tf_op jit(solution)/shard_map/ppermute | solution.py:457
  99.9 0.6 collective-permute-done.13.p1
  100.5 0.8 finish.1
  (14 shorter events, 0.1 us)
Async XLA Ops:
  0.6 31.6 %collective-permute-start = (bf16[4,3,128,128]{3,2,1,0:T(8,128)(2,1)}, bf16[4,3,128,128]{3,2,1,0:T(8,128)(2,1)}, u32[]{:S(2)}, u32[]{:S(2)}) collective-permute-start(bf16[4,3,128,128]{3,2,1,0:T(8,128)(2,1)} %vo.1), channel_id=1, source_target_pairs={{0,4},{4,8},{8,12},{12,16},{16,20},{20,24},{24,28},{28,32},{32,36}... | collective-permute-start | bytes 1179656 | tf_op jit(solution)/shard_map/ppermute | solution.py:308
  2.7 29.5 %collective-permute-start.1 = (bf16[4,3,128,128]{3,2,1,0:T(8,128)(2,1)}, bf16[4,3,128,128]{3,2,1,0:T(8,128)(2,1)}, u32[]{:S(2)}, u32[]{:S(2)}) collective-permute-start(bf16[4,3,128,128]{3,2,1,0:T(8,128)(2,1)} %vo.1), channel_id=1, source_target_pairs={{4,0},{8,4},{12,8},{16,12},{20,16},{24,20},{28,24},{32,28},{36,32}... | collective-permute-start | bytes 1179656 | tf_op jit(solution)/shard_map/ppermute | solution.py:308
  4.0 1.0 copy-start.3
  4.9 0.7 copy-start.8
  7.1 20.6 %all-to-all-start = ((bf16[32,4,1536]{2,1,0:T(4,128)(2,1)}), bf16[32,4,1536]{2,1,0:T(4,128)(2,1)S(1)}, u32[]{:S(2)}, u32[]{:S(2)}) async-start(bf16[32,4,1536]{2,1,0:T(4,128)(2,1)} %message.1), calls=%async_computation | async-start | bytes 786432 | tf_op jit(solution)/shard_map/all_to_all | solution.py:426
  17.8 14.5 %copy-start.2 = (bf16[4,3,128,128]{3,2,1,0:T(8,128)(2,1)S(1)}, bf16[4,3,128,128]{3,2,1,0:T(8,128)(2,1)}, u32[]{:S(2)}) copy-start(bf16[4,3,128,128]{3,2,1,0:T(8,128)(2,1)} %vo.1) | copy-start | bytes 1179652
  17.8 14.5 %copy-start.4 = (bf16[256,32]{0,1:T(8,128)(2,1)S(1)}, bf16[256,32]{0,1:T(8,128)(2,1)}, u32[]{:S(2)}) copy-start(bf16[256,32]{0,1:T(8,128)(2,1)} %param.26) | copy-start | bytes 49156
  17.8 14.5 %copy-start.5 = (bf16[2,32,32]{2,1,0:T(8,128)(2,1)S(1)}, bf16[2,32,32]{2,1,0:T(8,128)(2,1)}, u32[]{:S(2)}) copy-start(bf16[2,32,32]{2,1,0:T(8,128)(2,1)} %wf.3) | copy-start | bytes 12292
  17.8 14.5 %copy-start.6 = (bf16[2,32,32]{2,1,0:T(8,128)(2,1)S(1)}, bf16[2,32,32]{2,1,0:T(8,128)(2,1)}, u32[]{:S(2)}) copy-start(bf16[2,32,32]{2,1,0:T(8,128)(2,1)} %wg.3) | copy-start | bytes 12292
  17.8 14.5 %copy-start.7 = (bf16[32,96]{1,0:T(8,128)(2,1)S(1)}, bf16[32,96]{1,0:T(8,128)(2,1)}, u32[]{:S(2)}) copy-start(bf16[32,96]{1,0:T(8,128)(2,1)} %wm.1) | copy-start | bytes 18436
  17.8 14.5 %copy-start.9 = (f32[32]{0:T(128)S(1)}, f32[32]{0:T(128)}, u32[]{:S(2)}) copy-start(f32[32]{0:T(128)} %param.16) | copy-start | bytes 388
  17.8 14.5 %copy-start.10 = (f32[32]{0:T(128)S(1)}, f32[32]{0:T(128)}, u32[]{:S(2)}) copy-start(f32[32]{0:T(128)} %param.17) | copy-start | bytes 388
  17.8 14.5 %copy-start.11 = (f32[256]{0:T(256)S(1)}, f32[256]{0:T(256)}, u32[]{:S(2)}) copy-start(f32[256]{0:T(256)} %param.27) | copy-start | bytes 3076
  17.9 14.5 %copy-start.12 = (f32[32]{0:T(128)S(1)}, f32[32]{0:T(128)}, u32[]{:S(2)}) copy-start(f32[32]{0:T(128)} %param.19) | copy-start | bytes 388
  17.9 14.5 %copy-start.13 = (f32[32]{0:T(128)S(1)}, f32[32]{0:T(128)}, u32[]{:S(2)}) copy-start(f32[32]{0:T(128)} %param.21) | copy-start | bytes 388
  17.9 14.5 %copy-start.14 = (f32[32]{0:T(128)S(1)}, f32[32]{0:T(128)}, u32[]{:S(2)}) copy-start(f32[32]{0:T(128)} %param.25) | copy-start | bytes 388
  17.9 22.3 %copy-start = (bf16[2,32,32,512]{3,2,1,0:T(8,128)(2,1)S(1)}, bf16[2,32,32,512]{3,2,1,0:T(8,128)(2,1)}, u32[]{:S(2)}) copy-start(bf16[2,32,32,512]{3,2,1,0:T(8,128)(2,1)} %param.28) | copy-start | bytes 6291460
  17.9 22.3 %copy-start.1 = (bf16[2,256,512]{2,1,0:T(8,128)(2,1)S(1)}, bf16[2,256,512]{2,1,0:T(8,128)(2,1)}, u32[]{:S(2)}) copy-start(bf16[2,256,512]{2,1,0:T(8,128)(2,1)} %gs.3) | copy-start | bytes 1572868
  27.7 12.4 %collective-permute-start.3 = (bf16[1024,512]{1,0:T(8,128)(2,1)}, bf16[1024,512]{1,0:T(8,128)(2,1)S(1)}, u32[]{:S(2)}, u32[]{:S(2)}) collective-permute-start(bf16[1024,512]{1,0:T(8,128)(2,1)} %bitcast.34), channel_id=1, source_target_pairs={{4,0},{8,4},{12,8},{16,12},{20,16},{24,20},{28,24},{32,28},{36,32}... | collective-permute-start | bytes 3145736 | tf_op jit(solution)/shard_map/ppermute | solution.py:308
  29.0 11.2 %collective-permute-start.2 = (bf16[1024,512]{1,0:T(8,128)(2,1)}, bf16[1024,512]{1,0:T(8,128)(2,1)S(1)}, u32[]{:S(2)}, u32[]{:S(2)}) collective-permute-start(bf16[1024,512]{1,0:T(8,128)(2,1)} %bitcast.35), channel_id=1, source_target_pairs={{0,4},{4,8},{8,12},{12,16},{16,20},{20,24},{24,28},{28,32},{32,36}... | collective-permute-start | bytes 3145736 | tf_op jit(solution)/shard_map/ppermute | solution.py:308
  34.6 21.1 %collective-permute-start.5 = (bf16[1024,512]{1,0:T(8,128)(2,1)}, bf16[1024,512]{1,0:T(8,128)(2,1)S(1)}, u32[]{:S(2)}, u32[]{:S(2)}) collective-permute-start(bf16[1024,512]{1,0:T(8,128)(2,1)} %bitcast.32), channel_id=1, source_target_pairs={{4,0},{8,4},{12,8},{16,12},{20,16},{24,20},{28,24},{32,28},{36,32}... | collective-permute-start | bytes 3145736 | tf_op jit(solution)/shard_map/ppermute | solution.py:308
  35.9 19.8 %collective-permute-start.4 = (bf16[1024,512]{1,0:T(8,128)(2,1)}, bf16[1024,512]{1,0:T(8,128)(2,1)S(1)}, u32[]{:S(2)}, u32[]{:S(2)}) collective-permute-start(bf16[1024,512]{1,0:T(8,128)(2,1)} %bitcast.33), channel_id=1, source_target_pairs={{0,4},{4,8},{8,12},{12,16},{16,20},{20,24},{24,28},{28,32},{32,36}... | collective-permute-start | bytes 3145736 | tf_op jit(solution)/shard_map/ppermute | solution.py:308
  64.9 6.7 %collective-permute-start.6 = (f32[104,128]{1,0:T(8,128)S(1)}, f32[104,128]{1,0:T(8,128)S(1)}, u32[]{:S(2)}, u32[]{:S(2)}) collective-permute-start(f32[104,128]{1,0:T(8,128)S(1)} %add.24), channel_id=1, source_target_pairs={{0,4},{4,0},{8,12},{12,8},{16,20},{20,16},{24,28},{28,24},{32,36},... | collective-permute-start | bytes 159752 | tf_op jit(solution)/shard_map/ppermute | solution.py:312
  71.6 9.2 %collective-permute-start.9 = (f32[104,128]{1,0:T(8,128)S(1)}, f32[104,128]{1,0:T(8,128)S(1)}, u32[]{:S(2)}, u32[]{:S(2)}) collective-permute-start(f32[104,128]{1,0:T(8,128)S(1)} %add.25), channel_id=1, source_target_pairs={{0,24},{4,28},{8,0},{12,4},{16,8},{20,12},{24,16},{28,20},{32,56},... | collective-permute-start | bytes 159752 | tf_op jit(solution)/shard_map/ppermute | solution.py:312
  75.0 6.0 %collective-permute-start.8 = (f32[104,128]{1,0:T(8,128)S(1)}, f32[104,128]{1,0:T(8,128)S(1)}, u32[]{:S(2)}, u32[]{:S(2)}) collective-permute-start(f32[104,128]{1,0:T(8,128)S(1)} %add.25), channel_id=1, source_target_pairs={{0,16},{4,20},{8,24},{12,28},{16,0},{20,4},{24,8},{28,12},{32,48},... | collective-permute-start | bytes 159752 | tf_op jit(solution)/shard_map/ppermute | solution.py:312
  76.4 5.3 %collective-permute-start.7 = (f32[104,128]{1,0:T(8,128)S(1)}, f32[104,128]{1,0:T(8,128)S(1)}, u32[]{:S(2)}, u32[]{:S(2)}) collective-permute-start(f32[104,128]{1,0:T(8,128)S(1)} %add.25), channel_id=1, source_target_pairs={{0,8},{4,12},{8,16},{12,20},{16,24},{20,28},{24,0},{28,4},{32,40},... | collective-permute-start | bytes 159752 | tf_op jit(solution)/shard_map/ppermute | solution.py:312
  81.7 8.8 %collective-permute-start.12 = (f32[104,128]{1,0:T(8,128)S(1)}, f32[104,128]{1,0:T(8,128)S(1)}, u32[]{:S(2)}, u32[]{:S(2)}) collective-permute-start(f32[104,128]{1,0:T(8,128)S(1)} %add_add_fusion.1), channel_id=1, source_target_pairs={{0,96},{4,100},{8,104},{12,108},{16,112},{20,116},{24,120},{28,124... | collective-permute-start | bytes 159752 | tf_op jit(solution)/shard_map/ppermute | solution.py:312
  83.3 7.3 %collective-permute-start.11 = (f32[104,128]{1,0:T(8,128)S(1)}, f32[104,128]{1,0:T(8,128)S(1)}, u32[]{:S(2)}, u32[]{:S(2)}) collective-permute-start(f32[104,128]{1,0:T(8,128)S(1)} %add_add_fusion.1), channel_id=1, source_target_pairs={{0,64},{4,68},{8,72},{12,76},{16,80},{20,84},{24,88},{28,92},{32,9... | collective-permute-start | bytes 159752 | tf_op jit(solution)/shard_map/ppermute | solution.py:312
  86.1 5.3 %collective-permute-start.10 = (f32[104,128]{1,0:T(8,128)S(1)}, f32[104,128]{1,0:T(8,128)S(1)}, u32[]{:S(2)}, u32[]{:S(2)}) collective-permute-start(f32[104,128]{1,0:T(8,128)S(1)} %add_add_fusion.1), channel_id=1, source_target_pairs={{0,32},{4,36},{8,40},{12,44},{16,48},{20,52},{24,56},{28,60},{32,6... | collective-permute-start | bytes 159752 | tf_op jit(solution)/shard_map/ppermute | solution.py:312
  91.5 7.0 %collective-permute-start.15 = (f32[104,128]{1,0:T(8,128)S(1)}, f32[104,128]{1,0:T(8,128)S(1)}, u32[]{:S(2)}, u32[]{:S(2)}) collective-permute-start(f32[104,128]{1,0:T(8,128)S(1)} %add_add_fusion.p0), channel_id=1, source_target_pairs={{0,3},{1,0},{2,1},{3,2},{4,7},{5,4},{6,5},{7,6},{8,11},{9,8},{10,9... | collective-permute-start | bytes 159752 | tf_op jit(solution)/shard_map/ppermute | solution.py:457
  94.3 5.6 %collective-permute-start.14 = (f32[104,128]{1,0:T(8,128)S(1)}, f32[104,128]{1,0:T(8,128)S(1)}, u32[]{:S(2)}, u32[]{:S(2)}) collective-permute-start(f32[104,128]{1,0:T(8,128)S(1)} %add_add_fusion.p0), channel_id=1, source_target_pairs={{0,2},{1,3},{2,0},{3,1},{4,6},{5,7},{6,4},{7,5},{8,10},{9,11},{10,... | collective-permute-start | bytes 159752 | tf_op jit(solution)/shard_map/ppermute | solution.py:457
  95.1 5.4 %collective-permute-start.13 = (f32[104,128]{1,0:T(8,128)S(1)}, f32[104,128]{1,0:T(8,128)S(1)}, u32[]{:S(2)}, u32[]{:S(2)}) collective-permute-start(f32[104,128]{1,0:T(8,128)S(1)} %add_add_fusion.p0), channel_id=1, source_target_pairs={{0,1},{1,2},{2,3},{3,0},{4,5},{5,6},{6,7},{7,4},{8,9},{9,10},{10,1... | collective-permute-start | bytes 159752 | tf_op jit(solution)/shard_map/ppermute | solution.py:457

commit v3 on v2

--- a/solution.py
+++ b/solution.py
@@ -24,6 +24,8 @@
 BF16 = jnp.bfloat16
 A0F, A1F, CF, A0G, A1G, CG, WS, BS, BM = range(9)
 PAY = 104
+RES_SCALE = 1.0 / math.sqrt(8 * TOUT * 16384)
+SKIP_SCALE = 1.0 / math.sqrt(8 * 16384)
 VMEM_LIMIT = 40 * 1024 * 1024
 
 
@@ -50,22 +52,48 @@
     return jnp.where(r == c, full, 0.0)
 
 
-def message_kernel(cols, speeds, msg, wide):
+def message_kernel(cols_hbm, speeds, grad, msg, first, second, cols, rows, wide, stage, sems):
+    half = first.shape[0]
+    loads = [
+        pltpu.make_async_copy(src, dst, sems.at[n])
+        for n, (src, dst) in enumerate(
+            (
+                (speeds, rows),
+                (cols_hbm, cols),
+                (grad.at[pl.ds(0, half)], stage.at[0]),
+                (grad.at[pl.ds(half, half)], stage.at[1]),
+            )
+        )
+    ]
+    stores = [
+        pltpu.make_async_copy(stage.at[n], dst, sems.at[4 + n])
+        for n, dst in enumerate((first, second))
+    ]
+    for copy in loads:
+        copy.start()
     wide[:, 0:W] = jnp.zeros((4, W), F32)
     wide[:, W + 16384 :] = jnp.zeros((4, W), F32)
-    wide[0:3, W : W + 16384] = speeds[...]
-    first = lax.axis_index("seg") * TILES
+    loads[0].wait()
+    loads[1].wait()
+    wide[0:3, W : W + 16384] = rows[...]
+    base = lax.axis_index("seg") * TILES
     offsets = jnp.concatenate(
         [
-            jnp.broadcast_to((cols[t, k] - (first + t)).astype(F32), (4, TILE))
+            jnp.broadcast_to((cols[t, k] - (base + t)).astype(F32), (4, TILE))
             for t in range(TILES)
             for k in range(3)
         ],
         axis=1,
     )
     row = lax.broadcasted_iota(jnp.int32, (4, 3 * W), 0)
+    loads[2].wait()
+    stores[0].start()
     for d in range(32):
         msg[d] = jnp.where(row == 3, offsets, wide[:, d * W : (d + 3) * W]).astype(BF16)
+    loads[3].wait()
+    stores[1].start()
+    stores[0].wait()
+    stores[1].wait()
 
 
 def prep_kernel(
@@ -90,9 +118,9 @@
     put(BM, column(bm[...]))
     for h in range(3):
         w = wm[:, h * C : (h + 1) * C].astype(F32)
-        mix[:, h * ROWS : (h + 1) * ROWS] = block_diag(w).astype(BF16)
+        mix[:, h * ROWS : (h + 1) * ROWS] = block_diag(w * 0.5).astype(BF16)
         mixt[:, h * ROWS : (h + 1) * ROWS] = block_diag(w.T).astype(BF16)
-    wsk[...] = wskt[...].astype(F32).T.astype(BF16)
+    wsk[...] = (wskt[...].astype(F32) * 0.5).T.astype(BF16)
     bskc[...] = jnp.broadcast_to(column(bsk[...]), (SKIP, TILE))
 
     for i in range(32):
@@ -136,117 +164,173 @@
                 store(bandt, q, m, u)
 
 
-def two_hops(ext, one, band, p_two):
+def hops(ext, one, band, put, between):
     for p in range(4):
         one[:, p * PAIR : (p + 1) * PAIR] = dot(
             ext[:, p * PAIR : (p + 3) * PAIR], band[p]
         ).astype(BF16)
+        between()
     for p in range(2):
-        p_two(p, dot(one[:, p * PAIR : (p + 3) * PAIR], band[p + 1]).astype(BF16))
+        put(p, dot(one[:, p * PAIR : (p + 3) * PAIR], band[p + 1]).astype(BF16))
+        between()
 
 
 def coefs(coef, *which):
     return [coef[i * C : (i + 1) * C, :] for i in which]
 
 
-def forward_kernel(base, xs, coef, mix, bandt, *refs):
-    res, zext, one, stack = refs[-4:]
-    i = pl.program_id(0) + base
-    at = ((i // 4) * 6 + i % 4) * TG
-    x0 = xs.at[pl.ds(pl.multiple_of(at, TG), TG)]
-    x1 = xs.at[pl.ds(pl.multiple_of(at + DIL, TG), TG)]
-
-    def step(t, carry):
-        a0f, a1f, cf, a0g, a1g, cg = coefs(coef, A0F, A1F, CF, A0G, A1G, CG)
-        lanes = pl.ds(pl.multiple_of(t * TILE, TILE), TILE)
+def spread(bodies, slots):
+    queue = list(bodies)
+    share = -(-len(queue) // slots)
+
+    def emit():
+        for _ in range(min(share, len(queue))):
+            queue.pop(0)()
+
+    return emit
+
+
+def lane_tile(t):
+    return slice(t * TILE, (t + 1) * TILE)
+
+
+def slab_rows(k):
+    return slice(k * C, (k + 1) * C)
+
+
+def gates(coef, p, q):
+    a0f, a1f, cf, a0g, a1g, cg = coefs(coef, A0F, A1F, CF, A0G, A1G, CG)
+    return jnp.tanh(a0f * p + a1f * q + cf), jnp.tanh(a0g * p + a1g * q + cg) + 1.0
+
+
+def forward_kernel(base, count, xs, coef, mix, bandt, zown, *refs):
+    res, ahead, zext, one, stack = refs[-5:]
+    i = pl.program_id(0)
+
+    def at(step):
+        row = ((step // 4) * 6 + step % 4) * TG
+        return (
+            xs.at[pl.ds(pl.multiple_of(row, TG), TG)],
+            xs.at[pl.ds(pl.multiple_of(row + DIL, TG), TG)],
+        )
+
+    halo = [t for t in range(12) if not 4 <= t < 8]
+
+    def look_ahead(x0, x1, k, n):
+        def emit():
+            lanes = lane_tile(halo[n])
+            f, u = gates(coef, x0[k : k + 1, lanes], x1[k : k + 1, lanes])
+            ahead[slab_rows(k), lane_tile(n)] = (f * u).astype(BF16)
+
+        return emit
+
+    @pl.when(i == 0)
+    def _():
+        x0, x1 = at(i + base)
         for k in range(TG):
-            p = x0[k : k + 1, lanes]
-            q = x1[k : k + 1, lanes]
-            f = jnp.tanh(a0f * p + a1f * q + cf)
-            g = 0.5 * jnp.tanh(a0g * p + a1g * q + cg) + 0.5
-            zext[k * C : (k + 1) * C, lanes] = (f * g).astype(BF16)
-        return carry
-
-    lax.fori_loop(0, 3 * TILES, step, 0)
-    stack[0:ROWS, :] = zext[:, W : 2 * W]
+            for n in range(8):
+                look_ahead(x0, x1, k, n)()
+
+    zext[:, 0:W] = ahead[:, 0:W]
+    zext[:, W : 2 * W] = zown[...]
+    zext[:, 2 * W : 3 * W] = ahead[:, W : 2 * W]
+    stack[0:ROWS, :] = zown[...]
+    n0, n1 = at(jnp.minimum(i + 1, count - 1) + base)
+    emit = spread([look_ahead(n0, n1, k, n) for k in range(TG) for n in range(8)], 6)
 
     def put(p, v):
         stack[2 * ROWS : 3 * ROWS, p * PAIR : (p + 1) * PAIR] = v
 
-    two_hops(zext, one, bandt, put)
+    hops(zext, one, bandt, put, emit)
     stack[ROWS : 2 * ROWS, :] = one[:, PAIR : PAIR + W]
     mixed = dot(mix[...], stack[...])
     ws, bs, bm = coefs(coef, WS, BS, BM)
     bb = bs + bm
+    x1 = at(i + base)[1]
     for k in range(TG):
         for t in range(TILES):
             q = x1[k : k + 1, W + t * TILE : W + (t + 1) * TILE]
-            r, lanes = slice(k * C, (k + 1) * C), slice(t * TILE, (t + 1) * TILE)
+            r, lanes = slab_rows(k), lane_tile(t)
             res[r, lanes] = (mixed[r, lanes] + (ws * q + bb)).astype(BF16)
 
 
 def backward_kernel(sample, xs, coef, mixt, wsk, wskt, bsk, band, gl, go, gr, gs, *refs):
-    skip, pay, ext, one, stack, zb, dzs, acc, dmx, dsk = refs[-10:]
+    skip, pay, zb, ext, one, stack, dzs, fs, us, acc, dmx, dsk, extra = refs[-13:]
     i = pl.program_id(0)
     last = i == 3
     at = (sample * 6 + i) * TG
     x0 = xs.at[pl.ds(pl.multiple_of(at, TG), TG)]
     x1 = xs.at[pl.ds(pl.multiple_of(at + DIL, TG), TG)]
-    res_scale = 1.0 / math.sqrt(8 * TOUT * 16384)
-    skip_scale = 1.0 / math.sqrt(8 * 16384)
 
     @pl.when(i == 0)
     def _():
         acc[...] = jnp.zeros_like(acc)
         dmx[...] = jnp.zeros_like(dmx)
-        dsk[...] = jnp.zeros_like(dsk)
+        extra[...] = jnp.zeros_like(extra)
+
+    @pl.when(last)
+    def _():
+        extra[...] = dot(wskt[...], gs[0]) * (SKIP_SCALE / RES_SCALE)
 
     ext[:, 0:W] = gl[...]
     ext[:, W : 2 * W] = go[...]
     ext[:, 2 * W : 3 * W] = gr[...]
     stack[0:ROWS, :] = go[...]
 
+    def rows_of(k, t):
+        lanes = slice(W + t * TILE, W + (t + 1) * TILE)
+        return x0[k : k + 1, lanes], x1[k : k + 1, lanes]
+
+    def gate(k, t):
+        def emit():
+            r, lanes = slab_rows(k), lane_tile(t)
+            f, u = gates(coef, *rows_of(k, t))
+            fs[r, lanes] = f
+            us[r, lanes] = u
+            zb[r, lanes] = (f * u).astype(BF16)
+
+        return emit
+
     def put(p, v):
         stack[2 * ROWS : 3 * ROWS, p * PAIR : (p + 1) * PAIR] = v
 
-    two_hops(ext, one, band, put)
+    hops(ext, one, band, put, spread([gate(k, t) for k in range(TG) for t in range(TILES)], 6))
     stack[ROWS : 2 * ROWS, :] = one[:, PAIR : PAIR + W]
-    dzs[...] = dot(mixt[...], stack[...]) * res_scale
-
-    @pl.when(last)
-    def _():
-        dzs[ROWS - C : ROWS, :] += dot(wskt[...], gs[0]) * skip_scale
-
-    a0f, a1f, cf, a0g, a1g, cg = coefs(coef, A0F, A1F, CF, A0G, A1G, CG)
+    dzs[...] = dot(mixt[...], stack[...])
+    dzs[ROWS - C : ROWS, :] += extra[...]
+
     sums = [acc[j] for j in range(8)]
-    for k in range(TG):
-        for t in range(TILES):
-            r, lanes = slice(k * C, (k + 1) * C), slice(t * TILE, (t + 1) * TILE)
-            p = x0[k : k + 1, W + t * TILE : W + (t + 1) * TILE]
-            q = x1[k : k + 1, W + t * TILE : W + (t + 1) * TILE]
-            f = jnp.tanh(a0f * p + a1f * q + cf)
-            g = 0.5 * jnp.tanh(a0g * p + a1g * q + cg) + 0.5
-            zb[r, lanes] = (f * g).astype(BF16)
-            dg = dzs[r, lanes] * g
-            df = dg * (1.0 - f * f)
-            dgt = dg * f * (1.0 - g)
+
+    def local(k, t):
+        def emit():
+            r, lanes = slab_rows(k), lane_tile(t)
+            p, q = rows_of(k, t)
+            f, u = fs[r, lanes], us[r, lanes]
+            s = dzs[r, lanes] * u
+            df = s * (1.0 - f * f)
+            dgt = (s * f) * (2.0 - u)
             e = go[r, lanes].astype(F32)
             for j, term in enumerate((df * p, df * q, df, dgt * p, dgt * q, dgt, e * q, e)):
                 sums[j] = sums[j] + term
+
+        return emit
+
+    emit = spread([local(k, t) for k in range(TG) for t in range(TILES)], 3)
+    for h in range(3):
+        part = slice(h * ROWS, (h + 1) * ROWS)
+        dmx[part, :] += dot_nt(stack[part, :], zb[...])
+        emit()
     for j in range(8):
         acc[j] = sums[j]
-    dmx[...] += dot_nt(stack[...], zb[...])
 
     @pl.when(last)
     def _():
         z31 = zb[ROWS - C : ROWS, :]
-        ones = jnp.ones((16, W), BF16)
-        dsk[...] += dot_nt(jnp.concatenate([z31, ones], axis=0), gs[0])
+        twos = jnp.full((16, W), 2.0, BF16)
+        dsk[...] = dot_nt(jnp.concatenate([z31, twos], axis=0), gs[0])
         bias = jnp.concatenate([bsk[...]] * TILES, axis=1)
         skip[0] = (dot(wsk[...], z31) + bias).astype(BF16)
 
-    @pl.when(last)
-    def _():
         r = lax.broadcasted_iota(jnp.int32, (ROWS, ROWS), 0) // C
         c = lax.broadcasted_iota(jnp.int32, (ROWS, ROWS), 1) // C
         lane = lax.broadcasted_iota(jnp.int32, (C, TILE), 1)
@@ -260,46 +344,48 @@
             v = v + pltpu.roll(v, 64, 1)
             v = v + pltpu.roll(v, 32, 1)
             packed = jnp.where(lane // C == h, v, packed)
+        scales = (0.5,) * 3 + (0.25,) * 3 + (1.0,) * 2
+        packed = packed * (0.5 * RES_SCALE)
         for j in range(8):
-            s = jnp.sum(acc[j], axis=1, keepdims=True)
+            s = jnp.sum(acc[j], axis=1, keepdims=True) * (scales[j] * RES_SCALE)
             packed = jnp.where(lane == 96 + j, s, packed)
         pay[0:C, :] = packed
-        pay[C : 2 * C, :] = dsk[0:C, 0:TILE]
-        pay[2 * C : 3 * C, :] = dsk[0:C, TILE:]
+        pay[C : 2 * C, :] = dsk[0:C, 0:TILE] * (0.5 * SKIP_SCALE)
+        pay[2 * C : 3 * C, :] = dsk[0:C, TILE:] * (0.5 * SKIP_SCALE)
         sub = lax.broadcasted_iota(jnp.int32, (8, TILE), 0)
-        pay[3 * C : PAY, :] = jnp.where(sub == 0, dsk[C : C + 8, 0:TILE], dsk[C : C + 8, TILE:])
+        pay[3 * C : PAY, :] = jnp.where(
+            sub == 0, dsk[C : C + 8, 0:TILE], dsk[C : C + 8, TILE:]
+        ) * (0.5 * SKIP_SCALE)
 
 
 def finish_kernel(
     p0, p1, p2, p3, ws, bs, wf, wg,
     swg, dsb, dfil, dfb, dgat, dgb, dmix, dmixb, dskip, dskipb,
 ):
-    res_scale = 1.0 / math.sqrt(8 * TOUT * 16384)
-    skip_scale = 1.0 / math.sqrt(8 * 16384)
     v = (p0[...] + p1[...]) + (p2[...] + p3[...])
     wrow, brow = ws[...], bs[...]
     head = v[0:C]
     rows = head.T
     uf0, uf1, fb, ug0, ug1, gb = (head[:, 96 + j : 97 + j] for j in range(6))
-    dmix[...] = head[:, 0:96] * res_scale
+    dmix[...] = head[:, 0:96]
     dfil[0] = uf0 * wrow + fb * brow
     dfil[1] = uf1 * wrow + fb * brow
     dgat[0] = ug0 * wrow + gb * brow
     dgat[1] = ug1 * wrow + gb * brow
     dfb[...] = rows[98:99]
     dgb[...] = rows[101:102]
-    mb = rows[103:104] * res_scale
+    mb = rows[103:104]
     dmixb[...] = mb
     f0, f1, g0, g1 = wf[0].astype(F32), wf[1].astype(F32), wg[0].astype(F32), wg[1].astype(F32)
     swg[...] = (
         jnp.sum(f0 * uf0 + f1 * uf1 + g0 * ug0 + g1 * ug1, axis=0, keepdims=True)
-        + rows[102:103] * res_scale
+        + rows[102:103]
     )
     dsb[...] = jnp.sum((f0 + f1) * fb + (g0 + g1) * gb, axis=0, keepdims=True) + mb
-    dskip[:, 0:TILE] = v[C : 2 * C] * skip_scale
-    dskip[:, TILE:] = v[2 * C : 3 * C] * skip_scale
-    dskipb[:, 0:TILE] = v[3 * C : 3 * C + 1] * skip_scale
-    dskipb[:, TILE:] = v[3 * C + 1 : 3 * C + 2] * skip_scale
+    dskip[:, 0:TILE] = v[C : 2 * C]
+    dskip[:, TILE:] = v[2 * C : 3 * C]
+    dskipb[:, 0:TILE] = v[3 * C : 3 * C + 1]
+    dskipb[:, TILE:] = v[3 * C + 1 : 3 * C + 2]
 
 
 def neighbour(value, steps):
@@ -322,25 +408,29 @@
 
 VMEM = pl.BlockSpec(memory_space=pltpu.VMEM)
 ANY = pl.BlockSpec(memory_space=pl.ANY)
-
-
-def forward_call(base, count, xs, coef, mix, bandt, before):
+HBM = pl.BlockSpec(memory_space=pltpu.HBM)
+
+
+def forward_call(base, count, xs, coef, mix, bandt, zown, before):
     more = [] if before is None else [before]
     return pl.pallas_call(
-        functools.partial(forward_kernel, base),
+        functools.partial(forward_kernel, base, count),
         grid=(count,),
         out_shape=jax.ShapeDtypeStruct((BR * TOUT * C, W), BF16),
-        in_specs=[VMEM] * 4 + [ANY] * len(more),
+        in_specs=[VMEM] * 4
+        + [pl.BlockSpec((ROWS, W), lambda i: (i + base % 4, 0))]
+        + [ANY] * len(more),
         out_specs=pl.BlockSpec((ROWS, W), lambda i: (i + base, 0)),
         scratch_shapes=[
+            pltpu.VMEM((ROWS, 2 * W), BF16),
             pltpu.VMEM((ROWS, 3 * W), BF16),
             pltpu.VMEM((ROWS, 2 * W), BF16),
             pltpu.VMEM((3 * ROWS, W), BF16),
         ],
-        input_output_aliases={4: 0} if more else {},
+        input_output_aliases={5: 0} if more else {},
         compiler_params=params(),
         name="forward",
-    )(xs, coef, mix, bandt, *more)
+    )(xs, coef, mix, bandt, zown, *more)
 
 
 def backward_call(sample, xs, coef, mixt, wsk, wskt, bsk, band, gl, go, gr, gs, before):
@@ -354,18 +444,21 @@
         out_shape=(
             jax.ShapeDtypeStruct((BR, SKIP, W), BF16),
             jax.ShapeDtypeStruct((PAY, TILE), F32),
+            jax.ShapeDtypeStruct((TOUT * C, W), BF16),
         ),
         in_specs=[VMEM] * 7 + [slab, own, slab, per_sample] + [ANY] * len(more),
-        out_specs=(per_sample, whole((PAY, TILE))),
+        out_specs=(per_sample, whole((PAY, TILE)), slab),
         scratch_shapes=[
             pltpu.VMEM((ROWS, 3 * W), BF16),
             pltpu.VMEM((ROWS, 2 * W), BF16),
             pltpu.VMEM((3 * ROWS, W), BF16),
-            pltpu.VMEM((ROWS, W), BF16),
+            pltpu.VMEM((ROWS, W), F32),
+            pltpu.VMEM((ROWS, W), F32),
             pltpu.VMEM((ROWS, W), F32),
             pltpu.VMEM((8, C, TILE), F32),
             pltpu.VMEM((3 * ROWS, ROWS), F32),
             pltpu.VMEM((C + 16, SKIP), F32),
+            pltpu.VMEM((C, W), F32),
         ],
         input_output_aliases={11: 0} if more else {},
         compiler_params=params(),
@@ -373,20 +466,23 @@
     )(xs, coef, mixt, wsk, wskt, bsk, band, gl, go, gr, gs, *more)
 
 
-def send(speeds, cols):
+def send(speeds, cols, grad):
+    half = pltpu.HBM((grad.shape[0] // 2, W), BF16)
     return pl.pallas_call(
         message_kernel,
-        grid=(1,),
-        out_shape=jax.ShapeDtypeStruct((32, 4, 3 * W), BF16),
-        in_specs=[
-            pl.BlockSpec((TILES, 3), lambda i: (0, 0), memory_space=pltpu.SMEM),
-            whole((3, 16384)),
+        out_shape=(jax.ShapeDtypeStruct((32, 4, 3 * W), BF16), half, half),
+        in_specs=[HBM] * 3,
+        out_specs=(VMEM, HBM, HBM),
+        scratch_shapes=[
+            pltpu.SMEM((TILES, 3), jnp.int32),
+            pltpu.VMEM((3, 16384), F32),
+            pltpu.VMEM((4, 16384 + 2 * W), F32),
+            pltpu.VMEM((2, grad.shape[0] // 2, W), BF16),
+            pltpu.SemaphoreType.DMA((6,)),
         ],
-        out_specs=VMEM,
-        scratch_shapes=[pltpu.VMEM((4, 16384 + 2 * W), F32)],
         compiler_params=params(),
         name="message",
-    )(cols, speeds)
+    )(*(pltpu.with_memory_space_constraint(a, pltpu.HBM) for a in (cols, speeds, grad)))
 
 
 def prepare(msg, vals, w_start, b_start, w_filter, b_filter, w_gate, b_gate, w_mix, b_mix, w_skip, b_skip):
@@ -422,35 +518,35 @@
     barrier = lax.optimization_barrier
     half = TOUT * C
     grad = grad_res.reshape(BR * half, W)
-    vals = (neighbour(adj_vals, 1), adj_vals, neighbour(adj_vals, -1))
-    msg = lax.all_to_all(send(speeds, adj_cols), "seg", split_axis=0, concat_axis=0, tiled=True)
-    first = grad[:half]
-    msg, first = barrier((msg, first))
+    msg, first, second = send(speeds, adj_cols, grad)
     halo0 = neighbour(first, 1), neighbour(first, -1)
+    msg, vals = barrier((msg, adj_vals))
+    msg = lax.all_to_all(msg, "seg", split_axis=0, concat_axis=0, tiled=True)
+    vals = (neighbour(vals, 1), adj_vals, neighbour(vals, -1))
     coef, mix, mixt, wsk, bsk, band, bandt, xs = prepare(
         msg, vals, w_start, b_start, w_filter, b_filter, w_gate, b_gate, w_mix, b_mix, w_skip, b_skip
     )
-    xs, second = barrier((xs, grad[half:]))
+    xs, second = barrier((xs, second))
     halo1 = neighbour(second, 1), neighbour(second, -1)
 
     common = (coef, mixt, wsk, w_skip.T, bsk, band)
-    skip, pay0 = backward_call(0, xs, *common, halo0[0], grad, halo0[1], grad_skip, None)
+    skip, pay0, z0 = backward_call(0, xs, *common, halo0[0], grad, halo0[1], grad_skip, None)
     pay0, xs = barrier((pay0, xs))
-    res = forward_call(0, 3, xs, coef, mix, bandt, None)
+    res = forward_call(0, 4, xs, coef, mix, bandt, z0, None)
     res, xs = barrier((res, xs))
-    skip, pay1 = backward_call(1, xs, *common, halo1[0], grad, halo1[1], grad_skip, skip)
+    skip, pay1, z1 = backward_call(1, xs, *common, halo1[0], grad, halo1[1], grad_skip, skip)
 
     v = pay0 + pay1
     v = v + seg_ring(v, lambda i: i ^ 1)
 
     def forward(base, count, v, before):
-        v, xs_now = barrier((v, xs))
-        return v, forward_call(base, count, xs_now, coef, mix, bandt, before)
-
-    v, res = forward(3, 2, v, res)
+        v, z_now = barrier((v, z1))
+        return v, forward_call(base, count, xs, coef, mix, bandt, z_now, before)
+
+    v, res = forward(4, 2, v, res)
     v = v + sum(seg_ring(v, lambda i, k=k: (i // 8) * 8 + ((i // 2 + k) % 4) * 2 + i % 2) for k in (1, 2, 3))
     v, res = barrier((v, res))
-    v, res = forward(5, 2, v, res)
+    v, res = forward(6, 1, v, res)
     v = v + sum(seg_ring(v, lambda i, k=k: (i + 8 * k) % 32) for k in (1, 2, 3))
     v, res = barrier((v, res))
     v, res = forward(7, 1, v, res)

time: 102 us -> 92.3 us (0.905)
  local copies, waits for them, and re-layouts: 4.96 us -> 0.05 us
  Pallas kernels: 40.6 us -> 35.7 us
    slice x1 -> x0, local copies, waits for them, and re-layouts: 3.26 us -> none  [body(): xs, second = barrier((xs, grad[half:]))]
    pallas_call x2, Pallas kernels: 18.4 us -> 15.3 us  [backward_call(): pl.pallas_call(functools.partial(backward_kernel, sample), grid=(4,), out...]
    ppermute x7, waiting for transfers between devices: 2.66 us -> 5.09 us  [seg_ring(): lax.ppermute(value, 'seg', [(i, shift(i)) for i in range(lax.axis_size('s...]
    all_to_all x1, waiting for transfers between devices: 6.53 us -> 4.64 us  [body(): msg = lax.all_to_all(msg, 'seg', split_axis=0, concat_axis=0, tiled=True)]
    ppermute x7, starting transfers between devices: 14.9 us -> 13.1 us  [seg_ring(): lax.ppermute(value, 'seg', [(i, shift(i)) for i in range(lax.axis_size('s...]
    pallas_call x5, Pallas kernels: 19.2 us -> 17.4 us  [the longest x4 13.8 us: forward_call(): pl.pallas_call(functools.partial(forward_kernel, base, count), grid=(coun...]
    unnamed x30 -> x26, local copies, waits for them, and re-layouts: 1.71 us -> 0.05 us
    ppermute x6, starting transfers between devices: 13.4 us -> 14.9 us  [neighbour(): return lax.ppermute(value, 'seg', pairs)]
  transfers between devices with their start and end apart: 17 -> 17, of which waited for: 7 -> 8; matrix products, arithmetic and copies ran while one was open for 3% -> 0% of each run, Pallas kernels for 30% -> 26%
where the time goes in v3:
time: 92.3 us; the launch traced here: 91.9 us
  starting transfers between devices  43 us (47%)
  Pallas kernels  35.7 us (39%)
  waiting for transfers between devices  12.2 us (13%)
  between operations  0.94 us (1%)
    pallas_call x2, Pallas kernels, backward_call(): pl.pallas_call(functools.partial(backward_kernel, sample), grid=(4,), out...  15.3 us
    ppermute x6, starting transfers between devices, neighbour(): return lax.ppermute(value, 'seg', pairs)  14.9 us
    pallas_call x4, Pallas kernels, forward_call(): pl.pallas_call(functools.partial(forward_kernel, base, count), grid=(coun...  13.8 us
    ppermute x7, starting transfers between devices, seg_ring(): lax.ppermute(value, 'seg', [(i, shift(i)) for i in range(lax.axis_size('s...  13.1 us
    all_to_all x1, starting transfers between devices, body(): msg = lax.all_to_all(msg, 'seg', split_axis=0, concat_axis=0, tiled=True)  10.5 us
    ppermute x7, waiting for transfers between devices, seg_ring(): lax.ppermute(value, 'seg', [(i, shift(i)) for i in range(lax.axis_size('s...  5.09 us
    all_to_all x1, waiting for transfers between devices, body(): msg = lax.all_to_all(msg, 'seg', split_axis=0, concat_axis=0, tiled=True)  4.64 us
    ppermute x3, starting transfers between devices, body(): lax.ppermute(v, 'rep', [(i, (i + k) % 4) for i in range(4)])  4.51 us
  transfers between devices with their start and end apart: 17, of which 8 were waited for; matrix products, arithmetic and copies ran while one was open for 0% of the time, Pallas kernels for 26%

profile of v3, /device:TPU:0, one launch (start us, length us, event | category | flops | bytes accessed | tf_op | source)
XLA Modules:
  0.0 91.9 jit_solution(5964694719691561493)
XLA Ops:
  0.7 0.0 copy-start.2
  0.7 0.0 copy-start.5
  0.7 0.0 copy-start.4
  0.7 0.0 copy-start.9
  0.7 0.0 copy-start.3
  0.7 0.0 copy-start.12
  0.7 0.0 copy-start.6
  0.7 0.0 copy-start.11
  0.7 0.0 copy-start.10
  0.7 0.0 copy-start.8
  0.8 0.0 copy-start.7
  0.8 0.0 copy-start
  0.8 0.0 copy-start.1
  0.8 3.6 %message.1 = (bf16[32,4,1536]{2,1,0:T(4,128)(2,1)}, bf16[1024,512]{1,0:T(8,128)(2,1)}, bf16[1024,512]{1,0:T(8,128)(2,1)}) custom-call(s32[4,3]{1,0:T(4,128)} %cols_hbm.1, f32[3,16384]{1,0:T(4,128)} %speeds.1, bf16[2048,512]{1,0:T(8,128)(2,1)} %bitcast.16), custom_call_target="tpu_custom_call" | custom-call | tf_op jit(solution)/shard_map/message/pallas_call | solution.py:471
  4.4 0.0 copy-done.2
  4.4 1.3 %collective-permute-start.1 = (bf16[4,3,128,128]{3,2,1,0:T(8,128)(2,1)S(1)}, bf16[4,3,128,128]{3,2,1,0:T(8,128)(2,1)}, u32[]{:S(2)}, u32[]{:S(2)}) collective-permute-start(bf16[4,3,128,128]{3,2,1,0:T(8,128)(2,1)S(1)} %copy-done.2), channel_id=1, source_target_pairs={{4,0},{8,4},{12,8},{16,12},{20,16},{24,20},{28,24},{32,28},{36,32}... | collective-permute-start | bytes 1179656 | tf_op jit(solution)/shard_map/ppermute | solution.py:394
  5.7 3.8 %collective-permute-start = (bf16[4,3,128,128]{3,2,1,0:T(8,128)(2,1)S(1)}, bf16[4,3,128,128]{3,2,1,0:T(8,128)(2,1)}, u32[]{:S(2)}, u32[]{:S(2)}) collective-permute-start(bf16[4,3,128,128]{3,2,1,0:T(8,128)(2,1)S(1)} %copy-done.2), channel_id=1, source_target_pairs={{0,4},{4,8},{8,12},{12,16},{16,20},{20,24},{24,28},{28,32},{32,36}... | collective-permute-start | bytes 1179656 | tf_op jit(solution)/shard_map/ppermute | solution.py:394
  9.5 10.5 %all-to-all-start = ((bf16[32,4,1536]{2,1,0:T(4,128)(2,1)}), bf16[32,4,1536]{2,1,0:T(4,128)(2,1)S(1)}, u32[]{:S(2)}, u32[]{:S(2)}) async-start(bf16[32,4,1536]{2,1,0:T(4,128)(2,1)} %get-tuple-element.59), calls=%async_computation | async-start | bytes 786432 | tf_op jit(solution)/shard_map/all_to_all | solution.py:524
  20.0 1.3 %collective-permute-start.3 = (bf16[1024,512]{1,0:T(8,128)(2,1)}, bf16[1024,512]{1,0:T(8,128)(2,1)}, u32[]{:S(2)}, u32[]{:S(2)}) collective-permute-start(bf16[1024,512]{1,0:T(8,128)(2,1)} %get-tuple-element.68), channel_id=1, source_target_pairs={{4,0},{8,4},{12,8},{16,12},{20,16},{24,20},{28,24},{32,28},{36,32}... | collective-permute-start | bytes 3145736 | tf_op jit(solution)/shard_map/ppermute | solution.py:394
  21.3 4.0 %collective-permute-start.2 = (bf16[1024,512]{1,0:T(8,128)(2,1)}, bf16[1024,512]{1,0:T(8,128)(2,1)}, u32[]{:S(2)}, u32[]{:S(2)}) collective-permute-start(bf16[1024,512]{1,0:T(8,128)(2,1)} %get-tuple-element.68), channel_id=1, source_target_pairs={{0,4},{4,8},{8,12},{12,16},{16,20},{20,24},{24,28},{28,32},{32,36}... | collective-permute-start | bytes 3145736 | tf_op jit(solution)/shard_map/ppermute | solution.py:394
  25.3 4.6 %all-to-all-done.msg = bf16[32,4,1536]{2,1,0:T(4,128)(2,1)S(1)} async-done(((bf16[32,4,1536]{2,1,0:T(4,128)(2,1)}), bf16[32,4,1536]{2,1,0:T(4,128)(2,1)S(1)}, u32[]{:S(2)}, u32[]{:S(2)}) %all-to-all-start) | async-done | bytes 393248 | tf_op jit(solution)/shard_map/all_to_all | solution.py:524
  29.9 0.0 collective-permute-done.1.vr
  29.9 0.0 collective-permute-done.vl
  29.9 0.0 copy-done.5
  29.9 0.0 copy-done.4
  29.9 0.0 copy-done.9
  30.0 0.0 copy-done.3
  30.0 0.0 copy-done.12
  30.0 0.0 copy-done.6
  30.0 0.0 copy-done.11
  30.0 2.2 %prep.1 = (f32[288,128]{1,0:T(8,128)S(1)}, bf16[256,768]{1,0:T(8,128)(2,1)S(1)}, bf16[256,768]{1,0:T(8,128)(2,1)S(1)}, bf16[256,32]{1,0:T(8,128)(2,1)S(1)}, f32[...) custom-call(f32[1,32]{1,0:T(1,128)S(1)} %bitcast.22, ...), custom_call_target="tpu_custom_call" | custom-call | tf_op jit(solution)/shard_map/prep/pallas_call | solution.py:494
  32.2 1.3 %collective-permute-start.5 = (bf16[1024,512]{1,0:T(8,128)(2,1)}, bf16[1024,512]{1,0:T(8,128)(2,1)S(1)}, u32[]{:S(2)}, u32[]{:S(2)}) collective-permute-start(bf16[1024,512]{1,0:T(8,128)(2,1)} %get-tuple-element.76), channel_id=1, source_target_pairs={{4,0},{8,4},{12,8},{16,12},{20,16},{24,20},{28,24},{32,28},{36,32}... | collective-permute-start | bytes 3145736 | tf_op jit(solution)/shard_map/ppermute | solution.py:394
  33.5 3.3 %collective-permute-start.4 = (bf16[1024,512]{1,0:T(8,128)(2,1)}, bf16[1024,512]{1,0:T(8,128)(2,1)S(1)}, u32[]{:S(2)}, u32[]{:S(2)}) collective-permute-start(bf16[1024,512]{1,0:T(8,128)(2,1)} %get-tuple-element.76), channel_id=1, source_target_pairs={{0,4},{4,8},{8,12},{12,16},{16,20},{20,24},{24,28},{28,32},{32,36}... | collective-permute-start | bytes 3145736 | tf_op jit(solution)/shard_map/ppermute | solution.py:394
  36.8 0.0 collective-permute-done.3.gr
  36.8 0.0 collective-permute-done.2.gl
  36.8 8.2 %backward.2 = (bf16[2,256,512]{2,1,0:T(8,128)(2,1)}, f32[104,128]{1,0:T(8,128)S(1)}, bf16[1024,512]{1,0:T(8,128)(2,1)S(1)}) custom-call(f32[96,1536]{1,0:T(8,128)S(1)} %get-tuple-element.74.xs, f32[288,128]{1,0:T(8,128)S(1)} %get-tuple-element.63.coef, bf16[256,768]{1,0:T(8,128)(2,1)S(1)} %get-tuple-element.64.mixt, ...), custom_call_target="tpu_custom_call" | custom-call | tf_op jit(solution)/shard_map/backward/pallas_call | solution.py:441
  45.0 6.1 %forward.4.refs_0_ = bf16[2048,512]{1,0:T(8,128)(2,1)} custom-call(f32[96,1536]{1,0:T(8,128)S(1)} %get-tuple-element.74.xs, f32[288,128]{1,0:T(8,128)S(1)} %get-tuple-element.63.coef, bf16[256,768]{1,0:T(8,128)(2,1)S(1)} %get-tuple-element.71.mix, bf16[4,768,256]{2,1,0:T(8,128)(2,1)S(1)} %get-tuple-element.72.bandt, bf16[1024,512]{1,0:T(8,128)(2,1)S(1)} %get-tuple-element.73.zown), custom_call_target="tpu_custom_call" | custom-call | tf_op jit(solution)/shard_map/forward/pallas_call | solution.py:416
  51.1 0.0 collective-permute-done.5.gr
  51.1 0.0 collective-permute-done.4.gl
  51.1 7.1 %backward.3 = (bf16[2,256,512]{2,1,0:T(8,128)(2,1)}, f32[104,128]{1,0:T(8,128)S(1)}, bf16[1024,512]{1,0:T(8,128)(2,1)S(1)}) custom-call(f32[96,1536]{1,0:T(8,128)S(1)} %get-tuple-element.74.xs, f32[288,128]{1,0:T(8,128)S(1)} %get-tuple-element.63.coef, bf16[256,768]{1,0:T(8,128)(2,1)S(1)} %get-tuple-element.64.mixt, ...), custom_call_target="tpu_custom_call", output_to_operand_aliasing={{0}: (11, {})} | custom-call | tf_op jit(solution)/shard_map/backward/pallas_call | solution.py:441
  58.2 2.3 %collective-permute-start.6 = (f32[104,128]{1,0:T(8,128)S(1)}, f32[104,128]{1,0:T(8,128)S(1)}, u32[]{:S(2)}, u32[]{:S(2)}) collective-permute-start(f32[104,128]{1,0:T(8,128)S(1)} %add.24), channel_id=1, source_target_pairs={{0,4},{4,0},{8,12},{12,8},{16,20},{20,16},{24,28},{28,24},{32,36},... | collective-permute-start | bytes 159752 | tf_op jit(solution)/shard_map/ppermute | solution.py:398
  60.6 0.9 collective-permute-done.6
  61.5 3.8 %collective-permute-start.9 = (f32[104,128]{1,0:T(8,128)S(1)}, f32[104,128]{1,0:T(8,128)S(1)}, u32[]{:S(2)}, u32[]{:S(2)}) collective-permute-start(f32[104,128]{1,0:T(8,128)S(1)} %add.25), channel_id=1, source_target_pairs={{0,24},{4,28},{8,0},{12,4},{16,8},{20,12},{24,16},{28,20},{32,56},... | collective-permute-start | bytes 159752 | tf_op jit(solution)/shard_map/ppermute | solution.py:398
  65.3 0.1 collective-permute-start.8
  65.4 1.0 %collective-permute-start.7 = (f32[104,128]{1,0:T(8,128)S(1)}, f32[104,128]{1,0:T(8,128)S(1)}, u32[]{:S(2)}, u32[]{:S(2)}) collective-permute-start(f32[104,128]{1,0:T(8,128)S(1)} %add.25), channel_id=1, source_target_pairs={{0,8},{4,12},{8,16},{12,20},{16,24},{20,28},{24,0},{28,4},{32,40},... | collective-permute-start | bytes 159752 | tf_op jit(solution)/shard_map/ppermute | solution.py:398
  66.4 3.6 %forward.5.refs_0_ = bf16[2048,512]{1,0:T(8,128)(2,1)} custom-call(f32[96,1536]{1,0:T(8,128)S(1)} %get-tuple-element.74.xs, f32[288,128]{1,0:T(8,128)S(1)} %get-tuple-element.63.coef, bf16[256,768]{1,0:T(8,128)(2,1)S(1)} %get-tuple-element.71.mix, bf16[4,768,256]{2,1,0:T(8,128)(2,1)S(1)} %get-tuple-element.72.bandt, ...), custom_call_target="tpu_custom_call", output_to_operand_aliasing={{}: (5, {})} | custom-call | tf_op jit(solution)/shard_map/forward/pallas_call | solution.py:416
  70.1 0.0 collective-permute-done.9
  70.1 1.2 %collective-permute-done.8 = f32[104,128]{1,0:T(8,128)S(1)} collective-permute-done((f32[104,128]{1,0:T(8,128)S(1)}, f32[104,128]{1,0:T(8,128)S(1)}, u32[]{:S(2)}, u32[]{:S(2)}) %collective-permute-start.8) | collective-permute-done | bytes 53280 | tf_op jit(solution)/shard_map/ppermute | solution.py:398
  71.2 0.3 collective-permute-done.7
  71.5 4.4 %collective-permute-start.12 = (f32[104,128]{1,0:T(8,128)S(1)}, f32[104,128]{1,0:T(8,128)S(1)}, u32[]{:S(2)}, u32[]{:S(2)}) collective-permute-start(f32[104,128]{1,0:T(8,128)S(1)} %add_add_fusion.1), channel_id=1, source_target_pairs={{0,96},{4,100},{8,104},{12,108},{16,112},{20,116},{24,120},{28,124... | collective-permute-start | bytes 159752 | tf_op jit(solution)/shard_map/ppermute | solution.py:398
  75.9 0.5 collective-permute-start.11
  76.4 0.9 collective-permute-start.10
  77.3 2.0 %forward.6.refs_0_ = bf16[2048,512]{1,0:T(8,128)(2,1)} custom-call(f32[96,1536]{1,0:T(8,128)S(1)} %get-tuple-element.74.xs, f32[288,128]{1,0:T(8,128)S(1)} %get-tuple-element.63.coef, bf16[256,768]{1,0:T(8,128)(2,1)S(1)} %get-tuple-element.71.mix, bf16[4,768,256]{2,1,0:T(8,128)(2,1)S(1)} %get-tuple-element.72.bandt, ...), custom_call_target="tpu_custom_call", output_to_operand_aliasing={{}: (5, {})} | custom-call | tf_op jit(solution)/shard_map/forward/pallas_call | solution.py:416
  79.3 0.0 collective-permute-done.12
  79.3 2.2 %collective-permute-done.11 = f32[104,128]{1,0:T(8,128)S(1)} collective-permute-done((f32[104,128]{1,0:T(8,128)S(1)}, f32[104,128]{1,0:T(8,128)S(1)}, u32[]{:S(2)}, u32[]{:S(2)}) %collective-permute-start.11) | collective-permute-done | bytes 53280 | tf_op jit(solution)/shard_map/ppermute | solution.py:398
  81.6 0.5 collective-permute-done.10
  82.1 2.8 %collective-permute-start.15 = (f32[104,128]{1,0:T(8,128)S(1)}, f32[104,128]{1,0:T(8,128)S(1)}, u32[]{:S(2)}, u32[]{:S(2)}) collective-permute-start(f32[104,128]{1,0:T(8,128)S(1)} %add_add_fusion.p0), channel_id=1, source_target_pairs={{0,3},{1,0},{2,1},{3,2},{4,7},{5,4},{6,5},{7,6},{8,11},{9,8},{10,9... | collective-permute-start | bytes 159752 | tf_op jit(solution)/shard_map/ppermute | solution.py:553
  84.9 0.8 collective-permute-start.14
  85.7 0.9 collective-permute-start.13
  86.6 2.0 %forward.7 = bf16[2048,512]{1,0:T(8,128)(2,1)} custom-call(f32[96,1536]{1,0:T(8,128)S(1)} %get-tuple-element.74.xs, f32[288,128]{1,0:T(8,128)S(1)} %get-tuple-element.63.coef, bf16[256,768]{1,0:T(8,128)(2,1)S(1)} %get-tuple-element.71.mix, bf16[4,768,256]{2,1,0:T(8,128)(2,1)S(1)} %get-tuple-element.72.bandt, ...), custom_call_target="tpu_custom_call", output_to_operand_aliasing={{}: (5, {})} | custom-call | tf_op jit(solution)/shard_map/forward/pallas_call | solution.py:416
  88.7 0.0 collective-permute-done.15.p3
  88.7 1.9 %collective-permute-done.14.p2 = f32[104,128]{1,0:T(8,128)S(1)} collective-permute-done((f32[104,128]{1,0:T(8,128)S(1)}, f32[104,128]{1,0:T(8,128)S(1)}, u32[]{:S(2)}, u32[]{:S(2)}) %collective-permute-start.14) | collective-permute-done | bytes 53280 | tf_op jit(solution)/shard_map/ppermute | solution.py:553
  90.6 0.6 collective-permute-done.13.p1
  91.2 0.8 finish.1
  (9 shorter events, 0.1 us)
Async XLA Ops:
  0.7 3.8 %copy-start.2 = (bf16[4,3,128,128]{3,2,1,0:T(8,128)(2,1)S(1)}, bf16[4,3,128,128]{3,2,1,0:T(8,128)(2,1)}, u32[]{:S(2)}) copy-start(bf16[4,3,128,128]{3,2,1,0:T(8,128)(2,1)} %vo.1) | copy-start | bytes 1179652
  0.7 29.3 %copy-start.5 = (bf16[2,32,32]{2,1,0:T(8,128)(2,1)S(1)}, bf16[2,32,32]{2,1,0:T(8,128)(2,1)}, u32[]{:S(2)}) copy-start(bf16[2,32,32]{2,1,0:T(8,128)(2,1)} %wg.3) | copy-start | bytes 12292
  0.7 29.3 %copy-start.4 = (bf16[2,32,32]{2,1,0:T(8,128)(2,1)S(1)}, bf16[2,32,32]{2,1,0:T(8,128)(2,1)}, u32[]{:S(2)}) copy-start(bf16[2,32,32]{2,1,0:T(8,128)(2,1)} %wf.3) | copy-start | bytes 12292
  0.7 29.3 %copy-start.9 = (f32[256]{0:T(256)S(1)}, f32[256]{0:T(256)}, u32[]{:S(2)}) copy-start(f32[256]{0:T(256)} %param.27) | copy-start | bytes 3076
  0.7 29.3 %copy-start.3 = (bf16[256,32]{0,1:T(8,128)(2,1)S(1)}, bf16[256,32]{0,1:T(8,128)(2,1)}, u32[]{:S(2)}) copy-start(bf16[256,32]{0,1:T(8,128)(2,1)} %param.26) | copy-start | bytes 49156
  0.7 29.3 %copy-start.12 = (f32[32]{0:T(128)S(1)}, f32[32]{0:T(128)}, u32[]{:S(2)}) copy-start(f32[32]{0:T(128)} %param.25) | copy-start | bytes 388
  0.7 29.3 %copy-start.6 = (bf16[32,96]{1,0:T(8,128)(2,1)S(1)}, bf16[32,96]{1,0:T(8,128)(2,1)}, u32[]{:S(2)}) copy-start(bf16[32,96]{1,0:T(8,128)(2,1)} %wm.1) | copy-start | bytes 18436
  0.7 29.3 %copy-start.11 = (f32[32]{0:T(128)S(1)}, f32[32]{0:T(128)}, u32[]{:S(2)}) copy-start(f32[32]{0:T(128)} %param.21) | copy-start | bytes 388
  0.7 29.3 %copy-start.10 = (f32[32]{0:T(128)S(1)}, f32[32]{0:T(128)}, u32[]{:S(2)}) copy-start(f32[32]{0:T(128)} %param.19) | copy-start | bytes 388
  0.7 29.3 %copy-start.8 = (f32[32]{0:T(128)S(1)}, f32[32]{0:T(128)}, u32[]{:S(2)}) copy-start(f32[32]{0:T(128)} %param.17) | copy-start | bytes 388
  0.8 29.3 %copy-start.7 = (f32[32]{0:T(128)S(1)}, f32[32]{0:T(128)}, u32[]{:S(2)}) copy-start(f32[32]{0:T(128)} %param.16) | copy-start | bytes 388
  0.8 36.1 %copy-start = (bf16[2,32,32,512]{3,2,1,0:T(8,128)(2,1)S(1)}, bf16[2,32,32,512]{3,2,1,0:T(8,128)(2,1)}, u32[]{:S(2)}) copy-start(bf16[2,32,32,512]{3,2,1,0:T(8,128)(2,1)} %param.28) | copy-start | bytes 6291460
  0.8 36.1 %copy-start.1 = (bf16[2,256,512]{2,1,0:T(8,128)(2,1)S(1)}, bf16[2,256,512]{2,1,0:T(8,128)(2,1)}, u32[]{:S(2)}) copy-start(bf16[2,256,512]{2,1,0:T(8,128)(2,1)} %gs.3) | copy-start | bytes 1572868
  4.4 25.5 %collective-permute-start.1 = (bf16[4,3,128,128]{3,2,1,0:T(8,128)(2,1)S(1)}, bf16[4,3,128,128]{3,2,1,0:T(8,128)(2,1)}, u32[]{:S(2)}, u32[]{:S(2)}) collective-permute-start(bf16[4,3,128,128]{3,2,1,0:T(8,128)(2,1)S(1)} %copy-done.2), channel_id=1, source_target_pairs={{4,0},{8,4},{12,8},{16,12},{20,16},{24,20},{28,24},{32,28},{36,32}... | collective-permute-start | bytes 1179656 | tf_op jit(solution)/shard_map/ppermute | solution.py:394
  5.7 24.2 %collective-permute-start = (bf16[4,3,128,128]{3,2,1,0:T(8,128)(2,1)S(1)}, bf16[4,3,128,128]{3,2,1,0:T(8,128)(2,1)}, u32[]{:S(2)}, u32[]{:S(2)}) collective-permute-start(bf16[4,3,128,128]{3,2,1,0:T(8,128)(2,1)S(1)} %copy-done.2), channel_id=1, source_target_pairs={{0,4},{4,8},{8,12},{12,16},{16,20},{20,24},{24,28},{28,32},{32,36}... | collective-permute-start | bytes 1179656 | tf_op jit(solution)/shard_map/ppermute | solution.py:394
  9.5 20.4 %all-to-all-start = ((bf16[32,4,1536]{2,1,0:T(4,128)(2,1)}), bf16[32,4,1536]{2,1,0:T(4,128)(2,1)S(1)}, u32[]{:S(2)}, u32[]{:S(2)}) async-start(bf16[32,4,1536]{2,1,0:T(4,128)(2,1)} %get-tuple-element.59), calls=%async_computation | async-start | bytes 786432 | tf_op jit(solution)/shard_map/all_to_all | solution.py:524
  20.0 16.8 %collective-permute-start.3 = (bf16[1024,512]{1,0:T(8,128)(2,1)}, bf16[1024,512]{1,0:T(8,128)(2,1)}, u32[]{:S(2)}, u32[]{:S(2)}) collective-permute-start(bf16[1024,512]{1,0:T(8,128)(2,1)} %get-tuple-element.68), channel_id=1, source_target_pairs={{4,0},{8,4},{12,8},{16,12},{20,16},{24,20},{28,24},{32,28},{36,32}... | collective-permute-start | bytes 3145736 | tf_op jit(solution)/shard_map/ppermute | solution.py:394
  21.3 15.5 %collective-permute-start.2 = (bf16[1024,512]{1,0:T(8,128)(2,1)}, bf16[1024,512]{1,0:T(8,128)(2,1)}, u32[]{:S(2)}, u32[]{:S(2)}) collective-permute-start(bf16[1024,512]{1,0:T(8,128)(2,1)} %get-tuple-element.68), channel_id=1, source_target_pairs={{0,4},{4,8},{8,12},{12,16},{16,20},{20,24},{24,28},{28,32},{32,36}... | collective-permute-start | bytes 3145736 | tf_op jit(solution)/shard_map/ppermute | solution.py:394
  32.2 18.9 %collective-permute-start.5 = (bf16[1024,512]{1,0:T(8,128)(2,1)}, bf16[1024,512]{1,0:T(8,128)(2,1)S(1)}, u32[]{:S(2)}, u32[]{:S(2)}) collective-permute-start(bf16[1024,512]{1,0:T(8,128)(2,1)} %get-tuple-element.76), channel_id=1, source_target_pairs={{4,0},{8,4},{12,8},{16,12},{20,16},{24,20},{28,24},{32,28},{36,32}... | collective-permute-start | bytes 3145736 | tf_op jit(solution)/shard_map/ppermute | solution.py:394
  33.5 17.6 %collective-permute-start.4 = (bf16[1024,512]{1,0:T(8,128)(2,1)}, bf16[1024,512]{1,0:T(8,128)(2,1)S(1)}, u32[]{:S(2)}, u32[]{:S(2)}) collective-permute-start(bf16[1024,512]{1,0:T(8,128)(2,1)} %get-tuple-element.76), channel_id=1, source_target_pairs={{0,4},{4,8},{8,12},{12,16},{16,20},{20,24},{24,28},{28,32},{32,36}... | collective-permute-start | bytes 3145736 | tf_op jit(solution)/shard_map/ppermute | solution.py:394
  58.2 3.2 %collective-permute-start.6 = (f32[104,128]{1,0:T(8,128)S(1)}, f32[104,128]{1,0:T(8,128)S(1)}, u32[]{:S(2)}, u32[]{:S(2)}) collective-permute-start(f32[104,128]{1,0:T(8,128)S(1)} %add.24), channel_id=1, source_target_pairs={{0,4},{4,0},{8,12},{12,8},{16,20},{20,16},{24,28},{28,24},{32,36},... | collective-permute-start | bytes 159752 | tf_op jit(solution)/shard_map/ppermute | solution.py:398
  61.5 8.6 %collective-permute-start.9 = (f32[104,128]{1,0:T(8,128)S(1)}, f32[104,128]{1,0:T(8,128)S(1)}, u32[]{:S(2)}, u32[]{:S(2)}) collective-permute-start(f32[104,128]{1,0:T(8,128)S(1)} %add.25), channel_id=1, source_target_pairs={{0,24},{4,28},{8,0},{12,4},{16,8},{20,12},{24,16},{28,20},{32,56},... | collective-permute-start | bytes 159752 | tf_op jit(solution)/shard_map/ppermute | solution.py:398
  65.3 6.0 %collective-permute-start.8 = (f32[104,128]{1,0:T(8,128)S(1)}, f32[104,128]{1,0:T(8,128)S(1)}, u32[]{:S(2)}, u32[]{:S(2)}) collective-permute-start(f32[104,128]{1,0:T(8,128)S(1)} %add.25), channel_id=1, source_target_pairs={{0,16},{4,20},{8,24},{12,28},{16,0},{20,4},{24,8},{28,12},{32,48},... | collective-permute-start | bytes 159752 | tf_op jit(solution)/shard_map/ppermute | solution.py:398
  65.4 6.1 %collective-permute-start.7 = (f32[104,128]{1,0:T(8,128)S(1)}, f32[104,128]{1,0:T(8,128)S(1)}, u32[]{:S(2)}, u32[]{:S(2)}) collective-permute-start(f32[104,128]{1,0:T(8,128)S(1)} %add.25), channel_id=1, source_target_pairs={{0,8},{4,12},{8,16},{12,20},{16,24},{20,28},{24,0},{28,4},{32,40},... | collective-permute-start | bytes 159752 | tf_op jit(solution)/shard_map/ppermute | solution.py:398
  71.5 7.8 %collective-permute-start.12 = (f32[104,128]{1,0:T(8,128)S(1)}, f32[104,128]{1,0:T(8,128)S(1)}, u32[]{:S(2)}, u32[]{:S(2)}) collective-permute-start(f32[104,128]{1,0:T(8,128)S(1)} %add_add_fusion.1), channel_id=1, source_target_pairs={{0,96},{4,100},{8,104},{12,108},{16,112},{20,116},{24,120},{28,124... | collective-permute-start | bytes 159752 | tf_op jit(solution)/shard_map/ppermute | solution.py:398
  75.9 5.7 %collective-permute-start.11 = (f32[104,128]{1,0:T(8,128)S(1)}, f32[104,128]{1,0:T(8,128)S(1)}, u32[]{:S(2)}, u32[]{:S(2)}) collective-permute-start(f32[104,128]{1,0:T(8,128)S(1)} %add_add_fusion.1), channel_id=1, source_target_pairs={{0,64},{4,68},{8,72},{12,76},{16,80},{20,84},{24,88},{28,92},{32,9... | collective-permute-start | bytes 159752 | tf_op jit(solution)/shard_map/ppermute | solution.py:398
  76.4 5.7 %collective-permute-start.10 = (f32[104,128]{1,0:T(8,128)S(1)}, f32[104,128]{1,0:T(8,128)S(1)}, u32[]{:S(2)}, u32[]{:S(2)}) collective-permute-start(f32[104,128]{1,0:T(8,128)S(1)} %add_add_fusion.1), channel_id=1, source_target_pairs={{0,32},{4,36},{8,40},{12,44},{16,48},{20,52},{24,56},{28,60},{32,6... | collective-permute-start | bytes 159752 | tf_op jit(solution)/shard_map/ppermute | solution.py:398
  82.1 6.6 %collective-permute-start.15 = (f32[104,128]{1,0:T(8,128)S(1)}, f32[104,128]{1,0:T(8,128)S(1)}, u32[]{:S(2)}, u32[]{:S(2)}) collective-permute-start(f32[104,128]{1,0:T(8,128)S(1)} %add_add_fusion.p0), channel_id=1, source_target_pairs={{0,3},{1,0},{2,1},{3,2},{4,7},{5,4},{6,5},{7,6},{8,11},{9,8},{10,9... | collective-permute-start | bytes 159752 | tf_op jit(solution)/shard_map/ppermute | solution.py:553
  84.9 5.6 %collective-permute-start.14 = (f32[104,128]{1,0:T(8,128)S(1)}, f32[104,128]{1,0:T(8,128)S(1)}, u32[]{:S(2)}, u32[]{:S(2)}) collective-permute-start(f32[104,128]{1,0:T(8,128)S(1)} %add_add_fusion.p0), channel_id=1, source_target_pairs={{0,2},{1,3},{2,0},{3,1},{4,6},{5,7},{6,4},{7,5},{8,10},{9,11},{10,... | collective-permute-start | bytes 159752 | tf_op jit(solution)/shard_map/ppermute | solution.py:553
  85.7 5.4 %collective-permute-start.13 = (f32[104,128]{1,0:T(8,128)S(1)}, f32[104,128]{1,0:T(8,128)S(1)}, u32[]{:S(2)}, u32[]{:S(2)}) collective-permute-start(f32[104,128]{1,0:T(8,128)S(1)} %add_add_fusion.p0), channel_id=1, source_target_pairs={{0,1},{1,2},{2,3},{3,0},{4,5},{5,6},{6,7},{7,4},{8,9},{9,10},{10,1... | collective-permute-start | bytes 159752 | tf_op jit(solution)/shard_map/ppermute | solution.py:553

commit v4 on v3

--- a/solution.py
+++ b/solution.py
@@ -26,7 +26,7 @@
 PAY = 104
 RES_SCALE = 1.0 / math.sqrt(8 * TOUT * 16384)
 SKIP_SCALE = 1.0 / math.sqrt(8 * 16384)
-VMEM_LIMIT = 40 * 1024 * 1024
+VMEM_LIMIT = 20 * 1024 * 1024
 
 
 def dot(a, b):
@@ -52,22 +52,10 @@
     return jnp.where(r == c, full, 0.0)
 
 
-def message_kernel(cols_hbm, speeds, grad, msg, first, second, cols, rows, wide, stage, sems):
-    half = first.shape[0]
+def message_kernel(cols_hbm, speeds, msg, cols, rows, wide, sems):
     loads = [
-        pltpu.make_async_copy(src, dst, sems.at[n])
-        for n, (src, dst) in enumerate(
-            (
-                (speeds, rows),
-                (cols_hbm, cols),
-                (grad.at[pl.ds(0, half)], stage.at[0]),
-                (grad.at[pl.ds(half, half)], stage.at[1]),
-            )
-        )
-    ]
-    stores = [
-        pltpu.make_async_copy(stage.at[n], dst, sems.at[4 + n])
-        for n, dst in enumerate((first, second))
+        pltpu.make_async_copy(speeds, rows, sems.at[0]),
+        pltpu.make_async_copy(cols_hbm, cols, sems.at[1]),
     ]
     for copy in loads:
         copy.start()
@@ -86,14 +74,8 @@
         axis=1,
     )
     row = lax.broadcasted_iota(jnp.int32, (4, 3 * W), 0)
-    loads[2].wait()
-    stores[0].start()
     for d in range(32):
         msg[d] = jnp.where(row == 3, offsets, wide[:, d * W : (d + 3) * W]).astype(BF16)
-    loads[3].wait()
-    stores[1].start()
-    stores[0].wait()
-    stores[1].wait()
 
 
 def prep_kernel(
@@ -203,8 +185,10 @@
     return jnp.tanh(a0f * p + a1f * q + cf), jnp.tanh(a0g * p + a1g * q + cg) + 1.0
 
 
-def forward_kernel(base, count, xs, coef, mix, bandt, zown, *refs):
-    res, ahead, zext, one, stack = refs[-5:]
+def forward_kernel(
+    xs, coef, mix, bandt, wsk, bsk, wskt, grad, gskip,
+    res, skip, z, dfil, dgat, esum, dsk, extra, ahead, zext, one, stack,
+):
     i = pl.program_id(0)
 
     def at(step):
@@ -214,29 +198,35 @@
             xs.at[pl.ds(pl.multiple_of(row + DIL, TG), TG)],
         )
 
-    halo = [t for t in range(12) if not 4 <= t < 8]
-
-    def look_ahead(x0, x1, k, n):
+    def look_ahead(step, k, t):
+        x0, x1 = at(step)
+
         def emit():
-            lanes = lane_tile(halo[n])
+            lanes = lane_tile(t)
             f, u = gates(coef, x0[k : k + 1, lanes], x1[k : k + 1, lanes])
-            ahead[slab_rows(k), lane_tile(n)] = (f * u).astype(BF16)
+            fu = f * u
+            ahead[slab_rows(k), lanes] = fu.astype(BF16)
+            if 4 <= t < 8:
+                rows = pl.ds(pl.multiple_of(step * ROWS + k * C, C), C)
+                dfil[rows, lane_tile(t - 4)] = (u - f * fu).astype(BF16)
+                dgat[rows, lane_tile(t - 4)] = (fu * (2.0 - u)).astype(BF16)
 
         return emit
 
     @pl.when(i == 0)
     def _():
-        x0, x1 = at(i + base)
+        esum[...] = jnp.zeros_like(esum)
+        dsk[...] = jnp.zeros_like(dsk)
         for k in range(TG):
-            for n in range(8):
-                look_ahead(x0, x1, k, n)()
-
-    zext[:, 0:W] = ahead[:, 0:W]
-    zext[:, W : 2 * W] = zown[...]
-    zext[:, 2 * W : 3 * W] = ahead[:, W : 2 * W]
-    stack[0:ROWS, :] = zown[...]
-    n0, n1 = at(jnp.minimum(i + 1, count - 1) + base)
-    emit = spread([look_ahead(n0, n1, k, n) for k in range(TG) for n in range(8)], 6)
+            for t in range(12):
+                look_ahead(i, k, t)()
+
+    mine = pl.ds(pl.multiple_of(i * ROWS, ROWS), ROWS)
+    zext[...] = ahead[...]
+    stack[0:ROWS, :] = ahead[:, W : 2 * W]
+    z[mine, :] = ahead[:, W : 2 * W]
+    ahead_step = jnp.minimum(i + 1, 7)
+    emit = spread([look_ahead(ahead_step, k, t) for k in range(TG) for t in range(12)], 6)
 
     def put(p, v):
         stack[2 * ROWS : 3 * ROWS, p * PAIR : (p + 1) * PAIR] = v
@@ -246,19 +236,39 @@
     mixed = dot(mix[...], stack[...])
     ws, bs, bm = coefs(coef, WS, BS, BM)
     bb = bs + bm
-    x1 = at(i + base)[1]
+    x1 = at(i)[1]
+    go = grad.at[mine]
+    se, sq = esum[0], esum[1]
     for k in range(TG):
         for t in range(TILES):
             q = x1[k : k + 1, W + t * TILE : W + (t + 1) * TILE]
             r, lanes = slab_rows(k), lane_tile(t)
             res[r, lanes] = (mixed[r, lanes] + (ws * q + bb)).astype(BF16)
-
-
-def backward_kernel(sample, xs, coef, mixt, wsk, wskt, bsk, band, gl, go, gr, gs, *refs):
-    skip, pay, zb, ext, one, stack, dzs, fs, us, acc, dmx, dsk, extra = refs[-13:]
+            e = go[r, lanes].astype(F32)
+            se = se + e
+            sq = sq + e * q
+    esum[0] = se
+    esum[1] = sq
+
+    @pl.when(i % 4 == 3)
+    def _():
+        gs = gskip.at[i // 4]
+        bias = jnp.concatenate([bsk[...]] * TILES, axis=1)
+        z31 = stack[ROWS - C : ROWS, :]
+        twos = jnp.full((16, W), 2.0, BF16)
+        skip[0] = (dot(wsk[...], z31) + bias).astype(BF16)
+        dsk[...] += dot_nt(jnp.concatenate([z31, twos], axis=0), gs[...])
+        extra[i // 4] = dot(wskt[...], gs[...]) * (SKIP_SCALE / RES_SCALE)
+
+
+def backward_kernel(
+    xs, mixt, band, gl, grad, gr, z, dfil, dgat, esum, dsk, extra,
+    pay, ext, one, stack, dzs, acc, dmx,
+):
     i = pl.program_id(0)
-    last = i == 3
-    at = (sample * 6 + i) * TG
+    mine = pl.ds(pl.multiple_of(i * ROWS, ROWS), ROWS)
+    go, zb, fa, ga = (ref.at[mine] for ref in (grad, z, dfil, dgat))
+    at = ((i // 4) * 6 + i % 4) * TG
     x0 = xs.at[pl.ds(pl.multiple_of(at, TG), TG)]
     x1 = xs.at[pl.ds(pl.multiple_of(at + DIL, TG), TG)]
 
@@ -266,51 +276,31 @@
     def _():
         acc[...] = jnp.zeros_like(acc)
         dmx[...] = jnp.zeros_like(dmx)
-        extra[...] = jnp.zeros_like(extra)
-
-    @pl.when(last)
-    def _():
-        extra[...] = dot(wskt[...], gs[0]) * (SKIP_SCALE / RES_SCALE)
 
     ext[:, 0:W] = gl[...]
     ext[:, W : 2 * W] = go[...]
     ext[:, 2 * W : 3 * W] = gr[...]
     stack[0:ROWS, :] = go[...]
 
-    def rows_of(k, t):
-        lanes = slice(W + t * TILE, W + (t + 1) * TILE)
-        return x0[k : k + 1, lanes], x1[k : k + 1, lanes]
-
-    def gate(k, t):
-        def emit():
-            r, lanes = slab_rows(k), lane_tile(t)
-            f, u = gates(coef, *rows_of(k, t))
-            fs[r, lanes] = f
-            us[r, lanes] = u
-            zb[r, lanes] = (f * u).astype(BF16)
-
-        return emit
-
     def put(p, v):
         stack[2 * ROWS : 3 * ROWS, p * PAIR : (p + 1) * PAIR] = v
 
-    hops(ext, one, band, put, spread([gate(k, t) for k in range(TG) for t in range(TILES)], 6))
+    hops(ext, one, band, put, lambda: None)
     stack[ROWS : 2 * ROWS, :] = one[:, PAIR : PAIR + W]
     dzs[...] = dot(mixt[...], stack[...])
-    dzs[ROWS - C : ROWS, :] += extra[...]
-
-    sums = [acc[j] for j in range(8)]
+    dzs[ROWS - C : ROWS, :] += extra[i // 4] * jnp.where(i % 4 == 3, 1.0, 0.0)
+
+    sums = [acc[j] for j in range(6)]
 
     def local(k, t):
         def emit():
             r, lanes = slab_rows(k), lane_tile(t)
-            p, q = rows_of(k, t)
-            f, u = fs[r, lanes], us[r, lanes]
-            s = dzs[r, lanes] * u
-            df = s * (1.0 - f * f)
-            dgt = (s * f) * (2.0 - u)
-            e = go[r, lanes].astype(F32)
-            for j, term in enumerate((df * p, df * q, df, dgt * p, dgt * q, dgt, e * q, e)):
+            across = slice(W + t * TILE, W + (t + 1) * TILE)
+            p, q = x0[k : k + 1, across], x1[k : k + 1, across]
+            dz = dzs[r, lanes]
+            df = dz * fa[r, lanes].astype(F32)
+            dgt = dz * ga[r, lanes].astype(F32)
+            for j, term in enumerate((df * p, df * q, df, dgt * p, dgt * q, dgt)):
                 sums[j] = sums[j] + term
 
         return emit
@@ -320,17 +310,11 @@
         part = slice(h * ROWS, (h + 1) * ROWS)
         dmx[part, :] += dot_nt(stack[part, :], zb[...])
         emit()
-    for j in range(8):
+    for j in range(6):
         acc[j] = sums[j]
 
-    @pl.when(last)
+    @pl.when(i == 7)
     def _():
-        z31 = zb[ROWS - C : ROWS, :]
-        twos = jnp.full((16, W), 2.0, BF16)
-        dsk[...] = dot_nt(jnp.concatenate([z31, twos], axis=0), gs[0])
-        bias = jnp.concatenate([bsk[...]] * TILES, axis=1)
-        skip[0] = (dot(wsk[...], z31) + bias).astype(BF16)
-
         r = lax.broadcasted_iota(jnp.int32, (ROWS, ROWS), 0) // C
         c = lax.broadcasted_iota(jnp.int32, (ROWS, ROWS), 1) // C
         lane = lax.broadcasted_iota(jnp.int32, (C, TILE), 1)
@@ -344,10 +328,10 @@
             v = v + pltpu.roll(v, 64, 1)
             v = v + pltpu.roll(v, 32, 1)
             packed = jnp.where(lane // C == h, v, packed)
-        scales = (0.5,) * 3 + (0.25,) * 3 + (1.0,) * 2
         packed = packed * (0.5 * RES_SCALE)
-        for j in range(8):
-            s = jnp.sum(acc[j], axis=1, keepdims=True) * (scales[j] * RES_SCALE)
+        parts = [(acc[j], 0.5 if j < 3 else 0.25) for j in range(6)] + [(esum[1], 1.0), (esum[0], 1.0)]
+        for j, (a, scale) in enumerate(parts):
+            s = jnp.sum(a, axis=1, keepdims=True) * (scale * RES_SCALE)
             packed = jnp.where(lane == 96 + j, s, packed)
         pay[0:C, :] = packed
         pay[C : 2 * C, :] = dsk[0:C, 0:TILE] * (0.5 * SKIP_SCALE)
@@ -411,78 +395,81 @@
 HBM = pl.BlockSpec(memory_space=pltpu.HBM)
 
 
-def forward_call(base, count, xs, coef, mix, bandt, zown, before):
-    more = [] if before is None else [before]
+def forward_call(xs, coef, mix, bandt, wsk, bsk, wskt, grad, gskip):
+    rows = BR * TOUT * C
     return pl.pallas_call(
-        functools.partial(forward_kernel, base, count),
-        grid=(count,),
-        out_shape=jax.ShapeDtypeStruct((BR * TOUT * C, W), BF16),
-        in_specs=[VMEM] * 4
-        + [pl.BlockSpec((ROWS, W), lambda i: (i + base % 4, 0))]
-        + [ANY] * len(more),
-        out_specs=pl.BlockSpec((ROWS, W), lambda i: (i + base, 0)),
+        forward_kernel,
+        grid=(8,),
+        out_shape=(
+            jax.ShapeDtypeStruct((rows, W), BF16),
+            jax.ShapeDtypeStruct((BR, SKIP, W), BF16),
+            jax.ShapeDtypeStruct((rows, W), BF16),
+            jax.ShapeDtypeStruct((rows, W), BF16),
+            jax.ShapeDtypeStruct((rows, W), BF16),
+            jax.ShapeDtypeStruct((2, C, TILE), F32),
+            jax.ShapeDtypeStruct((C + 16, SKIP), F32),
+            jax.ShapeDtypeStruct((BR, C, W), F32),
+        ),
+        in_specs=[VMEM] * 9,
+        out_specs=(
+            pl.BlockSpec((ROWS, W), lambda i: (i, 0)),
+            pl.BlockSpec((1, SKIP, W), lambda i: (i // 4, 0, 0)),
+        )
+        + (VMEM,) * 6,
         scratch_shapes=[
-            pltpu.VMEM((ROWS, 2 * W), BF16),
+            pltpu.VMEM((ROWS, 3 * W), BF16),
             pltpu.VMEM((ROWS, 3 * W), BF16),
             pltpu.VMEM((ROWS, 2 * W), BF16),
             pltpu.VMEM((3 * ROWS, W), BF16),
         ],
-        input_output_aliases={5: 0} if more else {},
         compiler_params=params(),
+        cost_estimate=pl.CostEstimate(
+            flops=20_000_000_000, bytes_accessed=16_000_000, transcendentals=6_000_000
+        ),
         name="forward",
-    )(xs, coef, mix, bandt, zown, *more)
-
-
-def backward_call(sample, xs, coef, mixt, wsk, wskt, bsk, band, gl, go, gr, gs, before):
-    more = [] if before is None else [before]
+    )(xs, coef, mix, bandt, wsk, bsk, wskt, grad, gskip)
+
+
+def backward_call(xs, mixt, band, gl, go, gr, *early):
     slab = pl.BlockSpec((ROWS, W), lambda i: (i, 0))
-    own = pl.BlockSpec((ROWS, W), lambda i: (i + 4 * sample, 0))
-    per_sample = pl.BlockSpec((1, SKIP, W), lambda i: (sample, 0, 0))
     return pl.pallas_call(
-        functools.partial(backward_kernel, sample),
-        grid=(4,),
-        out_shape=(
-            jax.ShapeDtypeStruct((BR, SKIP, W), BF16),
-            jax.ShapeDtypeStruct((PAY, TILE), F32),
-            jax.ShapeDtypeStruct((TOUT * C, W), BF16),
-        ),
-        in_specs=[VMEM] * 7 + [slab, own, slab, per_sample] + [ANY] * len(more),
-        out_specs=(per_sample, whole((PAY, TILE)), slab),
+        backward_kernel,
+        grid=(8,),
+        out_shape=jax.ShapeDtypeStruct((PAY, TILE), F32),
+        in_specs=[VMEM] * 3 + [slab, VMEM, slab] + [VMEM] * 6,
+        out_specs=VMEM,
         scratch_shapes=[
             pltpu.VMEM((ROWS, 3 * W), BF16),
             pltpu.VMEM((ROWS, 2 * W), BF16),
             pltpu.VMEM((3 * ROWS, W), BF16),
             pltpu.VMEM((ROWS, W), F32),
-            pltpu.VMEM((ROWS, W), F32),
-            pltpu.VMEM((ROWS, W), F32),
-            pltpu.VMEM((8, C, TILE), F32),
+            pltpu.VMEM((6, C, TILE), F32),
             pltpu.VMEM((3 * ROWS, ROWS), F32),
-            pltpu.VMEM((C + 16, SKIP), F32),
-            pltpu.VMEM((C, W), F32),
         ],
-        input_output_aliases={11: 0} if more else {},
         compiler_params=params(),
         name="backward",
-    )(xs, coef, mixt, wsk, wskt, bsk, band, gl, go, gr, gs, *more)
-
-
-def send(speeds, cols, grad):
-    half = pltpu.HBM((grad.shape[0] // 2, W), BF16)
+    )(xs, mixt, band, gl, go, gr, *early)
+
+
+def in_hbm(a):
+    return pltpu.with_memory_space_constraint(a, pltpu.HBM)
+
+
+def send(speeds, cols):
     return pl.pallas_call(
         message_kernel,
-        out_shape=(jax.ShapeDtypeStruct((32, 4, 3 * W), BF16), half, half),
-        in_specs=[HBM] * 3,
-        out_specs=(VMEM, HBM, HBM),
+        out_shape=jax.ShapeDtypeStruct((32, 4, 3 * W), BF16),
+        in_specs=[HBM] * 2,
+        out_specs=VMEM,
         scratch_shapes=[
             pltpu.SMEM((TILES, 3), jnp.int32),
             pltpu.VMEM((3, 16384), F32),
             pltpu.VMEM((4, 16384 + 2 * W), F32),
-            pltpu.VMEM((2, grad.shape[0] // 2, W), BF16),
-            pltpu.SemaphoreType.DMA((6,)),
+            pltpu.SemaphoreType.DMA((2,)),
         ],
         compiler_params=params(),
         name="message",
-    )(*(pltpu.with_memory_space_constraint(a, pltpu.HBM) for a in (cols, speeds, grad)))
+    )(in_hbm(cols), in_hbm(speeds))
 
 
 def prepare(msg, vals, w_start, b_start, w_filter, b_filter, w_gate, b_gate, w_mix, b_mix, w_skip, b_skip):
@@ -508,7 +495,7 @@
         out_specs=(VMEM,) * 8,
         compiler_params=params(),
         name="prep",
-    )(*small, msg)
+    )(*(in_hbm(a) for a in small), msg)
 
 
 def body(
@@ -516,40 +503,22 @@
     w_mix, b_mix, w_skip, b_skip, grad_res, grad_skip,
 ):
     barrier = lax.optimization_barrier
-    half = TOUT * C
-    grad = grad_res.reshape(BR * half, W)
-    msg, first, second = send(speeds, adj_cols, grad)
-    halo0 = neighbour(first, 1), neighbour(first, -1)
+    grad = grad_res.reshape(BR * TOUT * C, W)
+    msg = send(speeds, adj_cols)
     msg, vals = barrier((msg, adj_vals))
     msg = lax.all_to_all(msg, "seg", split_axis=0, concat_axis=0, tiled=True)
     vals = (neighbour(vals, 1), adj_vals, neighbour(vals, -1))
+    *vals, grad_now = barrier((*vals, grad))
+    grad_l, grad_r = neighbour(grad_now, 1), neighbour(grad_now, -1)
     coef, mix, mixt, wsk, bsk, band, bandt, xs = prepare(
         msg, vals, w_start, b_start, w_filter, b_filter, w_gate, b_gate, w_mix, b_mix, w_skip, b_skip
     )
-    xs, second = barrier((xs, second))
-    halo1 = neighbour(second, 1), neighbour(second, -1)
-
-    common = (coef, mixt, wsk, w_skip.T, bsk, band)
-    skip, pay0, z0 = backward_call(0, xs, *common, halo0[0], grad, halo0[1], grad_skip, None)
-    pay0, xs = barrier((pay0, xs))
-    res = forward_call(0, 4, xs, coef, mix, bandt, z0, None)
-    res, xs = barrier((res, xs))
-    skip, pay1, z1 = backward_call(1, xs, *common, halo1[0], grad, halo1[1], grad_skip, skip)
-
-    v = pay0 + pay1
+    res, skip, *early = forward_call(xs, coef, mix, bandt, wsk, bsk, w_skip.T, grad, grad_skip)
+    v = backward_call(xs, mixt, band, grad_l, grad, grad_r, *early)
+
     v = v + seg_ring(v, lambda i: i ^ 1)
-
-    def forward(base, count, v, before):
-        v, z_now = barrier((v, z1))
-        return v, forward_call(base, count, xs, coef, mix, bandt, z_now, before)
-
-    v, res = forward(4, 2, v, res)
     v = v + sum(seg_ring(v, lambda i, k=k: (i // 8) * 8 + ((i // 2 + k) % 4) * 2 + i % 2) for k in (1, 2, 3))
-    v, res = barrier((v, res))
-    v, res = forward(6, 1, v, res)
     v = v + sum(seg_ring(v, lambda i, k=k: (i + 8 * k) % 32) for k in (1, 2, 3))
-    v, res = barrier((v, res))
-    v, res = forward(7, 1, v, res)
     others = [lax.ppermute(v, "rep", [(i, (i + k) % 4) for i in range(4)]) for k in (1, 2, 3)]
 
     row = jax.ShapeDtypeStruct((1, C), F32)

time: 92.3 us -> 89.3 us (0.967)
  Pallas kernels: 35.7 us -> 30.4 us
  waiting for transfers between devices: 12.2 us -> 16.3 us
  starting transfers between devices: 43 us -> 41.3 us
    ppermute x6 -> x4, starting transfers between devices: 14.9 us -> 7.41 us  [neighbour(): return lax.ppermute(value, 'seg', pairs)]
    pallas_call x7 -> x3, Pallas kernels: 32.7 us -> 27.2 us  [the longest x1 13.5 us: forward_call(): pl.pallas_call(forward_kernel, grid=(8,), out_shape=(jax.ShapeDtypeStruct...]
    ppermute x7, starting transfers between devices: 13.1 us -> 16.8 us  [seg_ring(): lax.ppermute(value, 'seg', [(i, shift(i)) for i in range(lax.axis_size('s...]
    ppermute x7, waiting for transfers between devices: 5.09 us -> 8.5 us  [seg_ring(): lax.ppermute(value, 'seg', [(i, shift(i)) for i in range(lax.axis_size('s...]
    ppermute x3, starting transfers between devices: 4.51 us -> 5.72 us  [body(): lax.ppermute(v, 'rep', [(i, (i + k) % 4) for i in range(4)])]
  transfers between devices with their start and end apart: 17 -> 15, of which waited for: 8 -> 8; matrix products, arithmetic and copies ran while one was open for 0% -> 0% of each run, Pallas kernels for 26% -> 18%
where the time goes in v4:
time: 89.3 us; the launch traced here: 88.9 us
  starting transfers between devices  41.3 us (46%)
  Pallas kernels  30.4 us (34%)
  waiting for transfers between devices  16.3 us (18%)
    ppermute x7, starting transfers between devices, seg_ring(): lax.ppermute(value, 'seg', [(i, shift(i)) for i in range(lax.axis_size('s...  16.8 us
    pallas_call x1, Pallas kernels, forward_call(): pl.pallas_call(forward_kernel, grid=(8,), out_shape=(jax.ShapeDtypeStruct...  13.5 us
    pallas_call x1, Pallas kernels, backward_call(): pl.pallas_call(backward_kernel, grid=(8,), out_shape=jax.ShapeDtypeStruct...  11.6 us
    all_to_all x1, starting transfers between devices, body(): msg = lax.all_to_all(msg, 'seg', split_axis=0, concat_axis=0, tiled=True)  11.4 us
    ppermute x7, waiting for transfers between devices, seg_ring(): lax.ppermute(value, 'seg', [(i, shift(i)) for i in range(lax.axis_size('s...  8.5 us
    ppermute x4, starting transfers between devices, neighbour(): return lax.ppermute(value, 'seg', pairs)  7.41 us
    ppermute x3, starting transfers between devices, body(): lax.ppermute(v, 'rep', [(i, (i + k) % 4) for i in range(4)])  5.72 us
    all_to_all x1, waiting for transfers between devices, body(): msg = lax.all_to_all(msg, 'seg', split_axis=0, concat_axis=0, tiled=True)  5.11 us
  transfers between devices with their start and end apart: 15, of which 8 were waited for; matrix products, arithmetic and copies ran while one was open for 0% of the time, Pallas kernels for 18%

profile of v4, /device:TPU:0, one launch (start us, length us, event | category | flops | bytes accessed | tf_op | source)
XLA Modules:
  0.0 88.9 jit_solution(1433097483135327815)
XLA Ops:
  0.6 0.0 copy-start
  0.7 0.0 copy-start.3
  0.7 0.0 copy-start.6
  0.7 2.0 %message.1 = bf16[32,4,1536]{2,1,0:T(4,128)(2,1)} custom-call(s32[4,3]{1,0:T(4,128)} %cols_hbm.1, f32[3,16384]{1,0:T(4,128)} %speeds.1), custom_call_target="tpu_custom_call" | custom-call | tf_op jit(solution)/shard_map/message/pallas_call | solution.py:459
  2.7 1.3 %collective-permute-start = (bf16[4,3,128,128]{3,2,1,0:T(8,128)(2,1)}, bf16[4,3,128,128]{3,2,1,0:T(8,128)(2,1)S(1)}, u32[]{:S(2)}, u32[]{:S(2)}) collective-permute-start(bf16[4,3,128,128]{3,2,1,0:T(8,128)(2,1)} %vo), channel_id=1, source_target_pairs={{0,4},{4,8},{8,12},{12,16},{16,20},{20,24},{24,28},{28,32},{32,36}... | collective-permute-start | bytes 1179656 | tf_op jit(solution)/shard_map/ppermute | solution.py:378
  4.0 1.3 %collective-permute-start.1 = (bf16[4,3,128,128]{3,2,1,0:T(8,128)(2,1)}, bf16[4,3,128,128]{3,2,1,0:T(8,128)(2,1)}, u32[]{:S(2)}, u32[]{:S(2)}) collective-permute-start(bf16[4,3,128,128]{3,2,1,0:T(8,128)(2,1)} %vo), channel_id=1, source_target_pairs={{4,0},{8,4},{12,8},{16,12},{20,16},{24,20},{28,24},{32,28},{36,32}... | collective-permute-start | bytes 1179656 | tf_op jit(solution)/shard_map/ppermute | solution.py:378
  5.3 11.4 %all-to-all-start = ((bf16[32,4,1536]{2,1,0:T(4,128)(2,1)}), bf16[32,4,1536]{2,1,0:T(4,128)(2,1)S(1)}, u32[]{:S(2)}, u32[]{:S(2)}) async-start(bf16[32,4,1536]{2,1,0:T(4,128)(2,1)} %message.1), calls=%async_computation | async-start | bytes 786432 | tf_op jit(solution)/shard_map/all_to_all | solution.py:509
  16.7 0.0 collective-permute-done.vl
  16.8 0.0 copy-start.7
  16.8 0.0 collective-permute-done.1.vr
  16.8 3.5 %collective-permute-start.2 = (bf16[2048,512]{1,0:T(8,128)(2,1)}, bf16[2048,512]{1,0:T(8,128)(2,1)}, u32[]{:S(2)}, u32[]{:S(2)}) collective-permute-start(bf16[2048,512]{1,0:T(8,128)(2,1)} %bitcast.16), channel_id=1, source_target_pairs={{0,4},{4,8},{8,12},{12,16},{16,20},{20,24},{24,28},{28,32},{32,36}... | collective-permute-start | bytes 6291464 | tf_op jit(solution)/shard_map/ppermute | solution.py:378
  20.3 1.3 %collective-permute-start.3 = (bf16[2048,512]{1,0:T(8,128)(2,1)}, bf16[2048,512]{1,0:T(8,128)(2,1)}, u32[]{:S(2)}, u32[]{:S(2)}) collective-permute-start(bf16[2048,512]{1,0:T(8,128)(2,1)} %bitcast.17), channel_id=1, source_target_pairs={{4,0},{8,4},{12,8},{16,12},{20,16},{24,20},{28,24},{32,28},{36,32}... | collective-permute-start | bytes 6291464 | tf_op jit(solution)/shard_map/ppermute | solution.py:378
  21.6 5.1 %all-to-all-done.msg = bf16[32,4,1536]{2,1,0:T(4,128)(2,1)S(1)} async-done(((bf16[32,4,1536]{2,1,0:T(4,128)(2,1)}), bf16[32,4,1536]{2,1,0:T(4,128)(2,1)S(1)}, u32[]{:S(2)}, u32[]{:S(2)}) %all-to-all-start) | async-done | bytes 393248 | tf_op jit(solution)/shard_map/all_to_all | solution.py:509
  26.7 0.0 copy-done.7
  26.7 2.4 %prep.1 = (f32[288,128]{1,0:T(8,128)S(1)}, bf16[256,768]{1,0:T(8,128)(2,1)S(1)}, bf16[256,768]{1,0:T(8,128)(2,1)S(1)}, bf16[256,32]{1,0:T(8,128)(2,1)S(1)}, f32[...) custom-call(f32[1,32]{1,0:T(1,128)} %bitcast.22, ...), custom_call_target="tpu_custom_call" | custom-call | tf_op jit(solution)/shard_map/prep/pallas_call | solution.py:481
  29.1 0.0 copy-done
  29.1 0.0 copy-done.3
  29.2 0.0 copy-done.6
  29.2 13.5 %forward.1 = (bf16[2048,512]{1,0:T(8,128)(2,1)}, bf16[2,256,512]{2,1,0:T(8,128)(2,1)}, bf16[2048,512]{1,0:T(8,128)(2,1)S(1)}, bf16[2048,512]{1,0:T(8,128)(2,1)S(...) custom-call(f32[96,1536]{1,0:T(8,128)S(1)} %get-tuple-element.49.xs,, ...), custom_call_target="tpu_custom_call" | custom-call | flops 20000000000 | bytes 16000000 | tf_op jit(solution)/shard_map/forward/pallas_call | solution.py:400
  42.7 0.0 collective-permute-done.2.gl
  42.7 0.0 collective-permute-done.3.gr
  42.7 0.0 copy-start.1
  42.7 0.0 copy-start.2
  42.7 0.0 copy-start.4
  42.7 0.0 copy-start.5
  42.8 11.6 %backward.1 = f32[104,128]{1,0:T(8,128)S(1)} custom-call(f32[96,1536]{1,0:T(8,128)S(1)} %get-tuple-element.49.xs, bf16[256,768]{1,0:T(8,128)(2,1)S(1)} %get-tuple-element.57.mixt, bf16[4,768,256]{2,1,0:T(8,128)(2,1)S(1)} %get-tuple-element.58.band, bf16[2048,512]{1,0:T(8,128)(2,1)} %collective-permute-done.2.gl, bf16[2048,512]{1,0:T(8,128)(2,1)S(1)} %bitcast.19, ...), custom_call_target="tpu_custom_call" | custom-call | tf_op jit(solution)/shard_map/backward/pallas_call | solution.py:435
  54.3 5.8 %collective-permute-start.4 = (f32[104,128]{1,0:T(8,128)S(1)}, f32[104,128]{1,0:T(8,128)S(1)}, u32[]{:S(2)}, u32[]{:S(2)}) collective-permute-start(f32[104,128]{1,0:T(8,128)S(1)} %backward.1), channel_id=1, source_target_pairs={{0,4},{4,0},{8,12},{12,8},{16,20},{20,16},{24,28},{28,24},{32,36},... | collective-permute-start | bytes 159752 | tf_op jit(solution)/shard_map/ppermute | solution.py:382
  60.1 0.9 collective-permute-done.4
  61.0 4.7 %collective-permute-start.7 = (f32[104,128]{1,0:T(8,128)S(1)}, f32[104,128]{1,0:T(8,128)S(1)}, u32[]{:S(2)}, u32[]{:S(2)}) collective-permute-start(f32[104,128]{1,0:T(8,128)S(1)} %add.21), channel_id=1, source_target_pairs={{0,24},{4,28},{8,0},{12,4},{16,8},{20,12},{24,16},{28,20},{32,56},... | collective-permute-start | bytes 159752 | tf_op jit(solution)/shard_map/ppermute | solution.py:382
  65.7 0.0 collective-permute-start.5
  65.7 1.5 %collective-permute-start.6 = (f32[104,128]{1,0:T(8,128)S(1)}, f32[104,128]{1,0:T(8,128)S(1)}, u32[]{:S(2)}, u32[]{:S(2)}) collective-permute-start(f32[104,128]{1,0:T(8,128)S(1)} %add.21), channel_id=1, source_target_pairs={{0,16},{4,20},{8,24},{12,28},{16,0},{20,4},{24,8},{28,12},{32,48},... | collective-permute-start | bytes 159752 | tf_op jit(solution)/shard_map/ppermute | solution.py:382
  67.2 0.2 collective-permute-done.7
  67.5 4.4 %collective-permute-done.5 = f32[104,128]{1,0:T(8,128)S(1)} collective-permute-done((f32[104,128]{1,0:T(8,128)S(1)}, f32[104,128]{1,0:T(8,128)S(1)}, u32[]{:S(2)}, u32[]{:S(2)}) %collective-permute-start.5) | collective-permute-done | bytes 53280 | tf_op jit(solution)/shard_map/ppermute | solution.py:382
  71.9 0.0 collective-permute-done.6
  71.9 0.2 collective-permute-start.10
  72.1 1.9 %collective-permute-start.8 = (f32[104,128]{1,0:T(8,128)S(1)}, f32[104,128]{1,0:T(8,128)S(1)}, u32[]{:S(2)}, u32[]{:S(2)}) collective-permute-start(f32[104,128]{1,0:T(8,128)S(1)} %add_add_fusion.1), channel_id=1, source_target_pairs={{0,32},{4,36},{8,40},{12,44},{16,48},{20,52},{24,56},{28,60},{32,6... | collective-permute-start | bytes 159752 | tf_op jit(solution)/shard_map/ppermute | solution.py:382
  74.0 2.7 %collective-permute-start.9 = (f32[104,128]{1,0:T(8,128)S(1)}, f32[104,128]{1,0:T(8,128)S(1)}, u32[]{:S(2)}, u32[]{:S(2)}) collective-permute-start(f32[104,128]{1,0:T(8,128)S(1)} %add_add_fusion.1), channel_id=1, source_target_pairs={{0,64},{4,68},{8,72},{12,76},{16,80},{20,84},{24,88},{28,92},{32,9... | collective-permute-start | bytes 159752 | tf_op jit(solution)/shard_map/ppermute | solution.py:382
  76.8 0.0 collective-permute-done.10
  76.8 1.3 %collective-permute-done.8 = f32[104,128]{1,0:T(8,128)S(1)} collective-permute-done((f32[104,128]{1,0:T(8,128)S(1)}, f32[104,128]{1,0:T(8,128)S(1)}, u32[]{:S(2)}, u32[]{:S(2)}) %collective-permute-start.8) | collective-permute-done | bytes 53280 | tf_op jit(solution)/shard_map/ppermute | solution.py:382
  78.1 1.6 %collective-permute-done.9 = f32[104,128]{1,0:T(8,128)S(1)} collective-permute-done((f32[104,128]{1,0:T(8,128)S(1)}, f32[104,128]{1,0:T(8,128)S(1)}, u32[]{:S(2)}, u32[]{:S(2)}) %collective-permute-start.9) | collective-permute-done | bytes 53280 | tf_op jit(solution)/shard_map/ppermute | solution.py:382
  79.7 1.6 %collective-permute-start.11 = (f32[104,128]{1,0:T(8,128)S(1)}, f32[104,128]{1,0:T(8,128)S(1)}, u32[]{:S(2)}, u32[]{:S(2)}) collective-permute-start(f32[104,128]{1,0:T(8,128)S(1)} %add_add_fusion.p0), channel_id=1, source_target_pairs={{0,1},{1,2},{2,3},{3,0},{4,5},{5,6},{6,7},{7,4},{8,9},{9,10},{10,1... | collective-permute-start | bytes 159752 | tf_op jit(solution)/shard_map/ppermute | solution.py:522
  81.3 2.7 %collective-permute-start.12 = (f32[104,128]{1,0:T(8,128)S(1)}, f32[104,128]{1,0:T(8,128)S(1)}, u32[]{:S(2)}, u32[]{:S(2)}) collective-permute-start(f32[104,128]{1,0:T(8,128)S(1)} %add_add_fusion.p0), channel_id=1, source_target_pairs={{0,2},{1,3},{2,0},{3,1},{4,6},{5,7},{6,4},{7,5},{8,10},{9,11},{10,... | collective-permute-start | bytes 159752 | tf_op jit(solution)/shard_map/ppermute | solution.py:522
  84.0 1.4 %collective-permute-start.13 = (f32[104,128]{1,0:T(8,128)S(1)}, f32[104,128]{1,0:T(8,128)S(1)}, u32[]{:S(2)}, u32[]{:S(2)}) collective-permute-start(f32[104,128]{1,0:T(8,128)S(1)} %add_add_fusion.p0), channel_id=1, source_target_pairs={{0,3},{1,0},{2,1},{3,2},{4,7},{5,4},{6,5},{7,6},{8,11},{9,8},{10,9... | collective-permute-start | bytes 159752 | tf_op jit(solution)/shard_map/ppermute | solution.py:522
  85.4 0.0 collective-permute-done.11.p1
  85.4 1.5 %collective-permute-done.12.p2 = f32[104,128]{1,0:T(8,128)S(1)} collective-permute-done((f32[104,128]{1,0:T(8,128)S(1)}, f32[104,128]{1,0:T(8,128)S(1)}, u32[]{:S(2)}, u32[]{:S(2)}) %collective-permute-start.12) | collective-permute-done | bytes 53280 | tf_op jit(solution)/shard_map/ppermute | solution.py:522
  86.9 1.2 %collective-permute-done.13.p3 = f32[104,128]{1,0:T(8,128)S(1)} collective-permute-done((f32[104,128]{1,0:T(8,128)S(1)}, f32[104,128]{1,0:T(8,128)S(1)}, u32[]{:S(2)}, u32[]{:S(2)}) %collective-permute-start.13) | collective-permute-done | bytes 53280 | tf_op jit(solution)/shard_map/ppermute | solution.py:522
  88.1 0.0 copy-done.1
  88.1 0.0 copy-done.2
  88.1 0.0 copy-done.4
  88.1 0.0 copy-done.5
  88.1 0.8 finish.1
  (3 shorter events, 0.0 us)
Async XLA Ops:
  0.6 28.5 %copy-start = (bf16[2,32,32,512]{3,2,1,0:T(8,128)(2,1)S(1)}, bf16[2,32,32,512]{3,2,1,0:T(8,128)(2,1)}, u32[]{:S(2)}) copy-start(bf16[2,32,32,512]{3,2,1,0:T(8,128)(2,1)} %param.28) | copy-start | bytes 6291460
  0.7 28.5 %copy-start.3 = (bf16[256,32]{0,1:T(8,128)(2,1)S(1)}, bf16[256,32]{0,1:T(8,128)(2,1)}, u32[]{:S(2)}) copy-start(bf16[256,32]{0,1:T(8,128)(2,1)} %param.26) | copy-start | bytes 49156
  0.7 28.5 %copy-start.6 = (bf16[2,256,512]{2,1,0:T(8,128)(2,1)S(1)}, bf16[2,256,512]{2,1,0:T(8,128)(2,1)}, u32[]{:S(2)}) copy-start(bf16[2,256,512]{2,1,0:T(8,128)(2,1)} %gskip.1) | copy-start | bytes 1572868
  2.7 14.0 %collective-permute-start = (bf16[4,3,128,128]{3,2,1,0:T(8,128)(2,1)}, bf16[4,3,128,128]{3,2,1,0:T(8,128)(2,1)S(1)}, u32[]{:S(2)}, u32[]{:S(2)}) collective-permute-start(bf16[4,3,128,128]{3,2,1,0:T(8,128)(2,1)} %vo), channel_id=1, source_target_pairs={{0,4},{4,8},{8,12},{12,16},{16,20},{20,24},{24,28},{28,32},{32,36}... | collective-permute-start | bytes 1179656 | tf_op jit(solution)/shard_map/ppermute | solution.py:378
  4.0 12.7 %collective-permute-start.1 = (bf16[4,3,128,128]{3,2,1,0:T(8,128)(2,1)}, bf16[4,3,128,128]{3,2,1,0:T(8,128)(2,1)}, u32[]{:S(2)}, u32[]{:S(2)}) collective-permute-start(bf16[4,3,128,128]{3,2,1,0:T(8,128)(2,1)} %vo), channel_id=1, source_target_pairs={{4,0},{8,4},{12,8},{16,12},{20,16},{24,20},{28,24},{32,28},{36,32}... | collective-permute-start | bytes 1179656 | tf_op jit(solution)/shard_map/ppermute | solution.py:378
  5.3 21.3 %all-to-all-start = ((bf16[32,4,1536]{2,1,0:T(4,128)(2,1)}), bf16[32,4,1536]{2,1,0:T(4,128)(2,1)S(1)}, u32[]{:S(2)}, u32[]{:S(2)}) async-start(bf16[32,4,1536]{2,1,0:T(4,128)(2,1)} %message.1), calls=%async_computation | async-start | bytes 786432 | tf_op jit(solution)/shard_map/all_to_all | solution.py:509
  16.8 9.9 %copy-start.7 = (bf16[4,3,128,128]{3,2,1,0:T(8,128)(2,1)}, bf16[4,3,128,128]{3,2,1,0:T(8,128)(2,1)S(1)}, u32[]{:S(2)}) copy-start(bf16[4,3,128,128]{3,2,1,0:T(8,128)(2,1)S(1)} %collective-permute-done.vl) | copy-start | bytes 1179652
  16.8 25.9 %collective-permute-start.2 = (bf16[2048,512]{1,0:T(8,128)(2,1)}, bf16[2048,512]{1,0:T(8,128)(2,1)}, u32[]{:S(2)}, u32[]{:S(2)}) collective-permute-start(bf16[2048,512]{1,0:T(8,128)(2,1)} %bitcast.16), channel_id=1, source_target_pairs={{0,4},{4,8},{8,12},{12,16},{16,20},{20,24},{24,28},{28,32},{32,36}... | collective-permute-start | bytes 6291464 | tf_op jit(solution)/shard_map/ppermute | solution.py:378
  20.3 22.4 %collective-permute-start.3 = (bf16[2048,512]{1,0:T(8,128)(2,1)}, bf16[2048,512]{1,0:T(8,128)(2,1)}, u32[]{:S(2)}, u32[]{:S(2)}) collective-permute-start(bf16[2048,512]{1,0:T(8,128)(2,1)} %bitcast.17), channel_id=1, source_target_pairs={{4,0},{8,4},{12,8},{16,12},{20,16},{24,20},{28,24},{32,28},{36,32}... | collective-permute-start | bytes 6291464 | tf_op jit(solution)/shard_map/ppermute | solution.py:378
  42.7 45.4 %copy-start.1 = (bf16[2,32,32]{2,1,0:T(8,128)(2,1)S(1)}, bf16[2,32,32]{2,1,0:T(8,128)(2,1)}, u32[]{:S(2)}) copy-start(bf16[2,32,32]{2,1,0:T(8,128)(2,1)} %wf.3) | copy-start | bytes 12292
  42.7 45.4 %copy-start.2 = (bf16[2,32,32]{2,1,0:T(8,128)(2,1)S(1)}, bf16[2,32,32]{2,1,0:T(8,128)(2,1)}, u32[]{:S(2)}) copy-start(bf16[2,32,32]{2,1,0:T(8,128)(2,1)} %wg.3) | copy-start | bytes 12292
  42.7 45.4 %copy-start.4 = (f32[32]{0:T(128)S(1)}, f32[32]{0:T(128)}, u32[]{:S(2)}) copy-start(f32[32]{0:T(128)} %param.16) | copy-start | bytes 388
  42.7 45.4 %copy-start.5 = (f32[32]{0:T(128)S(1)}, f32[32]{0:T(128)}, u32[]{:S(2)}) copy-start(f32[32]{0:T(128)} %param.17) | copy-start | bytes 388
  54.3 6.7 %collective-permute-start.4 = (f32[104,128]{1,0:T(8,128)S(1)}, f32[104,128]{1,0:T(8,128)S(1)}, u32[]{:S(2)}, u32[]{:S(2)}) collective-permute-start(f32[104,128]{1,0:T(8,128)S(1)} %backward.1), channel_id=1, source_target_pairs={{0,4},{4,0},{8,12},{12,8},{16,20},{20,16},{24,28},{28,24},{32,36},... | collective-permute-start | bytes 159752 | tf_op jit(solution)/shard_map/ppermute | solution.py:382
  61.0 6.5 %collective-permute-start.7 = (f32[104,128]{1,0:T(8,128)S(1)}, f32[104,128]{1,0:T(8,128)S(1)}, u32[]{:S(2)}, u32[]{:S(2)}) collective-permute-start(f32[104,128]{1,0:T(8,128)S(1)} %add.21), channel_id=1, source_target_pairs={{0,24},{4,28},{8,0},{12,4},{16,8},{20,12},{24,16},{28,20},{32,56},... | collective-permute-start | bytes 159752 | tf_op jit(solution)/shard_map/ppermute | solution.py:382
  65.7 6.2 %collective-permute-start.5 = (f32[104,128]{1,0:T(8,128)S(1)}, f32[104,128]{1,0:T(8,128)S(1)}, u32[]{:S(2)}, u32[]{:S(2)}) collective-permute-start(f32[104,128]{1,0:T(8,128)S(1)} %add.21), channel_id=1, source_target_pairs={{0,8},{4,12},{8,16},{12,20},{16,24},{20,28},{24,0},{28,4},{32,40},... | collective-permute-start | bytes 159752 | tf_op jit(solution)/shard_map/ppermute | solution.py:382
  65.7 6.2 %collective-permute-start.6 = (f32[104,128]{1,0:T(8,128)S(1)}, f32[104,128]{1,0:T(8,128)S(1)}, u32[]{:S(2)}, u32[]{:S(2)}) collective-permute-start(f32[104,128]{1,0:T(8,128)S(1)} %add.21), channel_id=1, source_target_pairs={{0,16},{4,20},{8,24},{12,28},{16,0},{20,4},{24,8},{28,12},{32,48},... | collective-permute-start | bytes 159752 | tf_op jit(solution)/shard_map/ppermute | solution.py:382
  71.9 4.8 %collective-permute-start.10 = (f32[104,128]{1,0:T(8,128)S(1)}, f32[104,128]{1,0:T(8,128)S(1)}, u32[]{:S(2)}, u32[]{:S(2)}) collective-permute-start(f32[104,128]{1,0:T(8,128)S(1)} %add_add_fusion.1), channel_id=1, source_target_pairs={{0,96},{4,100},{8,104},{12,108},{16,112},{20,116},{24,120},{28,124... | collective-permute-start | bytes 159752 | tf_op jit(solution)/shard_map/ppermute | solution.py:382
  72.1 5.9 %collective-permute-start.8 = (f32[104,128]{1,0:T(8,128)S(1)}, f32[104,128]{1,0:T(8,128)S(1)}, u32[]{:S(2)}, u32[]{:S(2)}) collective-permute-start(f32[104,128]{1,0:T(8,128)S(1)} %add_add_fusion.1), channel_id=1, source_target_pairs={{0,32},{4,36},{8,40},{12,44},{16,48},{20,52},{24,56},{28,60},{32,6... | collective-permute-start | bytes 159752 | tf_op jit(solution)/shard_map/ppermute | solution.py:382
  74.0 5.6 %collective-permute-start.9 = (f32[104,128]{1,0:T(8,128)S(1)}, f32[104,128]{1,0:T(8,128)S(1)}, u32[]{:S(2)}, u32[]{:S(2)}) collective-permute-start(f32[104,128]{1,0:T(8,128)S(1)} %add_add_fusion.1), channel_id=1, source_target_pairs={{0,64},{4,68},{8,72},{12,76},{16,80},{20,84},{24,88},{28,92},{32,9... | collective-permute-start | bytes 159752 | tf_op jit(solution)/shard_map/ppermute | solution.py:382
  79.7 5.7 %collective-permute-start.11 = (f32[104,128]{1,0:T(8,128)S(1)}, f32[104,128]{1,0:T(8,128)S(1)}, u32[]{:S(2)}, u32[]{:S(2)}) collective-permute-start(f32[104,128]{1,0:T(8,128)S(1)} %add_add_fusion.p0), channel_id=1, source_target_pairs={{0,1},{1,2},{2,3},{3,0},{4,5},{5,6},{6,7},{7,4},{8,9},{9,10},{10,1... | collective-permute-start | bytes 159752 | tf_op jit(solution)/shard_map/ppermute | solution.py:522
  81.3 5.6 %collective-permute-start.12 = (f32[104,128]{1,0:T(8,128)S(1)}, f32[104,128]{1,0:T(8,128)S(1)}, u32[]{:S(2)}, u32[]{:S(2)}) collective-permute-start(f32[104,128]{1,0:T(8,128)S(1)} %add_add_fusion.p0), channel_id=1, source_target_pairs={{0,2},{1,3},{2,0},{3,1},{4,6},{5,7},{6,4},{7,5},{8,10},{9,11},{10,... | collective-permute-start | bytes 159752 | tf_op jit(solution)/shard_map/ppermute | solution.py:522
  84.0 4.1 %collective-permute-start.13 = (f32[104,128]{1,0:T(8,128)S(1)}, f32[104,128]{1,0:T(8,128)S(1)}, u32[]{:S(2)}, u32[]{:S(2)}) collective-permute-start(f32[104,128]{1,0:T(8,128)S(1)} %add_add_fusion.p0), channel_id=1, source_target_pairs={{0,3},{1,0},{2,1},{3,2},{4,7},{5,4},{6,5},{7,6},{8,11},{9,8},{10,9... | collective-permute-start | bytes 159752 | tf_op jit(solution)/shard_map/ppermute | solution.py:522

commit v5 on v4

--- a/solution.py
+++ b/solution.py
@@ -186,8 +186,8 @@
 
 
 def forward_kernel(
-    xs, coef, mix, bandt, wsk, bsk, wskt, grad, gskip,
-    res, skip, z, dfil, dgat, esum, dsk, extra, ahead, zext, one, stack,
+    xs, coef, mix, mixt, band, bandt, wsk, bsk, wskt, grad, gskip,
+    res, skip, z, dfil, dgat, e0, g1, esum, dsk, extra, dm0, ahead, zext, one, stack,
 ):
     i = pl.program_id(0)
 
@@ -217,6 +217,7 @@
     def _():
         esum[...] = jnp.zeros_like(esum)
         dsk[...] = jnp.zeros_like(dsk)
+        dm0[...] = jnp.zeros_like(dm0)
         for k in range(TG):
             for t in range(12):
                 look_ahead(i, k, t)()
@@ -238,6 +239,15 @@
     bb = bs + bm
     x1 = at(i)[1]
     go = grad.at[mine]
+    e0[mine, :] = dot(mixt[:, 0:ROWS], go[...])
+    for p, cols, rows in (
+        (0, slice(0, PAIR), slice(2 * PAIR, 3 * PAIR)),
+        (1, slice(0, W), slice(PAIR, 3 * PAIR)),
+        (2, slice(0, W), slice(0, 2 * PAIR)),
+        (3, slice(PAIR, W), slice(0, PAIR)),
+    ):
+        g1[mine, p * PAIR : (p + 1) * PAIR] = dot(go[:, cols], band[p, rows, :])
+    dm0[...] += dot_nt(go[...], stack[0:ROWS, :])
     se, sq = esum[0], esum[1]
     for k in range(TG):
         for t in range(TILES):
@@ -262,8 +272,8 @@
 
 
 def backward_kernel(
-    xs, mixt, band, gl, grad, gr, z, dfil, dgat, esum, dsk, extra,
-    pay, ext, one, stack, dzs, acc, dmx,
+    xs, mixt, band, gl, grad, gr, z, dfil, dgat, e0, g1, esum, dsk, extra, dm0,
+    pay, one, stack, dzs, acc, dmx,
 ):
     i = pl.program_id(0)
     mine = pl.ds(pl.multiple_of(i * ROWS, ROWS), ROWS)
@@ -277,17 +287,21 @@
         acc[...] = jnp.zeros_like(acc)
         dmx[...] = jnp.zeros_like(dmx)
 
-    ext[:, 0:W] = gl[...]
-    ext[:, W : 2 * W] = go[...]
-    ext[:, 2 * W : 3 * W] = gr[...]
-    stack[0:ROWS, :] = go[...]
-
-    def put(p, v):
-        stack[2 * ROWS : 3 * ROWS, p * PAIR : (p + 1) * PAIR] = v
-
-    hops(ext, one, band, put, lambda: None)
-    stack[ROWS : 2 * ROWS, :] = one[:, PAIR : PAIR + W]
-    dzs[...] = dot(mixt[...], stack[...])
+    for p, halo, cols, rows in (
+        (0, gl, slice(0, W), slice(0, 2 * PAIR)),
+        (1, gl, slice(PAIR, W), slice(0, PAIR)),
+        (2, gr, slice(0, PAIR), slice(2 * PAIR, 3 * PAIR)),
+        (3, gr, slice(0, W), slice(PAIR, 3 * PAIR)),
+    ):
+        at = slice(p * PAIR, (p + 1) * PAIR)
+        one[:, at] = (dot(halo[:, cols], band[p, rows, :]) + g1[mine, at]).astype(BF16)
+    for p in range(2):
+        at = slice(p * PAIR, (p + 1) * PAIR)
+        stack[ROWS : 2 * ROWS, at] = dot(
+            one[:, p * PAIR : (p + 3) * PAIR], band[p + 1]
+        ).astype(BF16)
+    stack[0:ROWS, :] = one[:, PAIR : PAIR + W]
+    dzs[...] = dot(mixt[:, ROWS:], stack[...]) + e0[mine, :]
     dzs[ROWS - C : ROWS, :] += extra[i // 4] * jnp.where(i % 4 == 3, 1.0, 0.0)
 
     sums = [acc[j] for j in range(6)]
@@ -305,8 +319,8 @@
 
         return emit
 
-    emit = spread([local(k, t) for k in range(TG) for t in range(TILES)], 3)
-    for h in range(3):
+    emit = spread([local(k, t) for k in range(TG) for t in range(TILES)], 2)
+    for h in range(2):
         part = slice(h * ROWS, (h + 1) * ROWS)
         dmx[part, :] += dot_nt(stack[part, :], zb[...])
         emit()
@@ -320,7 +334,8 @@
         lane = lax.broadcasted_iota(jnp.int32, (C, TILE), 1)
         packed = jnp.zeros((C, TILE), F32)
         for h in range(3):
-            m = jnp.where(r == c, dmx[h * ROWS : (h + 1) * ROWS, :], 0.0)
+            m = dm0[...] if h == 0 else dmx[(h - 1) * ROWS : h * ROWS, :]
+            m = jnp.where(r == c, m, 0.0)
             v = m[0:C]
             for k in range(1, TG):
                 v = v + m[k * C : (k + 1) * C]
@@ -395,7 +410,7 @@
 HBM = pl.BlockSpec(memory_space=pltpu.HBM)
 
 
-def forward_call(xs, coef, mix, bandt, wsk, bsk, wskt, grad, gskip):
+def forward_call(xs, coef, mix, mixt, band, bandt, wsk, bsk, wskt, grad, gskip):
     rows = BR * TOUT * C
     return pl.pallas_call(
         forward_kernel,
@@ -406,16 +421,19 @@
             jax.ShapeDtypeStruct((rows, W), BF16),
             jax.ShapeDtypeStruct((rows, W), BF16),
             jax.ShapeDtypeStruct((rows, W), BF16),
+            jax.ShapeDtypeStruct((rows, W), F32),
+            jax.ShapeDtypeStruct((rows, 2 * W), F32),
             jax.ShapeDtypeStruct((2, C, TILE), F32),
             jax.ShapeDtypeStruct((C + 16, SKIP), F32),
             jax.ShapeDtypeStruct((BR, C, W), F32),
+            jax.ShapeDtypeStruct((ROWS, ROWS), F32),
         ),
-        in_specs=[VMEM] * 9,
+        in_specs=[VMEM] * 11,
         out_specs=(
             pl.BlockSpec((ROWS, W), lambda i: (i, 0)),
             pl.BlockSpec((1, SKIP, W), lambda i: (i // 4, 0, 0)),
         )
-        + (VMEM,) * 6,
+        + (VMEM,) * 9,
         scratch_shapes=[
             pltpu.VMEM((ROWS, 3 * W), BF16),
             pltpu.VMEM((ROWS, 3 * W), BF16),
@@ -427,7 +445,7 @@
             flops=20_000_000_000, bytes_accessed=16_000_000, transcendentals=6_000_000
         ),
         name="forward",
-    )(xs, coef, mix, bandt, wsk, bsk, wskt, grad, gskip)
+    )(xs, coef, mix, mixt, band, bandt, wsk, bsk, wskt, grad, gskip)
 
 
 def backward_call(xs, mixt, band, gl, go, gr, *early):
@@ -436,15 +454,14 @@
         backward_kernel,
         grid=(8,),
         out_shape=jax.ShapeDtypeStruct((PAY, TILE), F32),
-        in_specs=[VMEM] * 3 + [slab, VMEM, slab] + [VMEM] * 6,
+        in_specs=[VMEM] * 3 + [slab, VMEM, slab] + [VMEM] * 9,
         out_specs=VMEM,
         scratch_shapes=[
-            pltpu.VMEM((ROWS, 3 * W), BF16),
             pltpu.VMEM((ROWS, 2 * W), BF16),
-            pltpu.VMEM((3 * ROWS, W), BF16),
+            pltpu.VMEM((2 * ROWS, W), BF16),
             pltpu.VMEM((ROWS, W), F32),
             pltpu.VMEM((6, C, TILE), F32),
-            pltpu.VMEM((3 * ROWS, ROWS), F32),
+            pltpu.VMEM((2 * ROWS, ROWS), F32),
         ],
         compiler_params=params(),
         name="backward",
@@ -513,7 +530,9 @@
     coef, mix, mixt, wsk, bsk, band, bandt, xs = prepare(
         msg, vals, w_start, b_start, w_filter, b_filter, w_gate, b_gate, w_mix, b_mix, w_skip, b_skip
     )
-    res, skip, *early = forward_call(xs, coef, mix, bandt, wsk, bsk, w_skip.T, grad, grad_skip)
+    res, skip, *early = forward_call(
+        xs, coef, mix, mixt, band, bandt, wsk, bsk, w_skip.T, grad, grad_skip
+    )
     v = backward_call(xs, mixt, band, grad_l, grad, grad_r, *early)
 
     v = v + seg_ring(v, lambda i: i ^ 1)

time: 89.3 us -> 87.5 us (0.980)
  starting transfers between devices: 41.3 us -> 38.7 us
    pallas_call x1, Pallas kernels: 13.5 us -> 16.1 us  [forward_call(): pl.pallas_call(forward_kernel, grid=(8,), out_shape=(jax.ShapeDtypeStruct...]
    ppermute x7, starting transfers between devices: 16.8 us -> 14.2 us  [seg_ring(): lax.ppermute(value, 'seg', [(i, shift(i)) for i in range(lax.axis_size('s...]
    pallas_call x1, Pallas kernels: 11.6 us -> 9.71 us  [backward_call(): pl.pallas_call(backward_kernel, grid=(8,), out_shape=jax.ShapeDtypeStruct...]
  transfers between devices with their start and end apart: 15 -> 15, of which waited for: 8 -> 8; matrix products, arithmetic and copies ran while one was open for 0% -> 0% of each run, Pallas kernels for 18% -> 21%
where the time goes in v5:
time: 87.5 us; the launch traced here: 87.1 us
  starting transfers between devices  38.7 us (44%)
  Pallas kernels  31.1 us (36%)
  waiting for transfers between devices  16.3 us (19%)
    pallas_call x1, Pallas kernels, forward_call(): pl.pallas_call(forward_kernel, grid=(8,), out_shape=(jax.ShapeDtypeStruct...  16.1 us
    ppermute x7, starting transfers between devices, seg_ring(): lax.ppermute(value, 'seg', [(i, shift(i)) for i in range(lax.axis_size('s...  14.2 us
    all_to_all x1, starting transfers between devices, body(): msg = lax.all_to_all(msg, 'seg', split_axis=0, concat_axis=0, tiled=True)  11.4 us
    pallas_call x1, Pallas kernels, backward_call(): pl.pallas_call(backward_kernel, grid=(8,), out_shape=jax.ShapeDtypeStruct...  9.71 us
    ppermute x7, waiting for transfers between devices, seg_ring(): lax.ppermute(value, 'seg', [(i, shift(i)) for i in range(lax.axis_size('s...  8.5 us
    ppermute x4, starting transfers between devices, neighbour(): return lax.ppermute(value, 'seg', pairs)  7.41 us
    ppermute x3, starting transfers between devices, body(): lax.ppermute(v, 'rep', [(i, (i + k) % 4) for i in range(4)])  5.72 us
    all_to_all x1, waiting for transfers between devices, body(): msg = lax.all_to_all(msg, 'seg', split_axis=0, concat_axis=0, tiled=True)  5.11 us
  transfers between devices with their start and end apart: 15, of which 8 were waited for; matrix products, arithmetic and copies ran while one was open for 0% of the time, Pallas kernels for 21%

profile of v5, /device:TPU:0, one launch (start us, length us, event | category | flops | bytes accessed | tf_op | source)
XLA Modules:
  0.0 87.1 jit_solution(5266203604012915871)
XLA Ops:
  0.6 0.0 copy-start
  0.7 0.0 copy-start.3
  0.7 0.0 copy-start.6
  0.7 2.0 %message.1 = bf16[32,4,1536]{2,1,0:T(4,128)(2,1)} custom-call(s32[4,3]{1,0:T(4,128)} %cols_hbm.1, f32[3,16384]{1,0:T(4,128)} %speeds.1), custom_call_target="tpu_custom_call" | custom-call | tf_op jit(solution)/shard_map/message/pallas_call | solution.py:476
  2.7 1.3 %collective-permute-start = (bf16[4,3,128,128]{3,2,1,0:T(8,128)(2,1)}, bf16[4,3,128,128]{3,2,1,0:T(8,128)(2,1)S(1)}, u32[]{:S(2)}, u32[]{:S(2)}) collective-permute-start(bf16[4,3,128,128]{3,2,1,0:T(8,128)(2,1)} %vo), channel_id=1, source_target_pairs={{0,4},{4,8},{8,12},{12,16},{16,20},{20,24},{24,28},{28,32},{32,36}... | collective-permute-start | bytes 1179656 | tf_op jit(solution)/shard_map/ppermute | solution.py:393
  4.0 1.3 %collective-permute-start.1 = (bf16[4,3,128,128]{3,2,1,0:T(8,128)(2,1)}, bf16[4,3,128,128]{3,2,1,0:T(8,128)(2,1)}, u32[]{:S(2)}, u32[]{:S(2)}) collective-permute-start(bf16[4,3,128,128]{3,2,1,0:T(8,128)(2,1)} %vo), channel_id=1, source_target_pairs={{4,0},{8,4},{12,8},{16,12},{20,16},{24,20},{28,24},{32,28},{36,32}... | collective-permute-start | bytes 1179656 | tf_op jit(solution)/shard_map/ppermute | solution.py:393
  5.3 11.4 %all-to-all-start = ((bf16[32,4,1536]{2,1,0:T(4,128)(2,1)}), bf16[32,4,1536]{2,1,0:T(4,128)(2,1)S(1)}, u32[]{:S(2)}, u32[]{:S(2)}) async-start(bf16[32,4,1536]{2,1,0:T(4,128)(2,1)} %message.1), calls=%async_computation | async-start | bytes 786432 | tf_op jit(solution)/shard_map/all_to_all | solution.py:526
  16.7 0.0 collective-permute-done.vl
  16.8 0.0 copy-start.7
  16.8 0.0 collective-permute-done.1.vr
  16.8 3.5 %collective-permute-start.2 = (bf16[2048,512]{1,0:T(8,128)(2,1)}, bf16[2048,512]{1,0:T(8,128)(2,1)}, u32[]{:S(2)}, u32[]{:S(2)}) collective-permute-start(bf16[2048,512]{1,0:T(8,128)(2,1)} %bitcast.16), channel_id=1, source_target_pairs={{0,4},{4,8},{8,12},{12,16},{16,20},{20,24},{24,28},{28,32},{32,36}... | collective-permute-start | bytes 6291464 | tf_op jit(solution)/shard_map/ppermute | solution.py:393
  20.3 1.3 %collective-permute-start.3 = (bf16[2048,512]{1,0:T(8,128)(2,1)}, bf16[2048,512]{1,0:T(8,128)(2,1)}, u32[]{:S(2)}, u32[]{:S(2)}) collective-permute-start(bf16[2048,512]{1,0:T(8,128)(2,1)} %bitcast.17), channel_id=1, source_target_pairs={{4,0},{8,4},{12,8},{16,12},{20,16},{24,20},{28,24},{32,28},{36,32}... | collective-permute-start | bytes 6291464 | tf_op jit(solution)/shard_map/ppermute | solution.py:393
  21.6 5.1 %all-to-all-done.msg = bf16[32,4,1536]{2,1,0:T(4,128)(2,1)S(1)} async-done(((bf16[32,4,1536]{2,1,0:T(4,128)(2,1)}), bf16[32,4,1536]{2,1,0:T(4,128)(2,1)S(1)}, u32[]{:S(2)}, u32[]{:S(2)}) %all-to-all-start) | async-done | bytes 393248 | tf_op jit(solution)/shard_map/all_to_all | solution.py:526
  26.7 0.0 copy-done.7
  26.7 2.4 %prep.1 = (f32[288,128]{1,0:T(8,128)S(1)}, bf16[256,768]{1,0:T(8,128)(2,1)S(1)}, bf16[256,768]{1,0:T(8,128)(2,1)S(1)}, bf16[256,32]{1,0:T(8,128)(2,1)S(1)}, f32[...) custom-call(f32[1,32]{1,0:T(1,128)} %bitcast.22, ...), custom_call_target="tpu_custom_call" | custom-call | tf_op jit(solution)/shard_map/prep/pallas_call | solution.py:498
  29.1 0.0 copy-done
  29.1 0.0 copy-done.3
  29.2 0.0 copy-done.6
  29.2 16.1 %forward.1 = (bf16[2048,512]{1,0:T(8,128)(2,1)}, bf16[2,256,512]{2,1,0:T(8,128)(2,1)}, bf16[2048,512]{1,0:T(8,128)(2,1)S(1)}, bf16[2048,512]{1,0:T(8,128)(2,1)S(...) custom-call(f32[96,1536]{1,0:T(8,128)S(1)} %get-tuple-element.52.xs,, ...), custom_call_target="tpu_custom_call" | custom-call | flops 20000000000 | bytes 16000000 | tf_op jit(solution)/shard_map/forward/pallas_call | solution.py:415
  45.3 0.0 collective-permute-done.2.gl
  45.3 0.0 collective-permute-done.3.gr
  45.3 0.0 copy-start.1
  45.3 0.0 copy-start.2
  45.3 0.0 copy-start.4
  45.3 0.0 copy-start.5
  45.3 9.7 %backward.1 = f32[104,128]{1,0:T(8,128)S(1)} custom-call(f32[96,1536]{1,0:T(8,128)S(1)} %get-tuple-element.52.xs, bf16[256,768]{1,0:T(8,128)(2,1)S(1)} %get-tuple-element.55.mixt, bf16[4,768,256]{2,1,0:T(8,128)(2,1)S(1)} %get-tuple-element.56.band, bf16[2048,512]{1,0:T(8,128)(2,1)} %collective-permute-done.2.gl, bf16[2048,512]{1,0:T(8,128)(2,1)S(1)} %bitcast.19, ...), custom_call_target="tpu_custom_call" | custom-call | tf_op jit(solution)/shard_map/backward/pallas_call | solution.py:453
  55.1 3.2 %collective-permute-start.4 = (f32[104,128]{1,0:T(8,128)S(1)}, f32[104,128]{1,0:T(8,128)S(1)}, u32[]{:S(2)}, u32[]{:S(2)}) collective-permute-start(f32[104,128]{1,0:T(8,128)S(1)} %backward.1), channel_id=1, source_target_pairs={{0,4},{4,0},{8,12},{12,8},{16,20},{20,16},{24,28},{28,24},{32,36},... | collective-permute-start | bytes 159752 | tf_op jit(solution)/shard_map/ppermute | solution.py:397
  58.3 0.9 %collective-permute-done.4 = f32[104,128]{1,0:T(8,128)S(1)} collective-permute-done((f32[104,128]{1,0:T(8,128)S(1)}, f32[104,128]{1,0:T(8,128)S(1)}, u32[]{:S(2)}, u32[]{:S(2)}) %collective-permute-start.4) | collective-permute-done | bytes 53280 | tf_op jit(solution)/shard_map/ppermute | solution.py:397
  59.1 4.7 %collective-permute-start.7 = (f32[104,128]{1,0:T(8,128)S(1)}, f32[104,128]{1,0:T(8,128)S(1)}, u32[]{:S(2)}, u32[]{:S(2)}) collective-permute-start(f32[104,128]{1,0:T(8,128)S(1)} %add.21), channel_id=1, source_target_pairs={{0,24},{4,28},{8,0},{12,4},{16,8},{20,12},{24,16},{28,20},{32,56},... | collective-permute-start | bytes 159752 | tf_op jit(solution)/shard_map/ppermute | solution.py:397
  63.8 0.0 collective-permute-start.5
  63.8 1.5 %collective-permute-start.6 = (f32[104,128]{1,0:T(8,128)S(1)}, f32[104,128]{1,0:T(8,128)S(1)}, u32[]{:S(2)}, u32[]{:S(2)}) collective-permute-start(f32[104,128]{1,0:T(8,128)S(1)} %add.21), channel_id=1, source_target_pairs={{0,16},{4,20},{8,24},{12,28},{16,0},{20,4},{24,8},{28,12},{32,48},... | collective-permute-start | bytes 159752 | tf_op jit(solution)/shard_map/ppermute | solution.py:397
  65.4 0.2 collective-permute-done.7
  65.6 4.4 %collective-permute-done.5 = f32[104,128]{1,0:T(8,128)S(1)} collective-permute-done((f32[104,128]{1,0:T(8,128)S(1)}, f32[104,128]{1,0:T(8,128)S(1)}, u32[]{:S(2)}, u32[]{:S(2)}) %collective-permute-start.5) | collective-permute-done | bytes 53280 | tf_op jit(solution)/shard_map/ppermute | solution.py:397
  70.1 0.0 collective-permute-done.6
  70.1 0.2 collective-permute-start.10
  70.3 1.9 %collective-permute-start.8 = (f32[104,128]{1,0:T(8,128)S(1)}, f32[104,128]{1,0:T(8,128)S(1)}, u32[]{:S(2)}, u32[]{:S(2)}) collective-permute-start(f32[104,128]{1,0:T(8,128)S(1)} %add_add_fusion.1), channel_id=1, source_target_pairs={{0,32},{4,36},{8,40},{12,44},{16,48},{20,52},{24,56},{28,60},{32,6... | collective-permute-start | bytes 159752 | tf_op jit(solution)/shard_map/ppermute | solution.py:397
  72.2 2.7 %collective-permute-start.9 = (f32[104,128]{1,0:T(8,128)S(1)}, f32[104,128]{1,0:T(8,128)S(1)}, u32[]{:S(2)}, u32[]{:S(2)}) collective-permute-start(f32[104,128]{1,0:T(8,128)S(1)} %add_add_fusion.1), channel_id=1, source_target_pairs={{0,64},{4,68},{8,72},{12,76},{16,80},{20,84},{24,88},{28,92},{32,9... | collective-permute-start | bytes 159752 | tf_op jit(solution)/shard_map/ppermute | solution.py:397
  74.9 0.0 collective-permute-done.10
  74.9 1.3 %collective-permute-done.8 = f32[104,128]{1,0:T(8,128)S(1)} collective-permute-done((f32[104,128]{1,0:T(8,128)S(1)}, f32[104,128]{1,0:T(8,128)S(1)}, u32[]{:S(2)}, u32[]{:S(2)}) %collective-permute-start.8) | collective-permute-done | bytes 53280 | tf_op jit(solution)/shard_map/ppermute | solution.py:397
  76.2 1.6 %collective-permute-done.9 = f32[104,128]{1,0:T(8,128)S(1)} collective-permute-done((f32[104,128]{1,0:T(8,128)S(1)}, f32[104,128]{1,0:T(8,128)S(1)}, u32[]{:S(2)}, u32[]{:S(2)}) %collective-permute-start.9) | collective-permute-done | bytes 53280 | tf_op jit(solution)/shard_map/ppermute | solution.py:397
  77.8 1.6 %collective-permute-start.11 = (f32[104,128]{1,0:T(8,128)S(1)}, f32[104,128]{1,0:T(8,128)S(1)}, u32[]{:S(2)}, u32[]{:S(2)}) collective-permute-start(f32[104,128]{1,0:T(8,128)S(1)} %add_add_fusion.p0), channel_id=1, source_target_pairs={{0,1},{1,2},{2,3},{3,0},{4,5},{5,6},{6,7},{7,4},{8,9},{9,10},{10,1... | collective-permute-start | bytes 159752 | tf_op jit(solution)/shard_map/ppermute | solution.py:541
  79.4 2.7 %collective-permute-start.12 = (f32[104,128]{1,0:T(8,128)S(1)}, f32[104,128]{1,0:T(8,128)S(1)}, u32[]{:S(2)}, u32[]{:S(2)}) collective-permute-start(f32[104,128]{1,0:T(8,128)S(1)} %add_add_fusion.p0), channel_id=1, source_target_pairs={{0,2},{1,3},{2,0},{3,1},{4,6},{5,7},{6,4},{7,5},{8,10},{9,11},{10,... | collective-permute-start | bytes 159752 | tf_op jit(solution)/shard_map/ppermute | solution.py:541
  82.1 1.4 %collective-permute-start.13 = (f32[104,128]{1,0:T(8,128)S(1)}, f32[104,128]{1,0:T(8,128)S(1)}, u32[]{:S(2)}, u32[]{:S(2)}) collective-permute-start(f32[104,128]{1,0:T(8,128)S(1)} %add_add_fusion.p0), channel_id=1, source_target_pairs={{0,3},{1,0},{2,1},{3,2},{4,7},{5,4},{6,5},{7,6},{8,11},{9,8},{10,9... | collective-permute-start | bytes 159752 | tf_op jit(solution)/shard_map/ppermute | solution.py:541
  83.6 0.0 collective-permute-done.11.p1
  83.6 1.5 %collective-permute-done.12.p2 = f32[104,128]{1,0:T(8,128)S(1)} collective-permute-done((f32[104,128]{1,0:T(8,128)S(1)}, f32[104,128]{1,0:T(8,128)S(1)}, u32[]{:S(2)}, u32[]{:S(2)}) %collective-permute-start.12) | collective-permute-done | bytes 53280 | tf_op jit(solution)/shard_map/ppermute | solution.py:541
  85.0 1.2 %collective-permute-done.13.p3 = f32[104,128]{1,0:T(8,128)S(1)} collective-permute-done((f32[104,128]{1,0:T(8,128)S(1)}, f32[104,128]{1,0:T(8,128)S(1)}, u32[]{:S(2)}, u32[]{:S(2)}) %collective-permute-start.13) | collective-permute-done | bytes 53280 | tf_op jit(solution)/shard_map/ppermute | solution.py:541
  86.3 0.0 copy-done.1
  86.3 0.0 copy-done.2
  86.3 0.0 copy-done.4
  86.3 0.0 copy-done.5
  86.3 0.8 finish.1
  (3 shorter events, 0.0 us)
Async XLA Ops:
  0.6 28.5 %copy-start = (bf16[2,32,32,512]{3,2,1,0:T(8,128)(2,1)S(1)}, bf16[2,32,32,512]{3,2,1,0:T(8,128)(2,1)}, u32[]{:S(2)}) copy-start(bf16[2,32,32,512]{3,2,1,0:T(8,128)(2,1)} %param.28) | copy-start | bytes 6291460
  0.7 28.5 %copy-start.3 = (bf16[256,32]{0,1:T(8,128)(2,1)S(1)}, bf16[256,32]{0,1:T(8,128)(2,1)}, u32[]{:S(2)}) copy-start(bf16[256,32]{0,1:T(8,128)(2,1)} %param.26) | copy-start | bytes 49156
  0.7 28.5 %copy-start.6 = (bf16[2,256,512]{2,1,0:T(8,128)(2,1)S(1)}, bf16[2,256,512]{2,1,0:T(8,128)(2,1)}, u32[]{:S(2)}) copy-start(bf16[2,256,512]{2,1,0:T(8,128)(2,1)} %gskip.1) | copy-start | bytes 1572868
  2.7 14.0 %collective-permute-start = (bf16[4,3,128,128]{3,2,1,0:T(8,128)(2,1)}, bf16[4,3,128,128]{3,2,1,0:T(8,128)(2,1)S(1)}, u32[]{:S(2)}, u32[]{:S(2)}) collective-permute-start(bf16[4,3,128,128]{3,2,1,0:T(8,128)(2,1)} %vo), channel_id=1, source_target_pairs={{0,4},{4,8},{8,12},{12,16},{16,20},{20,24},{24,28},{28,32},{32,36}... | collective-permute-start | bytes 1179656 | tf_op jit(solution)/shard_map/ppermute | solution.py:393
  4.0 12.7 %collective-permute-start.1 = (bf16[4,3,128,128]{3,2,1,0:T(8,128)(2,1)}, bf16[4,3,128,128]{3,2,1,0:T(8,128)(2,1)}, u32[]{:S(2)}, u32[]{:S(2)}) collective-permute-start(bf16[4,3,128,128]{3,2,1,0:T(8,128)(2,1)} %vo), channel_id=1, source_target_pairs={{4,0},{8,4},{12,8},{16,12},{20,16},{24,20},{28,24},{32,28},{36,32}... | collective-permute-start | bytes 1179656 | tf_op jit(solution)/shard_map/ppermute | solution.py:393
  5.3 21.3 %all-to-all-start = ((bf16[32,4,1536]{2,1,0:T(4,128)(2,1)}), bf16[32,4,1536]{2,1,0:T(4,128)(2,1)S(1)}, u32[]{:S(2)}, u32[]{:S(2)}) async-start(bf16[32,4,1536]{2,1,0:T(4,128)(2,1)} %message.1), calls=%async_computation | async-start | bytes 786432 | tf_op jit(solution)/shard_map/all_to_all | solution.py:526
  16.8 9.9 %copy-start.7 = (bf16[4,3,128,128]{3,2,1,0:T(8,128)(2,1)}, bf16[4,3,128,128]{3,2,1,0:T(8,128)(2,1)S(1)}, u32[]{:S(2)}) copy-start(bf16[4,3,128,128]{3,2,1,0:T(8,128)(2,1)S(1)} %collective-permute-done.vl) | copy-start | bytes 1179652
  16.8 28.5 %collective-permute-start.2 = (bf16[2048,512]{1,0:T(8,128)(2,1)}, bf16[2048,512]{1,0:T(8,128)(2,1)}, u32[]{:S(2)}, u32[]{:S(2)}) collective-permute-start(bf16[2048,512]{1,0:T(8,128)(2,1)} %bitcast.16), channel_id=1, source_target_pairs={{0,4},{4,8},{8,12},{12,16},{16,20},{20,24},{24,28},{28,32},{32,36}... | collective-permute-start | bytes 6291464 | tf_op jit(solution)/shard_map/ppermute | solution.py:393
  20.3 25.0 %collective-permute-start.3 = (bf16[2048,512]{1,0:T(8,128)(2,1)}, bf16[2048,512]{1,0:T(8,128)(2,1)}, u32[]{:S(2)}, u32[]{:S(2)}) collective-permute-start(bf16[2048,512]{1,0:T(8,128)(2,1)} %bitcast.17), channel_id=1, source_target_pairs={{4,0},{8,4},{12,8},{16,12},{20,16},{24,20},{28,24},{32,28},{36,32}... | collective-permute-start | bytes 6291464 | tf_op jit(solution)/shard_map/ppermute | solution.py:393
  45.3 41.0 %copy-start.1 = (bf16[2,32,32]{2,1,0:T(8,128)(2,1)S(1)}, bf16[2,32,32]{2,1,0:T(8,128)(2,1)}, u32[]{:S(2)}) copy-start(bf16[2,32,32]{2,1,0:T(8,128)(2,1)} %wf.3) | copy-start | bytes 12292
  45.3 41.0 %copy-start.2 = (bf16[2,32,32]{2,1,0:T(8,128)(2,1)S(1)}, bf16[2,32,32]{2,1,0:T(8,128)(2,1)}, u32[]{:S(2)}) copy-start(bf16[2,32,32]{2,1,0:T(8,128)(2,1)} %wg.3) | copy-start | bytes 12292
  45.3 41.0 %copy-start.4 = (f32[32]{0:T(128)S(1)}, f32[32]{0:T(128)}, u32[]{:S(2)}) copy-start(f32[32]{0:T(128)} %param.16) | copy-start | bytes 388
  45.3 41.0 %copy-start.5 = (f32[32]{0:T(128)S(1)}, f32[32]{0:T(128)}, u32[]{:S(2)}) copy-start(f32[32]{0:T(128)} %param.17) | copy-start | bytes 388
  55.1 4.1 %collective-permute-start.4 = (f32[104,128]{1,0:T(8,128)S(1)}, f32[104,128]{1,0:T(8,128)S(1)}, u32[]{:S(2)}, u32[]{:S(2)}) collective-permute-start(f32[104,128]{1,0:T(8,128)S(1)} %backward.1), channel_id=1, source_target_pairs={{0,4},{4,0},{8,12},{12,8},{16,20},{20,16},{24,28},{28,24},{32,36},... | collective-permute-start | bytes 159752 | tf_op jit(solution)/shard_map/ppermute | solution.py:397
  59.1 6.5 %collective-permute-start.7 = (f32[104,128]{1,0:T(8,128)S(1)}, f32[104,128]{1,0:T(8,128)S(1)}, u32[]{:S(2)}, u32[]{:S(2)}) collective-permute-start(f32[104,128]{1,0:T(8,128)S(1)} %add.21), channel_id=1, source_target_pairs={{0,24},{4,28},{8,0},{12,4},{16,8},{20,12},{24,16},{28,20},{32,56},... | collective-permute-start | bytes 159752 | tf_op jit(solution)/shard_map/ppermute | solution.py:397
  63.8 6.2 %collective-permute-start.5 = (f32[104,128]{1,0:T(8,128)S(1)}, f32[104,128]{1,0:T(8,128)S(1)}, u32[]{:S(2)}, u32[]{:S(2)}) collective-permute-start(f32[104,128]{1,0:T(8,128)S(1)} %add.21), channel_id=1, source_target_pairs={{0,8},{4,12},{8,16},{12,20},{16,24},{20,28},{24,0},{28,4},{32,40},... | collective-permute-start | bytes 159752 | tf_op jit(solution)/shard_map/ppermute | solution.py:397
  63.8 6.2 %collective-permute-start.6 = (f32[104,128]{1,0:T(8,128)S(1)}, f32[104,128]{1,0:T(8,128)S(1)}, u32[]{:S(2)}, u32[]{:S(2)}) collective-permute-start(f32[104,128]{1,0:T(8,128)S(1)} %add.21), channel_id=1, source_target_pairs={{0,16},{4,20},{8,24},{12,28},{16,0},{20,4},{24,8},{28,12},{32,48},... | collective-permute-start | bytes 159752 | tf_op jit(solution)/shard_map/ppermute | solution.py:397
  70.1 4.8 %collective-permute-start.10 = (f32[104,128]{1,0:T(8,128)S(1)}, f32[104,128]{1,0:T(8,128)S(1)}, u32[]{:S(2)}, u32[]{:S(2)}) collective-permute-start(f32[104,128]{1,0:T(8,128)S(1)} %add_add_fusion.1), channel_id=1, source_target_pairs={{0,96},{4,100},{8,104},{12,108},{16,112},{20,116},{24,120},{28,124... | collective-permute-start | bytes 159752 | tf_op jit(solution)/shard_map/ppermute | solution.py:397
  70.3 5.9 %collective-permute-start.8 = (f32[104,128]{1,0:T(8,128)S(1)}, f32[104,128]{1,0:T(8,128)S(1)}, u32[]{:S(2)}, u32[]{:S(2)}) collective-permute-start(f32[104,128]{1,0:T(8,128)S(1)} %add_add_fusion.1), channel_id=1, source_target_pairs={{0,32},{4,36},{8,40},{12,44},{16,48},{20,52},{24,56},{28,60},{32,6... | collective-permute-start | bytes 159752 | tf_op jit(solution)/shard_map/ppermute | solution.py:397
  72.2 5.6 %collective-permute-start.9 = (f32[104,128]{1,0:T(8,128)S(1)}, f32[104,128]{1,0:T(8,128)S(1)}, u32[]{:S(2)}, u32[]{:S(2)}) collective-permute-start(f32[104,128]{1,0:T(8,128)S(1)} %add_add_fusion.1), channel_id=1, source_target_pairs={{0,64},{4,68},{8,72},{12,76},{16,80},{20,84},{24,88},{28,92},{32,9... | collective-permute-start | bytes 159752 | tf_op jit(solution)/shard_map/ppermute | solution.py:397
  77.8 5.7 %collective-permute-start.11 = (f32[104,128]{1,0:T(8,128)S(1)}, f32[104,128]{1,0:T(8,128)S(1)}, u32[]{:S(2)}, u32[]{:S(2)}) collective-permute-start(f32[104,128]{1,0:T(8,128)S(1)} %add_add_fusion.p0), channel_id=1, source_target_pairs={{0,1},{1,2},{2,3},{3,0},{4,5},{5,6},{6,7},{7,4},{8,9},{9,10},{10,1... | collective-permute-start | bytes 159752 | tf_op jit(solution)/shard_map/ppermute | solution.py:541
  79.4 5.6 %collective-permute-start.12 = (f32[104,128]{1,0:T(8,128)S(1)}, f32[104,128]{1,0:T(8,128)S(1)}, u32[]{:S(2)}, u32[]{:S(2)}) collective-permute-start(f32[104,128]{1,0:T(8,128)S(1)} %add_add_fusion.p0), channel_id=1, source_target_pairs={{0,2},{1,3},{2,0},{3,1},{4,6},{5,7},{6,4},{7,5},{8,10},{9,11},{10,... | collective-permute-start | bytes 159752 | tf_op jit(solution)/shard_map/ppermute | solution.py:541
  82.1 4.1 %collective-permute-start.13 = (f32[104,128]{1,0:T(8,128)S(1)}, f32[104,128]{1,0:T(8,128)S(1)}, u32[]{:S(2)}, u32[]{:S(2)}) collective-permute-start(f32[104,128]{1,0:T(8,128)S(1)} %add_add_fusion.p0), channel_id=1, source_target_pairs={{0,3},{1,0},{2,1},{3,2},{4,7},{5,4},{6,5},{7,6},{8,11},{9,8},{10,9... | collective-permute-start | bytes 159752 | tf_op jit(solution)/shard_map/ppermute | solution.py:541

commit v6 on v5

--- a/solution.py
+++ b/solution.py
@@ -536,9 +536,9 @@
     v = backward_call(xs, mixt, band, grad_l, grad, grad_r, *early)
 
     v = v + seg_ring(v, lambda i: i ^ 1)
-    v = v + sum(seg_ring(v, lambda i, k=k: (i // 8) * 8 + ((i // 2 + k) % 4) * 2 + i % 2) for k in (1, 2, 3))
-    v = v + sum(seg_ring(v, lambda i, k=k: (i + 8 * k) % 32) for k in (1, 2, 3))
-    others = [lax.ppermute(v, "rep", [(i, (i + k) % 4) for i in range(4)]) for k in (1, 2, 3)]
+    v = v + sum(seg_ring(v, lambda i, k=k: (i // 8) * 8 + ((i // 2 + k) % 4) * 2 + i % 2) for k in (1, 3, 2))
+    v = v + sum(seg_ring(v, lambda i, k=k: (i + 8 * k) % 32) for k in (1, 3, 2))
+    others = [lax.ppermute(v, "rep", [(i, (i + k) % 4) for i in range(4)]) for k in (1, 3, 2)]
 
     row = jax.ShapeDtypeStruct((1, C), F32)
     taps = jax.ShapeDtypeStruct((2, C, C), F32)

time: 87.5 us -> 87.3 us (level)
    ppermute x7, waiting for transfers between devices: 8.5 us -> 6.82 us  [seg_ring(): lax.ppermute(value, 'seg', [(i, shift(i)) for i in range(lax.axis_size('s...]
    ppermute x3, waiting for transfers between devices: 2.7 us -> 3.83 us  [body(): lax.ppermute(v, 'rep', [(i, (i + k) % 4) for i in range(4)])]
  transfers between devices with their start and end apart: 15 -> 15, of which waited for: 8 -> 7; matrix products, arithmetic and copies ran while one was open for 0% -> 0% of each run, Pallas kernels for 21% -> 21%
where the time goes in v6:
time: 87.3 us; the launch traced here: 86.8 us
  starting transfers between devices  39 us (45%)
  Pallas kernels  31.1 us (36%)
  waiting for transfers between devices  15.8 us (18%)
    pallas_call x1, Pallas kernels, forward_call(): pl.pallas_call(forward_kernel, grid=(8,), out_shape=(jax.ShapeDtypeStruct...  16.1 us
    ppermute x7, starting transfers between devices, seg_ring(): lax.ppermute(value, 'seg', [(i, shift(i)) for i in range(lax.axis_size('s...  15.1 us
    all_to_all x1, starting transfers between devices, body(): msg = lax.all_to_all(msg, 'seg', split_axis=0, concat_axis=0, tiled=True)  11.4 us
    pallas_call x1, Pallas kernels, backward_call(): pl.pallas_call(backward_kernel, grid=(8,), out_shape=jax.ShapeDtypeStruct...  9.71 us
    ppermute x4, starting transfers between devices, neighbour(): return lax.ppermute(value, 'seg', pairs)  7.41 us
    ppermute x7, waiting for transfers between devices, seg_ring(): lax.ppermute(value, 'seg', [(i, shift(i)) for i in range(lax.axis_size('s...  6.82 us
    ppermute x3, starting transfers between devices, body(): lax.ppermute(v, 'rep', [(i, (i + k) % 4) for i in range(4)])  5.11 us
    all_to_all x1, waiting for transfers between devices, body(): msg = lax.all_to_all(msg, 'seg', split_axis=0, concat_axis=0, tiled=True)  5.11 us
  transfers between devices with their start and end apart: 15, of which 7 were waited for; matrix products, arithmetic and copies ran while one was open for 0% of the time, Pallas kernels for 21%

profile of v6, /device:TPU:0, one launch (start us, length us, event | category | flops | bytes accessed | tf_op | source)
XLA Modules:
  0.0 86.8 jit_solution(8922257875143767676)
XLA Ops:
  0.6 0.0 copy-start
  0.7 0.0 copy-start.3
  0.7 0.0 copy-start.6
  0.7 2.0 %message.1 = bf16[32,4,1536]{2,1,0:T(4,128)(2,1)} custom-call(s32[4,3]{1,0:T(4,128)} %cols_hbm.1, f32[3,16384]{1,0:T(4,128)} %speeds.1), custom_call_target="tpu_custom_call" | custom-call | tf_op jit(solution)/shard_map/message/pallas_call | solution.py:476
  2.7 1.3 %collective-permute-start = (bf16[4,3,128,128]{3,2,1,0:T(8,128)(2,1)}, bf16[4,3,128,128]{3,2,1,0:T(8,128)(2,1)S(1)}, u32[]{:S(2)}, u32[]{:S(2)}) collective-permute-start(bf16[4,3,128,128]{3,2,1,0:T(8,128)(2,1)} %vo), channel_id=1, source_target_pairs={{0,4},{4,8},{8,12},{12,16},{16,20},{20,24},{24,28},{28,32},{32,36}... | collective-permute-start | bytes 1179656 | tf_op jit(solution)/shard_map/ppermute | solution.py:393
  4.0 1.3 %collective-permute-start.1 = (bf16[4,3,128,128]{3,2,1,0:T(8,128)(2,1)}, bf16[4,3,128,128]{3,2,1,0:T(8,128)(2,1)}, u32[]{:S(2)}, u32[]{:S(2)}) collective-permute-start(bf16[4,3,128,128]{3,2,1,0:T(8,128)(2,1)} %vo), channel_id=1, source_target_pairs={{4,0},{8,4},{12,8},{16,12},{20,16},{24,20},{28,24},{32,28},{36,32}... | collective-permute-start | bytes 1179656 | tf_op jit(solution)/shard_map/ppermute | solution.py:393
  5.3 11.4 %all-to-all-start = ((bf16[32,4,1536]{2,1,0:T(4,128)(2,1)}), bf16[32,4,1536]{2,1,0:T(4,128)(2,1)S(1)}, u32[]{:S(2)}, u32[]{:S(2)}) async-start(bf16[32,4,1536]{2,1,0:T(4,128)(2,1)} %message.1), calls=%async_computation | async-start | bytes 786432 | tf_op jit(solution)/shard_map/all_to_all | solution.py:526
  16.7 0.0 collective-permute-done.vl
  16.8 0.0 copy-start.7
  16.8 0.0 collective-permute-done.1.vr
  16.8 3.5 %collective-permute-start.2 = (bf16[2048,512]{1,0:T(8,128)(2,1)}, bf16[2048,512]{1,0:T(8,128)(2,1)}, u32[]{:S(2)}, u32[]{:S(2)}) collective-permute-start(bf16[2048,512]{1,0:T(8,128)(2,1)} %bitcast.16), channel_id=1, source_target_pairs={{0,4},{4,8},{8,12},{12,16},{16,20},{20,24},{24,28},{28,32},{32,36}... | collective-permute-start | bytes 6291464 | tf_op jit(solution)/shard_map/ppermute | solution.py:393
  20.3 1.3 %collective-permute-start.3 = (bf16[2048,512]{1,0:T(8,128)(2,1)}, bf16[2048,512]{1,0:T(8,128)(2,1)}, u32[]{:S(2)}, u32[]{:S(2)}) collective-permute-start(bf16[2048,512]{1,0:T(8,128)(2,1)} %bitcast.17), channel_id=1, source_target_pairs={{4,0},{8,4},{12,8},{16,12},{20,16},{24,20},{28,24},{32,28},{36,32}... | collective-permute-start | bytes 6291464 | tf_op jit(solution)/shard_map/ppermute | solution.py:393
  21.6 5.1 %all-to-all-done.msg = bf16[32,4,1536]{2,1,0:T(4,128)(2,1)S(1)} async-done(((bf16[32,4,1536]{2,1,0:T(4,128)(2,1)}), bf16[32,4,1536]{2,1,0:T(4,128)(2,1)S(1)}, u32[]{:S(2)}, u32[]{:S(2)}) %all-to-all-start) | async-done | bytes 393248 | tf_op jit(solution)/shard_map/all_to_all | solution.py:526
  26.7 0.0 copy-done.7
  26.7 2.4 %prep.1 = (f32[288,128]{1,0:T(8,128)S(1)}, bf16[256,768]{1,0:T(8,128)(2,1)S(1)}, bf16[256,768]{1,0:T(8,128)(2,1)S(1)}, bf16[256,32]{1,0:T(8,128)(2,1)S(1)}, f32[...) custom-call(f32[1,32]{1,0:T(1,128)} %bitcast.22, ...), custom_call_target="tpu_custom_call" | custom-call | tf_op jit(solution)/shard_map/prep/pallas_call | solution.py:498
  29.1 0.0 copy-done
  29.1 0.0 copy-done.3
  29.2 0.0 copy-done.6
  29.2 16.1 %forward.1 = (bf16[2048,512]{1,0:T(8,128)(2,1)}, bf16[2,256,512]{2,1,0:T(8,128)(2,1)}, bf16[2048,512]{1,0:T(8,128)(2,1)S(1)}, bf16[2048,512]{1,0:T(8,128)(2,1)S(...) custom-call(f32[96,1536]{1,0:T(8,128)S(1)} %get-tuple-element.52.xs,, ...), custom_call_target="tpu_custom_call" | custom-call | flops 20000000000 | bytes 16000000 | tf_op jit(solution)/shard_map/forward/pallas_call | solution.py:415
  45.3 0.0 collective-permute-done.2.gl
  45.3 0.0 collective-permute-done.3.gr
  45.3 0.0 copy-start.1
  45.3 0.0 copy-start.2
  45.3 0.0 copy-start.4
  45.3 0.0 copy-start.5
  45.3 9.7 %backward.1 = f32[104,128]{1,0:T(8,128)S(1)} custom-call(f32[96,1536]{1,0:T(8,128)S(1)} %get-tuple-element.52.xs, bf16[256,768]{1,0:T(8,128)(2,1)S(1)} %get-tuple-element.55.mixt, bf16[4,768,256]{2,1,0:T(8,128)(2,1)S(1)} %get-tuple-element.56.band, bf16[2048,512]{1,0:T(8,128)(2,1)} %collective-permute-done.2.gl, bf16[2048,512]{1,0:T(8,128)(2,1)S(1)} %bitcast.19, ...), custom_call_target="tpu_custom_call" | custom-call | tf_op jit(solution)/shard_map/backward/pallas_call | solution.py:453
  55.1 3.2 %collective-permute-start.4 = (f32[104,128]{1,0:T(8,128)S(1)}, f32[104,128]{1,0:T(8,128)S(1)}, u32[]{:S(2)}, u32[]{:S(2)}) collective-permute-start(f32[104,128]{1,0:T(8,128)S(1)} %backward.1), channel_id=1, source_target_pairs={{0,4},{4,0},{8,12},{12,8},{16,20},{20,16},{24,28},{28,24},{32,36},... | collective-permute-start | bytes 159752 | tf_op jit(solution)/shard_map/ppermute | solution.py:397
  58.3 0.9 %collective-permute-done.4 = f32[104,128]{1,0:T(8,128)S(1)} collective-permute-done((f32[104,128]{1,0:T(8,128)S(1)}, f32[104,128]{1,0:T(8,128)S(1)}, u32[]{:S(2)}, u32[]{:S(2)}) %collective-permute-start.4) | collective-permute-done | bytes 53280 | tf_op jit(solution)/shard_map/ppermute | solution.py:397
  59.1 2.6 %collective-permute-start.7 = (f32[104,128]{1,0:T(8,128)S(1)}, f32[104,128]{1,0:T(8,128)S(1)}, u32[]{:S(2)}, u32[]{:S(2)}) collective-permute-start(f32[104,128]{1,0:T(8,128)S(1)} %add.21), channel_id=1, source_target_pairs={{0,16},{4,20},{8,24},{12,28},{16,0},{20,4},{24,8},{28,12},{32,48},... | collective-permute-start | bytes 159752 | tf_op jit(solution)/shard_map/ppermute | solution.py:397
  61.8 2.9 %collective-permute-start.5 = (f32[104,128]{1,0:T(8,128)S(1)}, f32[104,128]{1,0:T(8,128)S(1)}, u32[]{:S(2)}, u32[]{:S(2)}) collective-permute-start(f32[104,128]{1,0:T(8,128)S(1)} %add.21), channel_id=1, source_target_pairs={{0,8},{4,12},{8,16},{12,20},{16,24},{20,28},{24,0},{28,4},{32,40},... | collective-permute-start | bytes 159752 | tf_op jit(solution)/shard_map/ppermute | solution.py:397
  64.7 0.3 collective-permute-start.6
  65.0 0.0 collective-permute-done.7
  65.0 2.1 %collective-permute-done.5 = f32[104,128]{1,0:T(8,128)S(1)} collective-permute-done((f32[104,128]{1,0:T(8,128)S(1)}, f32[104,128]{1,0:T(8,128)S(1)}, u32[]{:S(2)}, u32[]{:S(2)}) %collective-permute-start.5) | collective-permute-done | bytes 53280 | tf_op jit(solution)/shard_map/ppermute | solution.py:397
  67.1 1.7 %collective-permute-done.6 = f32[104,128]{1,0:T(8,128)S(1)} collective-permute-done((f32[104,128]{1,0:T(8,128)S(1)}, f32[104,128]{1,0:T(8,128)S(1)}, u32[]{:S(2)}, u32[]{:S(2)}) %collective-permute-start.6) | collective-permute-done | bytes 53280 | tf_op jit(solution)/shard_map/ppermute | solution.py:397
  68.8 2.8 %collective-permute-start.10 = (f32[104,128]{1,0:T(8,128)S(1)}, f32[104,128]{1,0:T(8,128)S(1)}, u32[]{:S(2)}, u32[]{:S(2)}) collective-permute-start(f32[104,128]{1,0:T(8,128)S(1)} %add_add_fusion.1), channel_id=1, source_target_pairs={{0,64},{4,68},{8,72},{12,76},{16,80},{20,84},{24,88},{28,92},{32,9... | collective-permute-start | bytes 159752 | tf_op jit(solution)/shard_map/ppermute | solution.py:397
  71.6 0.0 collective-permute-start.8
  71.6 3.2 %collective-permute-start.9 = (f32[104,128]{1,0:T(8,128)S(1)}, f32[104,128]{1,0:T(8,128)S(1)}, u32[]{:S(2)}, u32[]{:S(2)}) collective-permute-start(f32[104,128]{1,0:T(8,128)S(1)} %add_add_fusion.1), channel_id=1, source_target_pairs={{0,96},{4,100},{8,104},{12,108},{16,112},{20,116},{24,120},{28,124... | collective-permute-start | bytes 159752 | tf_op jit(solution)/shard_map/ppermute | solution.py:397
  74.9 0.0 collective-permute-done.10
  74.9 2.1 %collective-permute-done.8 = f32[104,128]{1,0:T(8,128)S(1)} collective-permute-done((f32[104,128]{1,0:T(8,128)S(1)}, f32[104,128]{1,0:T(8,128)S(1)}, u32[]{:S(2)}, u32[]{:S(2)}) %collective-permute-start.8) | collective-permute-done | bytes 53280 | tf_op jit(solution)/shard_map/ppermute | solution.py:397
  77.0 0.0 collective-permute-done.9
  77.0 1.5 %collective-permute-start.11 = (f32[104,128]{1,0:T(8,128)S(1)}, f32[104,128]{1,0:T(8,128)S(1)}, u32[]{:S(2)}, u32[]{:S(2)}) collective-permute-start(f32[104,128]{1,0:T(8,128)S(1)} %add_add_fusion.p0), channel_id=1, source_target_pairs={{0,1},{1,2},{2,3},{3,0},{4,5},{5,6},{6,7},{7,4},{8,9},{9,10},{10,1... | collective-permute-start | bytes 159752 | tf_op jit(solution)/shard_map/ppermute | solution.py:541
  78.6 1.8 %collective-permute-start.12 = (f32[104,128]{1,0:T(8,128)S(1)}, f32[104,128]{1,0:T(8,128)S(1)}, u32[]{:S(2)}, u32[]{:S(2)}) collective-permute-start(f32[104,128]{1,0:T(8,128)S(1)} %add_add_fusion.p0), channel_id=1, source_target_pairs={{0,3},{1,0},{2,1},{3,2},{4,7},{5,4},{6,5},{7,6},{8,11},{9,8},{10,9... | collective-permute-start | bytes 159752 | tf_op jit(solution)/shard_map/ppermute | solution.py:541
  80.3 1.8 %collective-permute-start.13 = (f32[104,128]{1,0:T(8,128)S(1)}, f32[104,128]{1,0:T(8,128)S(1)}, u32[]{:S(2)}, u32[]{:S(2)}) collective-permute-start(f32[104,128]{1,0:T(8,128)S(1)} %add_add_fusion.p0), channel_id=1, source_target_pairs={{0,2},{1,3},{2,0},{3,1},{4,6},{5,7},{6,4},{7,5},{8,10},{9,11},{10,... | collective-permute-start | bytes 159752 | tf_op jit(solution)/shard_map/ppermute | solution.py:541
  82.1 0.7 collective-permute-done.11.p1
  82.9 0.0 collective-permute-done.12.p2
  82.9 3.1 %collective-permute-done.13.p3 = f32[104,128]{1,0:T(8,128)S(1)} collective-permute-done((f32[104,128]{1,0:T(8,128)S(1)}, f32[104,128]{1,0:T(8,128)S(1)}, u32[]{:S(2)}, u32[]{:S(2)}) %collective-permute-start.13) | collective-permute-done | bytes 53280 | tf_op jit(solution)/shard_map/ppermute | solution.py:541
  86.0 0.0 copy-done.1
  86.0 0.0 copy-done.2
  86.0 0.0 copy-done.4
  86.0 0.0 copy-done.5
  86.0 0.8 finish.1
  (3 shorter events, 0.0 us)
Async XLA Ops:
  0.6 28.5 %copy-start = (bf16[2,32,32,512]{3,2,1,0:T(8,128)(2,1)S(1)}, bf16[2,32,32,512]{3,2,1,0:T(8,128)(2,1)}, u32[]{:S(2)}) copy-start(bf16[2,32,32,512]{3,2,1,0:T(8,128)(2,1)} %param.28) | copy-start | bytes 6291460
  0.7 28.5 %copy-start.3 = (bf16[256,32]{0,1:T(8,128)(2,1)S(1)}, bf16[256,32]{0,1:T(8,128)(2,1)}, u32[]{:S(2)}) copy-start(bf16[256,32]{0,1:T(8,128)(2,1)} %param.26) | copy-start | bytes 49156
  0.7 28.5 %copy-start.6 = (bf16[2,256,512]{2,1,0:T(8,128)(2,1)S(1)}, bf16[2,256,512]{2,1,0:T(8,128)(2,1)}, u32[]{:S(2)}) copy-start(bf16[2,256,512]{2,1,0:T(8,128)(2,1)} %gskip.1) | copy-start | bytes 1572868
  2.7 14.0 %collective-permute-start = (bf16[4,3,128,128]{3,2,1,0:T(8,128)(2,1)}, bf16[4,3,128,128]{3,2,1,0:T(8,128)(2,1)S(1)}, u32[]{:S(2)}, u32[]{:S(2)}) collective-permute-start(bf16[4,3,128,128]{3,2,1,0:T(8,128)(2,1)} %vo), channel_id=1, source_target_pairs={{0,4},{4,8},{8,12},{12,16},{16,20},{20,24},{24,28},{28,32},{32,36}... | collective-permute-start | bytes 1179656 | tf_op jit(solution)/shard_map/ppermute | solution.py:393
  4.0 12.7 %collective-permute-start.1 = (bf16[4,3,128,128]{3,2,1,0:T(8,128)(2,1)}, bf16[4,3,128,128]{3,2,1,0:T(8,128)(2,1)}, u32[]{:S(2)}, u32[]{:S(2)}) collective-permute-start(bf16[4,3,128,128]{3,2,1,0:T(8,128)(2,1)} %vo), channel_id=1, source_target_pairs={{4,0},{8,4},{12,8},{16,12},{20,16},{24,20},{28,24},{32,28},{36,32}... | collective-permute-start | bytes 1179656 | tf_op jit(solution)/shard_map/ppermute | solution.py:393
  5.3 21.3 %all-to-all-start = ((bf16[32,4,1536]{2,1,0:T(4,128)(2,1)}), bf16[32,4,1536]{2,1,0:T(4,128)(2,1)S(1)}, u32[]{:S(2)}, u32[]{:S(2)}) async-start(bf16[32,4,1536]{2,1,0:T(4,128)(2,1)} %message.1), calls=%async_computation | async-start | bytes 786432 | tf_op jit(solution)/shard_map/all_to_all | solution.py:526
  16.8 9.9 %copy-start.7 = (bf16[4,3,128,128]{3,2,1,0:T(8,128)(2,1)}, bf16[4,3,128,128]{3,2,1,0:T(8,128)(2,1)S(1)}, u32[]{:S(2)}) copy-start(bf16[4,3,128,128]{3,2,1,0:T(8,128)(2,1)S(1)} %collective-permute-done.vl) | copy-start | bytes 1179652
  16.8 28.5 %collective-permute-start.2 = (bf16[2048,512]{1,0:T(8,128)(2,1)}, bf16[2048,512]{1,0:T(8,128)(2,1)}, u32[]{:S(2)}, u32[]{:S(2)}) collective-permute-start(bf16[2048,512]{1,0:T(8,128)(2,1)} %bitcast.16), channel_id=1, source_target_pairs={{0,4},{4,8},{8,12},{12,16},{16,20},{20,24},{24,28},{28,32},{32,36}... | collective-permute-start | bytes 6291464 | tf_op jit(solution)/shard_map/ppermute | solution.py:393
  20.3 25.0 %collective-permute-start.3 = (bf16[2048,512]{1,0:T(8,128)(2,1)}, bf16[2048,512]{1,0:T(8,128)(2,1)}, u32[]{:S(2)}, u32[]{:S(2)}) collective-permute-start(bf16[2048,512]{1,0:T(8,128)(2,1)} %bitcast.17), channel_id=1, source_target_pairs={{4,0},{8,4},{12,8},{16,12},{20,16},{24,20},{28,24},{32,28},{36,32}... | collective-permute-start | bytes 6291464 | tf_op jit(solution)/shard_map/ppermute | solution.py:393
  45.3 40.7 %copy-start.1 = (bf16[2,32,32]{2,1,0:T(8,128)(2,1)S(1)}, bf16[2,32,32]{2,1,0:T(8,128)(2,1)}, u32[]{:S(2)}) copy-start(bf16[2,32,32]{2,1,0:T(8,128)(2,1)} %wf.3) | copy-start | bytes 12292
  45.3 40.7 %copy-start.2 = (bf16[2,32,32]{2,1,0:T(8,128)(2,1)S(1)}, bf16[2,32,32]{2,1,0:T(8,128)(2,1)}, u32[]{:S(2)}) copy-start(bf16[2,32,32]{2,1,0:T(8,128)(2,1)} %wg.3) | copy-start | bytes 12292
  45.3 40.7 %copy-start.4 = (f32[32]{0:T(128)S(1)}, f32[32]{0:T(128)}, u32[]{:S(2)}) copy-start(f32[32]{0:T(128)} %param.16) | copy-start | bytes 388
  45.3 40.7 %copy-start.5 = (f32[32]{0:T(128)S(1)}, f32[32]{0:T(128)}, u32[]{:S(2)}) copy-start(f32[32]{0:T(128)} %param.17) | copy-start | bytes 388
  55.1 4.1 %collective-permute-start.4 = (f32[104,128]{1,0:T(8,128)S(1)}, f32[104,128]{1,0:T(8,128)S(1)}, u32[]{:S(2)}, u32[]{:S(2)}) collective-permute-start(f32[104,128]{1,0:T(8,128)S(1)} %backward.1), channel_id=1, source_target_pairs={{0,4},{4,0},{8,12},{12,8},{16,20},{20,16},{24,28},{28,24},{32,36},... | collective-permute-start | bytes 159752 | tf_op jit(solution)/shard_map/ppermute | solution.py:397
  59.1 5.9 %collective-permute-start.7 = (f32[104,128]{1,0:T(8,128)S(1)}, f32[104,128]{1,0:T(8,128)S(1)}, u32[]{:S(2)}, u32[]{:S(2)}) collective-permute-start(f32[104,128]{1,0:T(8,128)S(1)} %add.21), channel_id=1, source_target_pairs={{0,16},{4,20},{8,24},{12,28},{16,0},{20,4},{24,8},{28,12},{32,48},... | collective-permute-start | bytes 159752 | tf_op jit(solution)/shard_map/ppermute | solution.py:397
  61.8 5.3 %collective-permute-start.5 = (f32[104,128]{1,0:T(8,128)S(1)}, f32[104,128]{1,0:T(8,128)S(1)}, u32[]{:S(2)}, u32[]{:S(2)}) collective-permute-start(f32[104,128]{1,0:T(8,128)S(1)} %add.21), channel_id=1, source_target_pairs={{0,8},{4,12},{8,16},{12,20},{16,24},{20,28},{24,0},{28,4},{32,40},... | collective-permute-start | bytes 159752 | tf_op jit(solution)/shard_map/ppermute | solution.py:397
  64.7 4.1 %collective-permute-start.6 = (f32[104,128]{1,0:T(8,128)S(1)}, f32[104,128]{1,0:T(8,128)S(1)}, u32[]{:S(2)}, u32[]{:S(2)}) collective-permute-start(f32[104,128]{1,0:T(8,128)S(1)} %add.21), channel_id=1, source_target_pairs={{0,24},{4,28},{8,0},{12,4},{16,8},{20,12},{24,16},{28,20},{32,56},... | collective-permute-start | bytes 159752 | tf_op jit(solution)/shard_map/ppermute | solution.py:397
  68.8 6.0 %collective-permute-start.10 = (f32[104,128]{1,0:T(8,128)S(1)}, f32[104,128]{1,0:T(8,128)S(1)}, u32[]{:S(2)}, u32[]{:S(2)}) collective-permute-start(f32[104,128]{1,0:T(8,128)S(1)} %add_add_fusion.1), channel_id=1, source_target_pairs={{0,64},{4,68},{8,72},{12,76},{16,80},{20,84},{24,88},{28,92},{32,9... | collective-permute-start | bytes 159752 | tf_op jit(solution)/shard_map/ppermute | solution.py:397
  71.6 5.3 %collective-permute-start.8 = (f32[104,128]{1,0:T(8,128)S(1)}, f32[104,128]{1,0:T(8,128)S(1)}, u32[]{:S(2)}, u32[]{:S(2)}) collective-permute-start(f32[104,128]{1,0:T(8,128)S(1)} %add_add_fusion.1), channel_id=1, source_target_pairs={{0,32},{4,36},{8,40},{12,44},{16,48},{20,52},{24,56},{28,60},{32,6... | collective-permute-start | bytes 159752 | tf_op jit(solution)/shard_map/ppermute | solution.py:397
  71.6 5.3 %collective-permute-start.9 = (f32[104,128]{1,0:T(8,128)S(1)}, f32[104,128]{1,0:T(8,128)S(1)}, u32[]{:S(2)}, u32[]{:S(2)}) collective-permute-start(f32[104,128]{1,0:T(8,128)S(1)} %add_add_fusion.1), channel_id=1, source_target_pairs={{0,96},{4,100},{8,104},{12,108},{16,112},{20,116},{24,120},{28,124... | collective-permute-start | bytes 159752 | tf_op jit(solution)/shard_map/ppermute | solution.py:397
  77.0 5.8 %collective-permute-start.11 = (f32[104,128]{1,0:T(8,128)S(1)}, f32[104,128]{1,0:T(8,128)S(1)}, u32[]{:S(2)}, u32[]{:S(2)}) collective-permute-start(f32[104,128]{1,0:T(8,128)S(1)} %add_add_fusion.p0), channel_id=1, source_target_pairs={{0,1},{1,2},{2,3},{3,0},{4,5},{5,6},{6,7},{7,4},{8,9},{9,10},{10,1... | collective-permute-start | bytes 159752 | tf_op jit(solution)/shard_map/ppermute | solution.py:541
  78.6 4.3 %collective-permute-start.12 = (f32[104,128]{1,0:T(8,128)S(1)}, f32[104,128]{1,0:T(8,128)S(1)}, u32[]{:S(2)}, u32[]{:S(2)}) collective-permute-start(f32[104,128]{1,0:T(8,128)S(1)} %add_add_fusion.p0), channel_id=1, source_target_pairs={{0,3},{1,0},{2,1},{3,2},{4,7},{5,4},{6,5},{7,6},{8,11},{9,8},{10,9... | collective-permute-start | bytes 159752 | tf_op jit(solution)/shard_map/ppermute | solution.py:541
  80.3 5.6 %collective-permute-start.13 = (f32[104,128]{1,0:T(8,128)S(1)}, f32[104,128]{1,0:T(8,128)S(1)}, u32[]{:S(2)}, u32[]{:S(2)}) collective-permute-start(f32[104,128]{1,0:T(8,128)S(1)} %add_add_fusion.p0), channel_id=1, source_target_pairs={{0,2},{1,3},{2,0},{3,1},{4,6},{5,7},{6,4},{7,5},{8,10},{9,11},{10,... | collective-permute-start | bytes 159752 | tf_op jit(solution)/shard_map/ppermute | solution.py:541
